TPU v7x, 32 devices: a whole 2x2x4 slice. The times are simulated.
32 devices in a mesh: dp: 2 (over x), ctx: 4 (over z), tp: 4 (over y, core).
Axes of the slice: x: 2, y: 2, z: 4, core: 2. Of those that a mesh axis runs over, the one named last changes fastest.
Arguments:
- inputs: bfloat16 [4, 2048, 768], P('dp', 'ctx'), may hold values from -6 to 6
- segment_ids: int32 [4, 2048], P('dp'), may hold values from 0 to 15, never falling along the last dimension, each value on 1 to 1536 neighbouring positions
- w_query: bfloat16 [768, 768], P('dp', 'tp'), may hold values from -0.3125 to 0.3125
- w_key: bfloat16 [768, 768], P('dp', 'tp'), may hold values from -0.3125 to 0.3125
- w_value: bfloat16 [768, 768], P('dp', 'tp'), may hold values from -0.21875 to 0.21875
- w_output: bfloat16 [768, 768], P('tp', 'dp'), may hold values from -0.875 to 0.875
- w_inner: bfloat16 [768, 3072], P('dp', 'tp'), may hold values from -0.21875 to 0.21875
- w_outer: bfloat16 [3072, 768], P('tp', 'dp'), may hold values from -0.109375 to 0.109375
- gain_attn: float32 [768], replicated, may hold values from 0.1 to 1.9
- shift_attn: float32 [768], replicated, may hold values from -3 to 3
- gain_ffn: float32 [768], replicated, may hold values from 0.1 to 1.9
- shift_ffn: float32 [768], replicated, may hold values from -3 to 3
- cotangent: bfloat16 [4, 2048, 768], P('dp', 'ctx'), may hold values from -6 to 6
Outputs:
- outputs: bfloat16 [4, 2048, 768], P('dp', 'ctx')
- input_grad: bfloat16 [4, 2048, 768], P('dp', 'ctx')
- grad_w_query: float32 [768, 768], P('dp', 'tp')
- grad_w_key: float32 [768, 768], P('dp', 'tp')
- grad_w_value: float32 [768, 768], P('dp', 'tp')
- grad_w_output: float32 [768, 768], P('tp', 'dp')
- grad_w_inner: float32 [768, 3072], P('dp', 'tp')
- grad_w_outer: float32 [3072, 768], P('tp', 'dp')
- grad_gain_attn: float32 [768], replicated
- grad_shift_attn: float32 [768], replicated
- grad_gain_ffn: float32 [768], replicated
- grad_shift_ffn: float32 [768], replicated
Inputs may be any that keep to these rules, and one draw needn't show every extreme that they name: `segment_ids`: along each sequence the document numbers never fall; each of the 16 numbers appears in every sequence, in 1 to 1536 positions, and one of them in exactly 1536.
All inputs are finite; a program needn't handle non-finite values.
Results may differ from a plain program's by a relative error of at most 0.02.
Values may be sent and summed in bfloat16 or wider, within the bound.
No kernel may reach another device: no remote copies, remote signals or barrier semaphores. Data moves between devices by JAX's collectives and lax.ppermute only.
A program may use at most 128 MiB of HBM per device.

v0:
```python
import functools
import math

import jax
import jax.numpy as jnp
from jax import lax
from jax.experimental import pallas as pl
from jax.experimental.pallas import tpu as pltpu
from jax.sharding import PartitionSpec as P

HEAD_DIM = 64
HALF = HEAD_DIM // 2
DOCS = 16
EPSILON = 1e-06
MASKED = -1e30
LOG2E = 1.0 / math.log(2.0)
F32 = jnp.float32
BF16 = jnp.bfloat16
GROUP = 4
KEY_BLOCKS = 8


def dot(left, right, left_dim, right_dim):
    return lax.dot_general(
        left, right, (((left_dim,), (right_dim,)), ((), ())), preferred_element_type=F32
    )


def swap(value, axis, k, size=GROUP):
    return lax.ppermute(value, axis, [(i, i ^ k) for i in range(size)])


def after(value, *others):
    return lax.optimization_barrier((value,) + others)[0]


def pick(stack, index):
    return lax.dynamic_index_in_dim(stack, index, 0, keepdims=False)


def split_bit(value, bit, axis=0):
    half = value.shape[axis] // 2
    keep = lax.dynamic_slice_in_dim(value, bit * half, half, axis)
    send = lax.dynamic_slice_in_dim(value, (1 - bit) * half, half, axis)
    return keep, send


def join_bit(own, other, bit, axis=0):
    low = jnp.where(bit == 0, own, other)
    high = jnp.where(bit == 0, other, own)
    return jnp.concatenate([low, high], axis)


def block_mask(base, span_ref, shape):
    key_index = base + lax.broadcasted_iota(jnp.int32, shape, 0)
    return (key_index >= span_ref[0, 0:1, :]) & (key_index < span_ref[0, 1:2, :])


def ones_below(value):
    return jnp.concatenate([value, jnp.ones((16, value.shape[1]), BF16)])


def minus_below(value, row):
    high = row.astype(BF16)
    rest = row - high.astype(F32)
    mid = rest.astype(BF16)
    last = (rest - mid.astype(F32)).astype(BF16)
    index = lax.broadcasted_iota(jnp.int32, (16, value.shape[1]), 0)
    parts = jnp.where(
        index == 0,
        high.astype(F32),
        jnp.where(index == 1, mid.astype(F32), jnp.where(index == 2, last.astype(F32), 0.0)),
    )
    return jnp.concatenate([value, (-parts).astype(BF16)])


def pair_flag(a, b):
    return jnp.where(a + b == 0, 0, jnp.where(a + b == 4, 2, 1))


def each_block(flags, i, work):
    def step(j, carry):
        flag = pair_flag(flags[i * KEY_BLOCKS + j], flags[i * KEY_BLOCKS + j + KEY_BLOCKS // 2])

        @pl.when(flag == 1)
        def _():
            work(j, True)

        @pl.when(flag == 2)
        def _():
            work(j, False)

        return carry

    lax.fori_loop(0, KEY_BLOCKS // 2, step, 0)


def attend_kernel(
    first, flags, bases, q_ref, k_ref, v_ref, span_ref, o_ref, lse_ref, m_s, q_s, acc_s
):
    i = first + pl.program_id(0)
    heads = q_ref.shape[1] // HEAD_DIM
    rows = q_ref.shape[2]
    parts = [slice(h * HEAD_DIM, (h + 1) * HEAD_DIM) for h in range(heads)]
    m_s[...] = jnp.full(m_s.shape, MASKED, F32)
    acc_s[...] = jnp.zeros(acc_s.shape, F32)

    def find_max(j, masked):
        both = (j, j + KEY_BLOCKS // 2)
        scores = [
            [dot(k_ref[b, part, :], q_ref[0, part, :], 0, 0) for part in parts] for b in both
        ]
        if masked:
            for n, b in enumerate(both):
                ok = block_mask(bases[b], span_ref, (rows, rows))
                scores[n] = [jnp.where(ok, s, MASKED) for s in scores[n]]
        tops = [
            [jnp.max(s.reshape(rows // 8, 8, rows), axis=0) for s in one] for one in scores
        ]
        for h in range(heads):
            m_s[h] = jnp.maximum(m_s[h], jnp.maximum(tops[0][h], tops[1][h]))

    each_block(flags, i, find_max)
    for h, part in enumerate(parts):
        top = jnp.max(m_s[h], axis=0, keepdims=True)
        lse_ref[0, h : h + 1, :] = top
        q_s[h] = minus_below(q_ref[0, part, :], top)

    def mix(j, masked):
        mixed = []
        for b in (j, j + KEY_BLOCKS // 2):
            probs = [
                jnp.exp2(dot(ones_below(k_ref[b, part, :]), q_s[h], 0, 0))
                for h, part in enumerate(parts)
            ]
            if masked:
                ok = block_mask(bases[b], span_ref, (rows, rows))
                probs = [jnp.where(ok, p, 0.0) for p in probs]
            mixed.append([
                dot(ones_below(v_ref[b, part, :]), p.astype(BF16), 1, 0)
                for part, p in zip(parts, probs)
            ])
        for h in range(heads):
            acc_s[h] += mixed[0][h] + mixed[1][h]

    each_block(flags, i, mix)
    for h, part in enumerate(parts):
        total = acc_s[h, HEAD_DIM : HEAD_DIM + 1, :]
        o_ref[0, part, :] = (acc_s[h, :HEAD_DIM, :] / total).astype(BF16)
        lse_ref[0, h : h + 1, :] = lse_ref[0, h : h + 1, :] + jnp.log2(total)


def attend(flags, bases, q, k, v, span, first, blocks):
    width, rows = q.shape[1:]
    heads = width // HEAD_DIM
    one = lambda shape: pl.BlockSpec((1,) + shape, lambda i, *_: (first + i, 0, 0))
    out = lambda shape: pl.BlockSpec((1,) + shape, lambda i, *_: (i, 0, 0))
    whole = pl.BlockSpec(k.shape, lambda i, *_: (0, 0, 0))
    return pl.pallas_call(
        functools.partial(attend_kernel, first),
        grid_spec=pltpu.PrefetchScalarGridSpec(
            num_scalar_prefetch=2,
            grid=(blocks,),
            in_specs=[one((width, rows)), whole, whole, one((2, rows))],
            out_specs=[out((width, rows)), out((heads, rows))],
            scratch_shapes=[
                pltpu.VMEM((heads, 8, rows), F32),
                pltpu.VMEM((heads, HEAD_DIM + 16, rows), BF16),
                pltpu.VMEM((heads, HEAD_DIM + 16, rows), F32),
            ],
        ),
        out_shape=[
            jax.ShapeDtypeStruct((blocks, width, rows), BF16),
            jax.ShapeDtypeStruct((blocks, heads, rows), F32),
        ],
        name="attend",
    )(flags, bases, q, k, v, span)


def attend_back_kernel(
    first, flags, bases, q_ref, k_ref, v_ref, span_ref, o_ref, d_ref, lse_ref, *refs
):
    if first == 0:
        dq_ref, dk_s, dv_s, q_s, d_s = refs
    else:
        dk_in, dv_in, dq_ref, own_k_ref, own_v_ref, far_k_ref, far_v_ref = refs[:7]
        dk_s, dv_s, q_s, d_s = refs[7:]
    i = first + pl.program_id(0)
    heads = q_ref.shape[1] // HEAD_DIM
    parts = [slice(h * HEAD_DIM, (h + 1) * HEAD_DIM) for h in range(heads)]
    rows = q_ref.shape[2]

    @pl.when(pl.program_id(0) == 0)
    def _():
        dk_s[...] = jnp.zeros(dk_s.shape, F32) if first == 0 else dk_in[...]
        dv_s[...] = jnp.zeros(dv_s.shape, F32) if first == 0 else dv_in[...]

    dq_ref[...] = jnp.zeros(dq_ref.shape, F32)
    for h, part in enumerate(parts):
        grad = d_ref[0, part, :]
        delta = jnp.sum(o_ref[0, part, :].astype(F32) * grad.astype(F32), axis=0, keepdims=True)
        q_s[h] = minus_below(q_ref[0, part, :], lse_ref[0, h : h + 1, :])
        d_s[h] = minus_below(grad, delta)

    def work(j, masked):
        results = []
        for b in (j, j + KEY_BLOCKS // 2):
            keys = [k_ref[b, part, :] for part in parts]
            probs = [jnp.exp2(dot(ones_below(keys[h]), q_s[h], 0, 0)) for h in range(heads)]
            if masked:
                ok = block_mask(bases[b], span_ref, (rows, rows))
                probs = [jnp.where(ok, p, 0.0) for p in probs]
            shifted = [
                dot(ones_below(v_ref[b, part, :]), d_s[h], 0, 0) for h, part in enumerate(parts)
            ]
            scores = [(p * s).astype(BF16) for p, s in zip(probs, shifted)]
            d_v = [dot(d_ref[0, part, :], p.astype(BF16), 1, 1) for part, p in zip(parts, probs)]
            d_k = [dot(q_ref[0, part, :], s, 1, 1) for part, s in zip(parts, scores)]
            d_q = [dot(k, s, 1, 0) for k, s in zip(keys, scores)]
            results.append((d_v, d_k, d_q))
        for n, b in enumerate((j, j + KEY_BLOCKS // 2)):
            d_v, d_k, d_q = results[n]
            for h, part in enumerate(parts):
                dv_s[b, part, :] += d_v[h]
                dk_s[b, part, :] += d_k[h]
        for h, part in enumerate(parts):
            dq_ref[0, part, :] += results[0][2][h] + results[1][2][h]

    each_block(flags, i, work)
    if first == 0:
        return

    @pl.when(pl.program_id(0) == pl.num_programs(0) - 1)
    def _():
        own = own_k_ref.shape[0]
        own_k_ref[...] = dk_s[:own]
        own_v_ref[...] = dv_s[:own]
        far_k_ref[...] = dk_s[own:].astype(BF16)
        far_v_ref[...] = dv_s[own:].astype(BF16)


def attend_back(flags, bases, q, k, v, span, o, grad, lse, first, sums):
    blocks = o.shape[0]
    width, rows = q.shape[1:]
    heads = width // HEAD_DIM
    at = lambda shape: pl.BlockSpec((1,) + shape, lambda i, *_: (first + i, 0, 0))
    one = lambda shape: pl.BlockSpec((1,) + shape, lambda i, *_: (i, 0, 0))
    whole = lambda n: pl.BlockSpec((n, width, rows), lambda i, *_: (0, 0, 0))
    total = jax.ShapeDtypeStruct(k.shape, F32)
    half = (k.shape[0] // 2, width, rows)
    out_shape = [jax.ShapeDtypeStruct((blocks, width, rows), F32)]
    out_specs = [one((width, rows))]
    scratch = [
        pltpu.VMEM((heads, HEAD_DIM + 16, rows), BF16),
        pltpu.VMEM((heads, HEAD_DIM + 16, rows), BF16),
    ]
    if first == 0:
        out_shape += [total, total]
        out_specs += [whole(k.shape[0])] * 2
    else:
        out_shape += [jax.ShapeDtypeStruct(half, d) for d in (F32, F32, BF16, BF16)]
        out_specs += [whole(half[0])] * 4
        scratch = [pltpu.VMEM(k.shape, F32), pltpu.VMEM(k.shape, F32)] + scratch
    return pl.pallas_call(
        functools.partial(attend_back_kernel, first),
        grid_spec=pltpu.PrefetchScalarGridSpec(
            num_scalar_prefetch=2,
            grid=(blocks,),
            in_specs=[at((width, rows)), whole(k.shape[0]), whole(k.shape[0]), at((2, rows))]
            + [one((width, rows)), one((width, rows)), one((heads, rows))]
            + [whole(k.shape[0])] * len(sums),
            out_specs=out_specs,
            scratch_shapes=scratch,
        ),
        out_shape=out_shape,
        name="attend_back",
    )(flags, bases, q, k, v, span, o, grad, lse, *sums)


def rotate(value, cosines, sines):
    rows = value.shape[-1]
    parts = value.reshape(-1, 2, HALF, rows)
    lead, trail = parts[:, 0], parts[:, 1]
    return jnp.stack(
        [lead * cosines - trail * sines, trail * cosines + lead * sines], axis=1
    ).reshape(value.shape)


def norm_stats(rows):
    centre = jnp.mean(rows, axis=-1, keepdims=True)
    centred = rows - centre
    spread = jnp.mean(centred * centred, axis=-1, keepdims=True)
    scale = lax.rsqrt(spread + EPSILON)
    return centred * scale, scale


def norm_back(grad, normal, scale, gain):
    dn = grad * gain
    return scale * (
        dn
        - jnp.mean(dn, axis=-1, keepdims=True)
        - normal * jnp.mean(dn * normal, axis=-1, keepdims=True)
    )


def per_device(
    dp_size, inputs, segment_ids, w_query, w_key, w_value, w_output, w_inner, w_outer,
    gain_attn, shift_attn, gain_ffn, shift_ffn, cotangent,
):
    seqs, local_rows, width = inputs.shape
    rows = local_rows // 2
    x = lax.axis_index("dp")
    z = lax.axis_index("ctx")
    t = lax.axis_index("tp")
    y, c = t // 2, t % 2
    pair = dp_size == 2
    head_cols = w_query.shape[1]
    half_width = width // 2
    group_cols = 3 * head_cols

    def turn(value):
        if not pair:
            return value
        own, other = split_bit(value, x, value.ndim - 1)
        return jnp.concatenate([own, other], value.ndim - 1)

    def corner(value):
        flat = lambda d, s: d * GROUP + s
        return lax.ppermute(
            value, ("dp", "tp"),
            [(flat(d, s), flat(d ^ 1, s ^ 2)) for d in range(2) for s in range(GROUP)],
        )

    def across(local):
        if not pair:
            return None, None
        return swap(local, "dp", 1, 2), swap(local, "tp", 2)

    def gather(local, across_x, across_y, far_corner, axis):
        if not pair:
            near = lax.all_gather(local, "dp", axis=axis, tiled=True)
            return near, swap(near, "tp", 2)
        return (
            jnp.concatenate([local, across_x], axis),
            jnp.concatenate([across_y, far_corner], axis),
        )

    def exchange(value, axis, k, size=GROUP):
        return swap(value.astype(BF16), axis, k, size).astype(F32)

    def sum_dp(value):
        if not pair:
            return lax.psum_scatter(
                value.astype(BF16), "dp", scatter_dimension=value.ndim - 1, tiled=True
            ).astype(F32)
        return value[..., :half_width] + exchange(value[..., half_width:], "dp", 1, 2)

    bit0, bit1 = z % 2, z // 2

    def ctx_first(value):
        keep, send = split_bit(value, bit0)
        return keep, swap(send.astype(BF16), "ctx", 1)

    def ctx_second(keep, got):
        keep, send = split_bit(keep + got.astype(F32), bit1)
        return (keep + exchange(send, "ctx", 2)).astype(BF16)

    def ctx_rest(keep):
        keep = join_bit(keep, swap(keep, "ctx", 2), bit1)
        return join_bit(keep, swap(keep, "ctx", 1), bit0).astype(F32)

    def own_tokens(value):
        return lax.dynamic_slice(value, (y, c * rows, 0), (1, rows, value.shape[2]))[0]

    own_in = turn(own_tokens(inputs))
    local = jnp.concatenate([w_query, w_key, w_value], 1)
    near, far = gather(local, *across(local), corner(local) if pair else None, 0)
    in_2 = swap(own_in, "ctx", 2)
    in_blocks = [own_in, swap(own_in, "ctx", 1), in_2, swap(in_2, "ctx", 1)]
    own_cot = turn(own_tokens(cotangent)).astype(F32)
    gain_a, shift_a, gain_f, shift_f = [
        turn(v)[None, :] for v in (gain_attn, shift_attn, gain_ffn, shift_ffn)
    ]
    def by_group(near, far):
        mine = jnp.stack([near, far])
        other = swap(mine, "tp", 1)
        stack = jnp.stack([mine[0], other[0], mine[1], other[1]])
        return [pick(stack, (t ^ z) ^ k) for k in range(GROUP)]

    w_qkv = by_group(near, far)
    mid = head_cols + w_outer.shape[0]
    down = jnp.concatenate([w_output, w_outer, w_inner.T])
    down = after(down, far)
    down_x, down_y = across(down)

    docs = pick(segment_ids, y)
    doc_names = jnp.arange(DOCS, dtype=jnp.int32)[:, None]
    doc_start = jnp.sum((docs[None, :] < doc_names).astype(jnp.int32), 1)
    doc_end = jnp.sum((docs[None, :] <= doc_names).astype(jnp.int32), 1)
    doc_blocks = docs.reshape(GROUP, 2, rows)
    order = jnp.stack([z ^ k for k in range(GROUP)])
    query_docs = jnp.stack([doc_blocks[z ^ k, c] for k in range(GROUP)])
    far_docs = jnp.stack([doc_blocks[z ^ k, 1 - c] for k in range(GROUP)])
    hot = query_docs[:, None, :] == doc_names[None]
    starts = jnp.sum(jnp.where(hot, doc_start[None, :, None], 0), 1)
    ends = jnp.sum(jnp.where(hot, doc_end[None, :, None], 0), 1)
    span = jnp.stack([starts, ends], 1)
    query_bases = (order * 2 + c) * rows
    bases = jnp.concatenate([query_bases, (order * 2 + 1 - c) * rows])
    key_docs = jnp.concatenate([query_docs, far_docs])
    key_low, key_high = key_docs[:, 0], key_docs[:, -1]
    low, high = query_docs[:, :1], query_docs[:, -1:]
    meets = (low <= key_high[None]) & (key_low[None] <= high)
    one_doc = (low == high) & (key_low == low) & (key_high == low)
    flags = jnp.where(meets, jnp.where(one_doc, 2, 1), 0).astype(jnp.int32).reshape(-1)
    position = (
        query_bases[:, None] + jnp.arange(rows, dtype=jnp.int32)[None] - starts
    ).astype(F32)
    theta = jnp.power(10000.0, -2.0 * jnp.arange(HALF, dtype=F32) / HEAD_DIM)
    angle = position[:, None, :] * theta[None, :, None]
    cosines, sines = jnp.cos(angle), jnp.sin(angle)

    factor = 1.0 / math.sqrt(HEAD_DIM)
    queries, keys, values = [], [], []
    for k, block in enumerate(in_blocks):
        lin = dot(w_qkv[0], block, 0, 1)
        query = rotate(lin[:head_cols], cosines[k], sines[k])
        queries.append((query * (factor * LOG2E)).astype(BF16))
        keys.append(rotate(lin[head_cols : 2 * head_cols], cosines[k], sines[k]).astype(BF16))
        values.append(lin[2 * head_cols :].astype(BF16))
    queries = jnp.stack(queries)
    own = jnp.stack(keys + values)
    got = swap(own, "tp", 1)
    down_corner = swap(after(down_x, own), "tp", 2) if pair else None
    keys = jnp.concatenate([own[:GROUP], got[:GROUP]])
    values = jnp.concatenate([own[GROUP:], got[GROUP:]])

    mixed_b, lse_b = attend(flags, bases, queries, keys, values, span, 2, 2)
    mixed_a, lse_a = attend(
        flags, after(bases, mixed_b), queries, keys, values, span, 0, 2
    )
    if pair:
        down_x, down_y, down_corner = [after(v, mixed_a) for v in (down_x, down_y, down_corner)]
    near, far = gather(down, down_x, down_y, down_corner, 1)
    w_out = by_group(near[:head_cols], far[:head_cols])
    w_up = jnp.concatenate([near[head_cols:mid], far[head_cols:mid]])
    w_in = jnp.concatenate([near[mid:], far[mid:]])
    own_mixed = [
        mixed_a[0], swap(mixed_a[1], "ctx", 1), swap(mixed_b[0], "ctx", 2), swap(mixed_b[1], "ctx", 3)
    ]
    attended = functools.reduce(
        jnp.add, [dot(own_mixed[k], w_out[k], 0, 0) for k in (3, 2, 0, 1)]
    )

    normal_a, scale_a = norm_stats(own_in.astype(F32) + attended)
    first = normal_a * gain_a + shift_a
    first_own = first.astype(BF16)
    first_low = jnp.concatenate([first_own, swap(first_own, "tp", 1)])
    inner = dot(first_low, w_in, 1, 1)
    below = 0.5 * (1.0 + lax.erf(inner * math.sqrt(0.5)))
    density = jnp.exp(-0.5 * inner * inner) * (1.0 / math.sqrt(2.0 * math.pi))
    active = (inner * below).astype(BF16)
    slope = (below + inner * density).astype(BF16)
    active, slope = lax.optimization_barrier((active, slope))
    feed = dot(active, w_up, 1, 0)
    feed = feed[:rows] + exchange(feed[rows:], "tp", 1)
    normal_f, scale_f = norm_stats(first + feed)
    second = (normal_f * gain_f + shift_f).astype(BF16)

    d_second = norm_back(own_cot, normal_f, scale_f, gain_f)
    d_feed_own = d_second.astype(BF16)
    d_feed = jnp.concatenate([d_feed_own, swap(d_feed_own, "tp", 1)])
    hidden_cut = active.shape[1] // 2
    up_cut, in_cut = hidden_cut // 2, hidden_cut * 2 // 3

    def pieces(left, right, cut):
        part = lambda lo, hi: dot(left[:, lo:hi], right, 0, 0)
        near_low, far_low = part(0, cut), part(hidden_cut, hidden_cut + cut)
        near_high = part(cut, hidden_cut)
        far_high = part(hidden_cut + cut, 2 * hidden_cut)
        return near_low, far_low, near_high, far_high

    def send_dp(high):
        return swap(high[:, half_width:].astype(BF16), "dp", 1, 2) if pair else None

    def keep_dp(high, got):
        if pair:
            return high[:, :half_width] + got.astype(F32)
        return sum_dp(high)

    up = pieces(active, d_feed, up_cut)
    up_high = jnp.concatenate([up[2], up[3]])
    up_got = (swap(up[1].astype(BF16), "tp", 2), send_dp(up_high))
    d_inner = (dot(d_feed, w_up, 1, 1) * slope).astype(BF16)
    hidden = dot(d_inner, w_in, 1, 0)
    d_first = d_second + hidden[:rows] + exchange(hidden[rows:], "tp", 1)
    d_resid = norm_back(d_first, normal_a, scale_a, gain_a)
    d_attended = d_resid.astype(BF16)

    sent = [dot(w_out[k], d_attended, 1, 1).astype(BF16) for k in range(GROUP)]
    sent = list(lax.optimization_barrier(tuple(sent)))
    d_mixed = [sent[0]] + [swap(sent[k], "ctx", k) for k in range(1, GROUP)]

    late_first = after(first_low, *sent)
    inside = pieces(d_inner, late_first, in_cut)
    late_resid = after(d_attended, *sent)
    grad_out = jnp.stack([dot(own_mixed[k], late_resid, 1, 0) for k in range(GROUP)])
    ordered = [pick(grad_out, (t ^ z) ^ k) for k in range(GROUP)]
    got = exchange(jnp.stack([ordered[1], ordered[3]]), "tp", 1)
    out_near, out_far = ordered[0] + got[0], ordered[2] + got[1]
    in_high = jnp.concatenate([inside[2], out_near, inside[3], out_far])
    in_got = (swap(inside[1].astype(BF16), "tp", 2), send_dp(in_high))

    def second_stage(near_low, high, got_low, got_high, *others):
        got_low = after(got_low, *others)
        low = near_low + got_low.astype(F32)
        high = keep_dp(high, after(got_high, *others) if pair else None)
        cut = high.shape[0] // 2
        high, far = high[:cut], high[cut:]
        return low, high, send_dp(low), swap(far.astype(BF16), "tp", 2)

    def last_stage(low, high, got_low, got_high, *others):
        low = keep_dp(low, after(got_low, *others) if pair else None)
        return jnp.concatenate([low, high + after(got_high, *others).astype(F32)])

    up_low, up_high, *up_got = second_stage(up[0], up_high, *up_got, *sent)
    dq_a, sum_k, sum_v = attend_back(
        flags, after(bases, up_low, up_high), queries, keys, values, span, mixed_a,
        jnp.stack(d_mixed[:2]), lse_a, 0, (),
    )
    up = last_stage(up_low, up_high, *up_got, dq_a)
    up_keep, up_got = ctx_first(up)
    in_low, in_high, *in_got = second_stage(inside[0], in_high, *in_got, dq_a)

    d_query, d_key, d_value, sent_key, sent_value = attend_back(
        flags, after(bases, up_keep, in_low, in_high), queries, keys, values, span,
        mixed_b, jnp.stack(d_mixed[2:]), lse_b, 2, (sum_k, sum_v),
    )
    mark = d_query
    d_query = [dq_a[0], dq_a[1], d_query[0], d_query[1]]
    sibling = exchange(jnp.stack([sent_key, sent_value]), "tp", 1)
    d_key = d_key + sibling[0]
    d_value = d_value + sibling[1]
    lin = [
        jnp.concatenate(
            [
                rotate(d_query[k] * factor, cosines[k], -sines[k]).astype(BF16),
                rotate(d_key[k] * (1.0 / LOG2E), cosines[k], -sines[k]).astype(BF16),
                d_value[k].astype(BF16),
            ]
        )
        for k in range(GROUP)
    ]
    received = [lin[0]] + [swap(lin[k], "ctx", k) for k in range(1, GROUP)]
    grad_qkv = functools.reduce(
        jnp.add, [dot(lin[k], in_blocks[k], 1, 0) for k in range(GROUP)]
    )
    through = functools.reduce(
        jnp.add, [dot(received[k], w_qkv[k], 0, 1) for k in range(GROUP)]
    )
    input_own = (d_resid + through).astype(BF16)

    def spread(value):
        value = turn(value)
        a = jnp.stack([value, swap(value, "tp", 2)])
        b = swap(a, "tp", 1)
        quad = [a[0], b[0], a[1], b[1]]
        quad = jnp.stack(quad)
        parts = [pick(quad, (k ^ t)) for k in range(GROUP)]
        return jnp.stack(parts).reshape(seqs, local_rows, width)

    outputs = spread(second)
    input_grad = spread(input_own)

    inside = last_stage(in_low, in_high, *in_got, mark)
    in_keep, in_got = ctx_first(after(inside, *lin))

    part = sum_dp(grad_qkv)
    both = ("ctx", "tp")
    up = ctx_second(up_keep, after(up_got, part))
    part = part + lax.ppermute(
        part.astype(BF16), both,
        [(g * 4 + s, g * 4 + (s ^ 2)) for g in range(4) for s in range(4) if s // 2 != g // 2],
    ).astype(F32)
    inside = ctx_second(in_keep, after(in_got, part))
    part = part + lax.ppermute(
        part.astype(BF16), both, [(g * 4 + (g ^ 1), g * 4 + g) for g in range(4)]
    ).astype(F32)
    shard_up = ctx_rest(after(up, part))
    shard_in = ctx_rest(inside)
    shard_out = shard_in[hidden_cut:]
    shard_in = shard_in[:hidden_cut]
    part = part.astype(BF16)
    moved = [
        lax.ppermute(part, both, [(g * 4 + g, (g ^ k) * 4 + g) for g in range(4)])
        for k in range(1, GROUP)
    ]
    shard_qkv = jnp.where(t == z, part, moved[0] + moved[1] + moved[2]).astype(F32)

    sums = jnp.stack(
        [
            jnp.sum(d_first * normal_a, 0),
            jnp.sum(d_first, 0),
            jnp.sum(own_cot * normal_f, 0),
            jnp.sum(own_cot, 0),
        ]
    )
    sums = after(turn(sums), *lin)
    sums = sums + swap(sums, "tp", 1)
    sums = sums + swap(sums, "tp", 2)
    sums = after(sums, input_own)
    sums = sums + swap(sums, "dp", 1, 2) if pair else lax.psum(sums, "dp")
    sums = sums + swap(sums, "ctx", 1)
    sums = sums + swap(sums, "ctx", 2)

    return (
        outputs,
        input_grad,
        shard_qkv[:head_cols].T,
        shard_qkv[head_cols : 2 * head_cols].T,
        shard_qkv[2 * head_cols :].T,
        shard_out,
        shard_in.T,
        shard_up,
        sums[0],
        sums[1],
        sums[2],
        sums[3],
    )


def solution(mesh):
    tokens = P("dp", "ctx", None)
    return jax.shard_map(
        functools.partial(per_device, mesh.shape["dp"]),
        mesh=mesh,
        in_specs=(
            tokens,
            P("dp", None),
            P("dp", "tp"),
            P("dp", "tp"),
            P("dp", "tp"),
            P("tp", "dp"),
            P("dp", "tp"),
            P("tp", "dp"),
            P(),
            P(),
            P(),
            P(),
            tokens,
        ),
        out_specs=(
            tokens,
            tokens,
            P("dp", "tp"),
            P("dp", "tp"),
            P("dp", "tp"),
            P("tp", "dp"),
            P("dp", "tp"),
            P("tp", "dp"),
            P(),
            P(),
            P(),
            P(),
        ),
        check_vma=False,
    )
```

profile of v0, /device:TPU:0, one launch (start us, length us, event | category | flops | bytes accessed | tf_op | source)
XLA Modules:
  0.0 332.6 jit_solution(4424510767341127066)
XLA Ops:
  3.5 3.1 collective-permute-start.1
  10.2 3.0 collective-permute-start.5
  13.2 1.6 collective-permute-start.4
  18.2 8.0 %collective-permute-done.1 = bf16[384,576]{0,1:T(8,128)(2,1)S(1)} collective-permute-done((bf16[384,576]{0,1:T(8,128)(2,1)S(1)}, bf16[384,576]{0,1:T(8,128)(2,1)S(1)}, u32[]{:S(2)}, u32[]{:S(2)}) %collective-permute-start.1) | collective-permute-done | bytes 442400 | tf_op jit(solution)/shard_map/ppermute | solution.py:30
  35.5 1.8 collective-permute-start.6
  40.3 1.5 fusion.149
  42.6 1.7 fusion.29
  44.3 3.0 collective-permute-done.6
  52.4 17.6 %collective-permute-done.9 = bf16[1728,384]{1,0:T(8,128)(2,1)} collective-permute-done((bf16[1728,384]{1,0:T(8,128)(2,1)S(1)}, bf16[1728,384]{1,0:T(8,128)(2,1)}, u32[]{:S(2)}, u32[]{:S(2)}) %collective-permute-start.9) | collective-permute-done | bytes 1327136 | tf_op jit(solution)/shard_map/ppermute | solution.py:30
  72.7 11.7 %attend.2 = (bf16[2,192,256]{2,1,0:T(8,128)(2,1)}, f32[2,3,256]{2,1,0:T(4,128)}) custom-call(s32[32]{0:T(128)} %reshape.374.flags, s32[8]{0:T(128)} %pad_add_fusion.2.bases, bf16[4,192,256]{2,1,0:T(8,128)(2,1)} %pad_maximum_fusion.27.q_ref, bf16[8,192,256]{2,1,0:T(8,128)(2,1)} %copy-done.2, bf16[8,192,256]{2,1,0:T(8,128)(2,1)} %copy-done.3, ...), custom_call_target="tpu_custom_call" | custom-call | tf_op jit(solution)/shard_map/attend/pallas_call | solution.py:159
  84.3 8.5 %attend.3 = (bf16[2,192,256]{2,1,0:T(8,128)(2,1)}, f32[2,3,256]{2,1,0:T(4,128)}) custom-call(s32[32]{0:T(128)} %reshape.374.flags, s32[8]{0:T(128)} %pad_add_fusion.2.bases, bf16[4,192,256]{2,1,0:T(8,128)(2,1)} %pad_maximum_fusion.27.q_ref, bf16[8,192,256]{2,1,0:T(8,128)(2,1)} %copy-done.2, bf16[8,192,256]{2,1,0:T(8,128)(2,1)} %copy-done.3, ...), custom_call_target="tpu_custom_call" | custom-call | tf_op jit(solution)/shard_map/attend/pallas_call | solution.py:159
  92.9 2.6 constant_dynamic-update-slice_fusion.21
  97.9 2.4 collective-permute-done.11
  100.4 1.6 constant_dynamic-update-slice_fusion.23
  102.0 1.6 copy-done.9
  103.8 2.7 collective-permute-start.13
  108.0 6.2 %collective-permute-done.13 = bf16[192,256]{1,0:T(8,128)(2,1)S(1)} collective-permute-done((bf16[192,256]{1,0:T(8,128)(2,1)S(1)}, bf16[192,256]{1,0:T(8,128)(2,1)S(1)}, u32[]{:S(2)}, u32[]{:S(2)}) %collective-permute-start.13) | collective-permute-done | bytes 98336 | tf_op jit(solution)/shard_map/ppermute | solution.py:30
  120.1 4.8 %fusion.4 = (bf16[512,1536]{1,0:T(8,128)(2,1)}, bf16[512,1536]{1,0:T(8,128)(2,1)S(1)}) fusion(bf16[768,768]{1,0:T(8,128)(2,1)S(1)} %get-tuple-element.184, bf16[768,768]{1,0:T(8,128)(2,1)S(1)} %get-tuple-element.182, bf16[256,768]{1,0:T(8,128)(2,1)S(1)} %collective-permute-done.15, bf16[256,768]{1,0:T(8,128)(2,1)S(1)} %fusion.50), kind=kOutput, calls=%fused_computation.7 | convolution fusion | flops 1222901760 | bytes 6291456 | tf_op jit(solution)/shard_map/dot_general | solution.py:24
  133.8 3.6 %fusion.5 = bf16[512,1536]{1,0:T(8,128)(2,1)S(1)} fusion(bf16[512,1536]{1,0:T(8,128)(2,1)} %get-tuple-element.63, bf16[768,768]{1,0:T(8,128)(2,1)} %copy-done.33, bf16[768,768]{1,0:T(8,128)(2,1)S(1)} %copy-done.30, bf16[256,768]{1,0:T(8,128)(2,1)} %collective-permute-done.19, bf16[256,768]{1,0:T(8,128)(2,1)} %fusion.139), kind=kOutput, calls=%fused_computation.10 | convolution fusion | flops 1216610304 | bytes 6291456 | tf_op jit(solution)/shard_map/dot_general | solution.py:24
  139.3 1.6 convolution_convert_fusion.1
  141.0 2.5 collective-permute-start.21
  143.5 1.6 fusion.68
  145.1 1.6 fusion.66
  147.7 1.5 multiply_reduce_fusion
  151.6 1.7 collective-permute-start.23
  153.3 2.5 collective-permute-start.30
  161.9 1.6 convolution_add_fusion
  166.4 2.0 collective-permute-start.25
  169.1 10.4 %attend_back.2 = (f32[2,192,256]{2,1,0:T(8,128)}, f32[8,192,256]{2,1,0:T(8,128)}, f32[8,192,256]{2,1,0:T(8,128)}) custom-call(s32[32]{0:T(128)} %reshape.374.flags, s32[8]{0:T(128)} %pad_add_fusion.2.bases, bf16[4,192,256]{2,1,0:T(8,128)(2,1)} %pad_maximum_fusion.27.q_ref, bf16[8,192,256]{2,1,0:T(8,128)(2,1)} %copy-done.2, bf16[8,192,256]{2,1,0:T(8,128)(2,1)} %copy-done.3, ...), custom_call_target="tpu_custom_call" | custom-call | tf_op jit(solution)/shard_map/attend_back/pallas_call | solution.py:264
  179.5 1.8 slice_multiply_fusion.7
  181.3 5.2 %collective-permute-done.25 = bf16[384,384]{1,0:T(8,128)(2,1)} collective-permute-done((bf16[384,384]{1,0:T(8,128)(2,1)}, bf16[384,384]{1,0:T(8,128)(2,1)}, u32[]{:S(2)}, u32[]{:S(2)}) %collective-permute-start.25) | collective-permute-done | bytes 294944 | tf_op jit(solution)/shard_map/ppermute | solution.py:30
  193.1 1.9 convert_add_fusion
  196.5 1.6 collective-permute-start.49
  198.1 14.2 %attend_back.3 = (f32[2,192,256]{2,1,0:T(8,128)}, f32[4,192,256]{2,1,0:T(8,128)}, f32[4,192,256]{2,1,0:T(8,128)}, bf16[4,192,256]{2,1,0:T(8,128)(2,1)}, bf16[4,192,256]{2,1,0:T(8,128)(2,1)}) custom-call(s32[32]{0:T(128)} %reshape.374.flags, s32[8]{0:T(128)} %pad_add_fusion.2.bases, bf16[4,192,256]{2,1,0:T(8,128)(2,1)} %pad_maximum_fusion.27.q_ref, ...), custom_call_target="tpu_custom_call" | custom-call | tf_op jit(solution)/shard_map/attend_back/pallas_call | solution.py:264
  213.7 3.1 collective-permute-done.43
  221.2 1.7 collective-permute-start.32
  228.0 2.3 collective-permute-done.54
  236.1 10.0 %collective-permute-done.33 = bf16[576,256]{1,0:T(8,128)(2,1)S(1)} collective-permute-done((bf16[576,256]{1,0:T(8,128)(2,1)S(1)}, bf16[576,256]{1,0:T(8,128)(2,1)S(1)}, u32[]{:S(2)}, u32[]{:S(2)}) %collective-permute-start.33) | collective-permute-done | bytes 294944 | tf_op jit(solution)/shard_map/ppermute | solution.py:30
  247.5 2.9 collective-permute-done.55
  251.5 2.6 collective-permute-done.56
  256.5 2.2 collective-permute-done.57
  261.3 10.3 %collective-permute-done.38 = bf16[576,384]{1,0:T(8,128)(2,1)S(1)} collective-permute-done((bf16[576,384]{1,0:T(8,128)(2,1)S(1)}, bf16[576,384]{1,0:T(8,128)(2,1)S(1)}, u32[]{:S(2)}, u32[]{:S(2)}) %collective-permute-start.38) | collective-permute-done | bytes 442400 | tf_op jit(solution)/shard_map/ppermute | solution.py:581
  271.9 1.6 collective-permute-start.46
  275.1 10.8 %collective-permute-done.46 = bf16[240,384]{1,0:T(8,128)(2,1)S(1)} collective-permute-done((bf16[240,384]{1,0:T(8,128)(2,1)S(1)}, bf16[240,384]{1,0:T(8,128)(2,1)S(1)}, u32[]{:S(2)}, u32[]{:S(2)}) %collective-permute-start.46) | collective-permute-done | bytes 184352 | tf_op jit(solution)/shard_map/ppermute | solution.py:30
  286.0 4.9 %collective-permute-done.50 = bf16[192,384]{1,0:T(8,128)(2,1)S(1)} collective-permute-done((bf16[192,384]{1,0:T(8,128)(2,1)S(1)}, bf16[192,384]{1,0:T(8,128)(2,1)S(1)}, u32[]{:S(2)}, u32[]{:S(2)}) %collective-permute-start.50) | collective-permute-done | bytes 147488 | tf_op jit(solution)/shard_map/ppermute | solution.py:30
  294.7 2.9 collective-permute-start.42
  303.8 15.7 %collective-permute-done.51 = bf16[192,384]{1,0:T(8,128)(2,1)S(1)} collective-permute-done((bf16[192,384]{1,0:T(8,128)(2,1)S(1)}, bf16[192,384]{1,0:T(8,128)(2,1)S(1)}, u32[]{:S(2)}, u32[]{:S(2)}) %collective-permute-start.51) | collective-permute-done | bytes 147488 | tf_op jit(solution)/shard_map/ppermute | solution.py:30
  322.0 7.2 %collective-permute-done.52 = bf16[384,384]{1,0:T(8,128)(2,1)} collective-permute-done((bf16[384,384]{1,0:T(8,128)(2,1)S(1)}, bf16[384,384]{1,0:T(8,128)(2,1)}, u32[]{:S(2)}, u32[]{:S(2)}) %collective-permute-start.52) | collective-permute-done | bytes 294944 | tf_op jit(solution)/shard_map/ppermute | solution.py:30
  (477 shorter events, 112.8 us)
Async XLA Ops:
  3.5 22.7 %collective-permute-start.1 = (bf16[384,576]{0,1:T(8,128)(2,1)S(1)}, bf16[384,576]{0,1:T(8,128)(2,1)S(1)}, u32[]{:S(2)}, u32[]{:S(2)}) collective-permute-start(bf16[384,576]{0,1:T(8,128)(2,1)S(1)} %constant_dynamic-update-slice_fusion), channel_id=1, source_target_pairs={{0,2},{1,3},{2,0},{3,1},{4,6},{5,7},{6,4},{7,5},{8,10},{9,11},{10,... | collective-permute-start | bytes 1327112 | tf_op jit(solution)/shard_map/ppermute | solution.py:30
  6.6 21.0 %collective-permute-start.2 = (bf16[384,576]{0,1:T(8,128)(2,1)S(1)}, bf16[384,576]{0,1:T(8,128)(2,1)S(1)}, u32[]{:S(2)}, u32[]{:S(2)}) collective-permute-start(bf16[384,576]{0,1:T(8,128)(2,1)S(1)} %constant_dynamic-update-slice_fusion), channel_id=1, source_target_pairs={{0,18},{1,19},{2,16},{3,17},{16,2},{17,3},{18,0},{19,1},{4,22},{5,... | collective-permute-start | bytes 1327112 | tf_op jit(solution)/shard_map/ppermute | solution.py:329
  8.0 19.5 %collective-permute-start = (bf16[384,576]{0,1:T(8,128)(2,1)S(1)}, bf16[384,576]{0,1:T(8,128)(2,1)S(1)}, u32[]{:S(2)}, u32[]{:S(2)}) collective-permute-start(bf16[384,576]{0,1:T(8,128)(2,1)S(1)} %constant_dynamic-update-slice_fusion), channel_id=1, source_target_pairs={{0,16},{16,0},{1,17},{17,1},{2,18},{18,2},{3,19},{19,3},{4,20},{20... | collective-permute-start | bytes 1327112 | tf_op jit(solution)/shard_map/ppermute | solution.py:30
  10.2 25.3 %collective-permute-start.5 = (bf16[256,768]{1,0:T(8,128)(2,1)}, bf16[256,768]{1,0:T(8,128)(2,1)}, u32[]{:S(2)}, u32[]{:S(2)}) collective-permute-start(bf16[256,768]{1,0:T(8,128)(2,1)} %pad_maximum_fusion.26), channel_id=1, source_target_pairs={{0,8},{4,12},{8,0},{12,4},{1,9},{5,13},{9,1},{13,5},{2,10},{6,14},... | collective-permute-start | bytes 1179656 | tf_op jit(solution)/shard_map/ppermute | solution.py:30
  13.2 35.1 %collective-permute-start.4 = (bf16[256,768]{1,0:T(8,128)(2,1)}, bf16[256,768]{1,0:T(8,128)(2,1)}, u32[]{:S(2)}, u32[]{:S(2)}) collective-permute-start(bf16[256,768]{1,0:T(8,128)(2,1)} %pad_maximum_fusion.26), channel_id=1, source_target_pairs={{0,4},{4,0},{8,12},{12,8},{1,5},{5,1},{9,13},{13,9},{2,6},{6,2},{1... | collective-permute-start | bytes 1179656 | tf_op jit(solution)/shard_map/ppermute | solution.py:30
  29.0 11.3 %collective-permute-start.3 = (bf16[2,768,576]{1,2,0:T(8,128)(2,1)}, bf16[2,768,576]{1,2,0:T(8,128)(2,1)}, u32[]{:S(2)}, u32[]{:S(2)}) collective-permute-start(bf16[2,768,576]{1,2,0:T(8,128)(2,1)} %pad_maximum_fusion.5), channel_id=1, source_target_pairs={{0,1},{1,0},{2,3},{3,2},{4,5},{5,4},{6,7},{7,6},{8,9},{9,8},{10,11... | collective-permute-start | bytes 5308424 | tf_op jit(solution)/shard_map/ppermute | solution.py:30
  35.5 11.8 %collective-permute-start.6 = (bf16[256,768]{1,0:T(8,128)(2,1)}, bf16[256,768]{1,0:T(8,128)(2,1)S(1)}, u32[]{:S(2)}, u32[]{:S(2)}) collective-permute-start(bf16[256,768]{1,0:T(8,128)(2,1)} %collective-permute-done.5), channel_id=1, source_target_pairs={{0,4},{4,0},{8,12},{12,8},{1,5},{5,1},{9,13},{13,9},{2,6},{6,2},{1... | collective-permute-start | bytes 1179656 | tf_op jit(solution)/shard_map/ppermute | solution.py:30
  37.3 55.5 %collective-permute-start.10 = (bf16[1728,384]{1,0:T(8,128)(2,1)S(1)}, bf16[1728,384]{1,0:T(8,128)(2,1)}, u32[]{:S(2)}, u32[]{:S(2)}) collective-permute-start(bf16[1728,384]{1,0:T(8,128)(2,1)S(1)} %pad_maximum_fusion.15), channel_id=1, source_target_pairs={{0,2},{1,3},{2,0},{3,1},{4,6},{5,7},{6,4},{7,5},{8,10},{9,11},{10,... | collective-permute-start | bytes 3981320 | tf_op jit(solution)/shard_map/ppermute | solution.py:30
  38.8 31.1 %collective-permute-start.9 = (bf16[1728,384]{1,0:T(8,128)(2,1)S(1)}, bf16[1728,384]{1,0:T(8,128)(2,1)}, u32[]{:S(2)}, u32[]{:S(2)}) collective-permute-start(bf16[1728,384]{1,0:T(8,128)(2,1)S(1)} %pad_maximum_fusion.15), channel_id=1, source_target_pairs={{0,16},{16,0},{1,17},{17,1},{2,18},{18,2},{3,19},{19,3},{4,20},{20... | collective-permute-start | bytes 3981320 | tf_op jit(solution)/shard_map/ppermute | solution.py:30
  51.0 20.3 %collective-permute-start.7 = (bf16[8,192,256]{2,1,0:T(8,128)(2,1)S(1)}, bf16[8,192,256]{2,1,0:T(8,128)(2,1)S(1)}, u32[]{:S(2)}, u32[]{:S(2)}) collective-permute-start(bf16[8,192,256]{2,1,0:T(8,128)(2,1)S(1)} %get-tuple-element.224), channel_id=1, source_target_pairs={{0,1},{1,0},{2,3},{3,2},{4,5},{5,4},{6,7},{7,6},{8,9},{9,8},{10,11... | collective-permute-start | bytes 2359304 | tf_op jit(solution)/shard_map/ppermute | solution.py:30
  69.9 30.4 %collective-permute-start.11 = (bf16[1728,384]{1,0:T(8,128)(2,1)}, bf16[1728,384]{1,0:T(8,128)(2,1)}, u32[]{:S(2)}, u32[]{:S(2)}) collective-permute-start(bf16[1728,384]{1,0:T(8,128)(2,1)} %collective-permute-done.9), channel_id=1, source_target_pairs={{0,2},{1,3},{2,0},{3,1},{4,6},{5,7},{6,4},{7,5},{8,10},{9,11},{10,... | collective-permute-start | bytes 3981320 | tf_op jit(solution)/shard_map/ppermute | solution.py:30
  103.8 10.3 %collective-permute-start.13 = (bf16[192,256]{1,0:T(8,128)(2,1)S(1)}, bf16[192,256]{1,0:T(8,128)(2,1)S(1)}, u32[]{:S(2)}, u32[]{:S(2)}) collective-permute-start(bf16[192,256]{1,0:T(8,128)(2,1)S(1)} %get-tuple-element.292), channel_id=1, source_target_pairs={{0,8},{4,12},{8,0},{12,4},{1,9},{5,13},{9,1},{13,5},{2,10},{6,14},... | collective-permute-start | bytes 294920 | tf_op jit(solution)/shard_map/ppermute | solution.py:30
  106.5 8.0 %collective-permute-start.8 = (bf16[192,256]{1,0:T(8,128)(2,1)S(1)}, bf16[192,256]{1,0:T(8,128)(2,1)S(1)}, u32[]{:S(2)}, u32[]{:S(2)}) collective-permute-start(bf16[192,256]{1,0:T(8,128)(2,1)S(1)} %get-tuple-element.291), channel_id=1, source_target_pairs={{0,12},{4,8},{8,4},{12,0},{1,13},{5,9},{9,5},{13,1},{2,14},{6,10},... | collective-permute-start | bytes 294920 | tf_op jit(solution)/shard_map/ppermute | solution.py:30
  106.7 8.9 %collective-permute-start.14 = (bf16[192,256]{1,0:T(8,128)(2,1)S(1)}, bf16[192,256]{1,0:T(8,128)(2,1)S(1)}, u32[]{:S(2)}, u32[]{:S(2)}) collective-permute-start(bf16[192,256]{1,0:T(8,128)(2,1)S(1)} %slice_bitcast_fusion.11), channel_id=1, source_target_pairs={{0,4},{4,0},{8,12},{12,8},{1,5},{5,1},{9,13},{13,9},{2,6},{6,2},{1... | collective-permute-start | bytes 294920 | tf_op jit(solution)/shard_map/ppermute | solution.py:30
  138.8 8.1 %collective-permute-start.20 = (bf16[256,768]{1,0:T(8,128)(2,1)S(1)}, bf16[256,768]{1,0:T(8,128)(2,1)S(1)}, u32[]{:S(2)}, u32[]{:S(2)}) collective-permute-start(bf16[256,768]{1,0:T(8,128)(2,1)S(1)} %slice.873), channel_id=1, source_target_pairs={{0,1},{1,0},{2,3},{3,2},{4,5},{5,4},{6,7},{7,6},{8,9},{9,8},{10,11... | collective-permute-start | bytes 1179656 | tf_op jit(solution)/shard_map/ppermute | solution.py:30
  141.0 21.0 %collective-permute-start.21 = (bf16[384,768]{1,0:T(8,128)(2,1)S(1)}, bf16[384,768]{1,0:T(8,128)(2,1)S(1)}, u32[]{:S(2)}, u32[]{:S(2)}) collective-permute-start(bf16[384,768]{1,0:T(8,128)(2,1)S(1)} %convolution_convert_fusion.1), channel_id=1, source_target_pairs={{0,2},{1,3},{2,0},{3,1},{4,6},{5,7},{6,4},{7,5},{8,10},{9,11},{10,... | collective-permute-start | bytes 1769480 | tf_op jit(solution)/shard_map/ppermute | solution.py:30
  146.8 17.6 %collective-permute-start.22 = (bf16[768,384]{1,0:T(8,128)(2,1)S(1)}, bf16[768,384]{1,0:T(8,128)(2,1)S(1)}, u32[]{:S(2)}, u32[]{:S(2)}) collective-permute-start(bf16[768,384]{1,0:T(8,128)(2,1)S(1)} %fusion.16), channel_id=1, source_target_pairs={{0,16},{16,0},{1,17},{17,1},{2,18},{18,2},{3,19},{19,3},{4,20},{20... | collective-permute-start | bytes 1769480 | tf_op jit(solution)/shard_map/ppermute | solution.py:30
  151.6 9.1 %collective-permute-start.23 = (bf16[192,256]{1,0:T(8,128)(2,1)S(1)}, bf16[192,256]{1,0:T(8,128)(2,1)S(1)}, u32[]{:S(2)}, u32[]{:S(2)}) collective-permute-start(bf16[192,256]{1,0:T(8,128)(2,1)S(1)} %convolution_convert_fusion.4), channel_id=1, source_target_pairs={{0,4},{4,0},{8,12},{12,8},{1,5},{5,1},{9,13},{13,9},{2,6},{6,2},{1... | collective-permute-start | bytes 294920 | tf_op jit(solution)/shard_map/ppermute | solution.py:30
  153.3 13.1 %collective-permute-start.30 = (bf16[192,256]{1,0:T(8,128)(2,1)S(1)}, bf16[192,256]{1,0:T(8,128)(2,1)S(1)}, u32[]{:S(2)}, u32[]{:S(2)}) collective-permute-start(bf16[192,256]{1,0:T(8,128)(2,1)S(1)} %convolution_convert_fusion.2), channel_id=1, source_target_pairs={{0,12},{4,8},{8,4},{12,0},{1,13},{5,9},{9,5},{13,1},{2,14},{6,10},... | collective-permute-start | bytes 294920 | tf_op jit(solution)/shard_map/ppermute | solution.py:30
  155.8 12.6 %collective-permute-start.29 = (bf16[192,256]{1,0:T(8,128)(2,1)S(1)}, bf16[192,256]{1,0:T(8,128)(2,1)S(1)}, u32[]{:S(2)}, u32[]{:S(2)}) collective-permute-start(bf16[192,256]{1,0:T(8,128)(2,1)S(1)} %convolution_convert_fusion.3), channel_id=1, source_target_pairs={{0,8},{4,12},{8,0},{12,4},{1,9},{5,13},{9,1},{13,5},{2,10},{6,14},... | collective-permute-start | bytes 294920 | tf_op jit(solution)/shard_map/ppermute | solution.py:30
  160.8 32.4 %collective-permute-start.26 = (bf16[512,768]{1,0:T(8,128)(2,1)}, bf16[512,768]{1,0:T(8,128)(2,1)}, u32[]{:S(2)}, u32[]{:S(2)}) collective-permute-start(bf16[512,768]{1,0:T(8,128)(2,1)} %convolution_convert_fusion), channel_id=1, source_target_pairs={{0,2},{1,3},{2,0},{3,1},{4,6},{5,7},{6,4},{7,5},{8,10},{9,11},{10,... | collective-permute-start | bytes 2359304 | tf_op jit(solution)/shard_map/ppermute | solution.py:30
  161.9 27.7 %collective-permute-start.27 = (bf16[2,192,768]{2,1,0:T(8,128)(2,1)}, bf16[2,192,768]{2,1,0:T(8,128)(2,1)}, u32[]{:S(2)}, u32[]{:S(2)}) collective-permute-start(bf16[2,192,768]{2,1,0:T(8,128)(2,1)} %pad_maximum_fusion.25), channel_id=1, source_target_pairs={{0,1},{1,0},{2,3},{3,2},{4,5},{5,4},{6,7},{7,6},{8,9},{9,8},{10,11... | collective-permute-start | bytes 1769480 | tf_op jit(solution)/shard_map/ppermute | solution.py:30
  164.7 16.6 %collective-permute-start.24 = (bf16[384,384]{1,0:T(8,128)(2,1)}, bf16[384,384]{1,0:T(8,128)(2,1)}, u32[]{:S(2)}, u32[]{:S(2)}) collective-permute-start(bf16[384,384]{1,0:T(8,128)(2,1)} %slice.877), channel_id=1, source_target_pairs={{0,16},{16,0},{1,17},{17,1},{2,18},{18,2},{3,19},{19,3},{4,20},{20... | collective-permute-start | bytes 884744 | tf_op jit(solution)/shard_map/ppermute | solution.py:30
  166.4 20.0 %collective-permute-start.25 = (bf16[384,384]{1,0:T(8,128)(2,1)}, bf16[384,384]{1,0:T(8,128)(2,1)}, u32[]{:S(2)}, u32[]{:S(2)}) collective-permute-start(bf16[384,384]{1,0:T(8,128)(2,1)} %slice.876), channel_id=1, source_target_pairs={{0,2},{1,3},{2,0},{3,1},{4,6},{5,7},{6,4},{7,5},{8,10},{9,11},{10,... | collective-permute-start | bytes 884744 | tf_op jit(solution)/shard_map/ppermute | solution.py:30
  192.2 24.7 %collective-permute-start.28 = (bf16[896,384]{1,0:T(8,128)(2,1)}, bf16[896,384]{1,0:T(8,128)(2,1)S(1)}, u32[]{:S(2)}, u32[]{:S(2)}) collective-permute-start(bf16[896,384]{1,0:T(8,128)(2,1)} %slice.870), channel_id=1, source_target_pairs={{0,16},{16,0},{1,17},{17,1},{2,18},{18,2},{3,19},{19,3},{4,20},{20... | collective-permute-start | bytes 2064392 | tf_op jit(solution)/shard_map/ppermute | solution.py:30
  195.1 21.7 %collective-permute-start.43 = (bf16[512,384]{1,0:T(8,128)(2,1)S(1)}, bf16[512,384]{1,0:T(8,128)(2,1)S(1)}, u32[]{:S(2)}, u32[]{:S(2)}) collective-permute-start(bf16[512,384]{1,0:T(8,128)(2,1)S(1)} %slice.872), channel_id=1, source_target_pairs={{0,16},{16,0},{1,17},{17,1},{2,18},{18,2},{3,19},{19,3},{4,20},{20... | collective-permute-start | bytes 1179656 | tf_op jit(solution)/shard_map/ppermute | solution.py:30
  196.5 63.9 %collective-permute-start.49 = (bf16[384,384]{1,0:T(8,128)(2,1)S(1)}, bf16[384,384]{1,0:T(8,128)(2,1)}, u32[]{:S(2)}, u32[]{:S(2)}) collective-permute-start(bf16[384,384]{1,0:T(8,128)(2,1)S(1)} %fusion.52), channel_id=1, source_target_pairs={{0,4},{4,0},{8,12},{12,8},{1,5},{5,1},{9,13},{13,9},{2,6},{6,2},{1... | collective-permute-start | bytes 884744 | tf_op jit(solution)/shard_map/ppermute | solution.py:30
  217.1 14.6 %collective-permute-start.44 = (bf16[448,384]{1,0:T(8,128)(2,1)S(1)}, bf16[448,384]{1,0:T(8,128)(2,1)S(1)}, u32[]{:S(2)}, u32[]{:S(2)}) collective-permute-start(bf16[448,384]{1,0:T(8,128)(2,1)S(1)} %slice.875), channel_id=1, source_target_pairs={{0,2},{1,3},{2,0},{3,1},{4,6},{5,7},{6,4},{7,5},{8,10},{9,11},{10,... | collective-permute-start | bytes 1032200 | tf_op jit(solution)/shard_map/ppermute | solution.py:30
  219.6 13.1 %collective-permute-start.34 = (bf16[576,256]{1,0:T(8,128)(2,1)S(1)}, bf16[576,256]{1,0:T(8,128)(2,1)S(1)}, u32[]{:S(2)}, u32[]{:S(2)}) collective-permute-start(bf16[576,256]{1,0:T(8,128)(2,1)S(1)} %pad_maximum_fusion.35), channel_id=1, source_target_pairs={{0,12},{4,8},{8,4},{12,0},{1,13},{5,9},{9,5},{13,1},{2,14},{6,10},... | collective-permute-start | bytes 884744 | tf_op jit(solution)/shard_map/ppermute | solution.py:30
  221.2 13.9 %collective-permute-start.32 = (bf16[576,256]{1,0:T(8,128)(2,1)S(1)}, bf16[576,256]{1,0:T(8,128)(2,1)S(1)}, u32[]{:S(2)}, u32[]{:S(2)}) collective-permute-start(bf16[576,256]{1,0:T(8,128)(2,1)S(1)} %pad_maximum_fusion.33), channel_id=1, source_target_pairs={{0,4},{4,0},{8,12},{12,8},{1,5},{5,1},{9,13},{13,9},{2,6},{6,2},{1... | collective-permute-start | bytes 884744 | tf_op jit(solution)/shard_map/ppermute | solution.py:30
  230.2 15.8 %collective-permute-start.33 = (bf16[576,256]{1,0:T(8,128)(2,1)S(1)}, bf16[576,256]{1,0:T(8,128)(2,1)S(1)}, u32[]{:S(2)}, u32[]{:S(2)}) collective-permute-start(bf16[576,256]{1,0:T(8,128)(2,1)S(1)} %pad_maximum_fusion.34), channel_id=1, source_target_pairs={{0,8},{4,12},{8,0},{12,4},{1,9},{5,13},{9,1},{13,5},{2,10},{6,14},... | collective-permute-start | bytes 884744 | tf_op jit(solution)/shard_map/ppermute | solution.py:30
  231.7 23.3 %collective-permute-start.37 = (bf16[576,384]{1,0:T(8,128)(2,1)S(1)}, bf16[576,384]{1,0:T(8,128)(2,1)S(1)}, u32[]{:S(2)}, u32[]{:S(2)}) collective-permute-start(bf16[576,384]{1,0:T(8,128)(2,1)S(1)} %slice.871), channel_id=1, source_target_pairs={{0,16},{16,0},{1,17},{17,1},{2,18},{18,2},{3,19},{19,3},{4,20},{20... | collective-permute-start | bytes 1327112 | tf_op jit(solution)/shard_map/ppermute | solution.py:30
  232.7 39.0 %collective-permute-start.45 = (bf16[480,384]{1,0:T(8,128)(2,1)S(1)}, bf16[480,384]{1,0:T(8,128)(2,1)S(1)}, u32[]{:S(2)}, u32[]{:S(2)}) collective-permute-start(bf16[480,384]{1,0:T(8,128)(2,1)S(1)} %dynamic-slice_convert_fusion), channel_id=1, source_target_pairs={{0,4},{4,0},{8,12},{12,8},{1,5},{5,1},{9,13},{13,9},{2,6},{6,2},{1... | collective-permute-start | bytes 1105928 | tf_op jit(solution)/shard_map/ppermute | solution.py:30
  250.4 24.5 %collective-permute-start.17 = (bf16[256,768]{1,0:T(8,128)(2,1)S(1)}, bf16[256,768]{1,0:T(8,128)(2,1)S(1)}, u32[]{:S(2)}, u32[]{:S(2)}) collective-permute-start(bf16[256,768]{1,0:T(8,128)(2,1)S(1)} %get-tuple-element.252), channel_id=1, source_target_pairs={{0,2},{1,3},{2,0},{3,1},{4,6},{5,7},{6,4},{7,5},{8,10},{9,11},{10,... | collective-permute-start | bytes 1179656 | tf_op jit(solution)/shard_map/ppermute | solution.py:30
  254.1 4.7 %collective-permute-start.57 = (f32[4,768]{1,0:T(4,128)S(1)}, f32[4,768]{1,0:T(4,128)S(1)}, u32[]{:S(2)}, u32[]{:S(2)}) collective-permute-start(f32[4,768]{1,0:T(4,128)S(1)} %add.510), channel_id=1, source_target_pairs={{0,8},{4,12},{8,0},{12,4},{1,9},{5,13},{9,1},{13,5},{2,10},{6,14},... | collective-permute-start | bytes 36872 | tf_op jit(solution)/shard_map/ppermute | solution.py:30
  255.1 16.5 %collective-permute-start.38 = (bf16[576,384]{1,0:T(8,128)(2,1)S(1)}, bf16[576,384]{1,0:T(8,128)(2,1)S(1)}, u32[]{:S(2)}, u32[]{:S(2)}) collective-permute-start(bf16[576,384]{1,0:T(8,128)(2,1)S(1)} %get-tuple-element.166), channel_id=1, source_target_pairs={{2,0},{3,1},{6,4},{7,5},{8,10},{9,11},{12,14},{13,15},{18,16},{19,... | collective-permute-start | bytes 1327112 | tf_op jit(solution)/shard_map/ppermute | solution.py:581
  258.7 33.5 %collective-permute-start.35 = (bf16[256,768]{1,0:T(8,128)(2,1)S(1)}, bf16[256,768]{1,0:T(8,128)(2,1)S(1)}, u32[]{:S(2)}, u32[]{:S(2)}) collective-permute-start(bf16[256,768]{1,0:T(8,128)(2,1)S(1)} %get-tuple-element.240), channel_id=1, source_target_pairs={{0,2},{1,3},{2,0},{3,1},{4,6},{5,7},{6,4},{7,5},{8,10},{9,11},{10,... | collective-permute-start | bytes 1179656 | tf_op jit(solution)/shard_map/ppermute | solution.py:30
  271.9 14.0 %collective-permute-start.46 = (bf16[240,384]{1,0:T(8,128)(2,1)S(1)}, bf16[240,384]{1,0:T(8,128)(2,1)S(1)}, u32[]{:S(2)}, u32[]{:S(2)}) collective-permute-start(bf16[240,384]{1,0:T(8,128)(2,1)S(1)} %dynamic-slice_convert_fusion.3), channel_id=1, source_target_pairs={{0,8},{4,12},{8,0},{12,4},{1,9},{5,13},{9,1},{13,5},{2,10},{6,14},... | collective-permute-start | bytes 552968 | tf_op jit(solution)/shard_map/ppermute | solution.py:30
  273.5 17.4 %collective-permute-start.50 = (bf16[192,384]{1,0:T(8,128)(2,1)S(1)}, bf16[192,384]{1,0:T(8,128)(2,1)S(1)}, u32[]{:S(2)}, u32[]{:S(2)}) collective-permute-start(bf16[192,384]{1,0:T(8,128)(2,1)S(1)} %dynamic-slice_convert_fusion.4), channel_id=1, source_target_pairs={{0,8},{4,12},{8,0},{12,4},{1,9},{5,13},{9,1},{13,5},{2,10},{6,14},... | collective-permute-start | bytes 442376 | tf_op jit(solution)/shard_map/ppermute | solution.py:30
  275.0 23.9 %collective-permute-start.18 = (bf16[2,256,768]{2,1,0:T(8,128)(2,1)S(1)}, bf16[2,256,768]{2,1,0:T(8,128)(2,1)S(1)}, u32[]{:S(2)}, u32[]{:S(2)}) collective-permute-start(bf16[2,256,768]{2,1,0:T(8,128)(2,1)S(1)} %pad_maximum_fusion.19), channel_id=1, source_target_pairs={{0,1},{1,0},{2,3},{3,2},{4,5},{5,4},{6,7},{7,6},{8,9},{9,8},{10,11... | collective-permute-start | bytes 2359304 | tf_op jit(solution)/shard_map/ppermute | solution.py:30
  285.9 7.6 %collective-permute-start.47 = (bf16[240,384]{1,0:T(8,128)(2,1)S(1)}, bf16[240,384]{1,0:T(8,128)(2,1)S(1)}, u32[]{:S(2)}, u32[]{:S(2)}) collective-permute-start(bf16[240,384]{1,0:T(8,128)(2,1)S(1)} %add_convert_fusion.1), channel_id=1, source_target_pairs={{0,8},{4,12},{8,0},{12,4},{1,9},{5,13},{9,1},{13,5},{2,10},{6,14},... | collective-permute-start | bytes 552968 | tf_op jit(solution)/shard_map/ppermute | solution.py:30
  292.3 8.2 %collective-permute-start.36 = (bf16[2,256,768]{2,1,0:T(8,128)(2,1)S(1)}, bf16[2,256,768]{2,1,0:T(8,128)(2,1)S(1)}, u32[]{:S(2)}, u32[]{:S(2)}) collective-permute-start(bf16[2,256,768]{2,1,0:T(8,128)(2,1)S(1)} %pad_maximum_fusion.22), channel_id=1, source_target_pairs={{0,1},{1,0},{2,3},{3,2},{4,5},{5,4},{6,7},{7,6},{8,9},{9,8},{10,11... | collective-permute-start | bytes 2359304 | tf_op jit(solution)/shard_map/ppermute | solution.py:30
  293.7 26.0 %collective-permute-start.48 = (bf16[480,384]{1,0:T(8,128)(2,1)S(1)}, bf16[480,384]{1,0:T(8,128)(2,1)S(1)}, u32[]{:S(2)}, u32[]{:S(2)}) collective-permute-start(bf16[480,384]{1,0:T(8,128)(2,1)S(1)} %pad_maximum_fusion.31), channel_id=1, source_target_pairs={{0,4},{4,0},{8,12},{12,8},{1,5},{5,1},{9,13},{13,9},{2,6},{6,2},{1... | collective-permute-start | bytes 1105928 | tf_op jit(solution)/shard_map/ppermute | solution.py:30
  294.7 36.7 %collective-permute-start.42 = (bf16[576,384]{1,0:T(8,128)(2,1)S(1)}, bf16[576,384]{1,0:T(8,128)(2,1)S(1)}, u32[]{:S(2)}, u32[]{:S(2)}) collective-permute-start(bf16[576,384]{1,0:T(8,128)(2,1)S(1)} %convert_add_fusion.1), channel_id=1, source_target_pairs={{0,12},{5,9},{10,6},{15,3},{16,28},{21,25},{26,22},{31,19}} | collective-permute-start | bytes 1327112 | tf_op jit(solution)/shard_map/ppermute | solution.py:595
  297.6 33.8 %collective-permute-start.40 = (bf16[576,384]{1,0:T(8,128)(2,1)S(1)}, bf16[576,384]{1,0:T(8,128)(2,1)S(1)}, u32[]{:S(2)}, u32[]{:S(2)}) collective-permute-start(bf16[576,384]{1,0:T(8,128)(2,1)S(1)} %convert_add_fusion.1), channel_id=1, source_target_pairs={{0,4},{5,1},{10,14},{15,11},{16,20},{21,17},{26,30},{31,27}} | collective-permute-start | bytes 1327112 | tf_op jit(solution)/shard_map/ppermute | solution.py:595
  298.9 32.4 %collective-permute-start.41 = (bf16[576,384]{1,0:T(8,128)(2,1)S(1)}, bf16[576,384]{1,0:T(8,128)(2,1)S(1)}, u32[]{:S(2)}, u32[]{:S(2)}) collective-permute-start(bf16[576,384]{1,0:T(8,128)(2,1)S(1)} %convert_add_fusion.1), channel_id=1, source_target_pairs={{0,8},{5,13},{10,2},{15,7},{16,24},{21,29},{26,18},{31,23}} | collective-permute-start | bytes 1327112 | tf_op jit(solution)/shard_map/ppermute | solution.py:595
  300.6 19.0 %collective-permute-start.51 = (bf16[192,384]{1,0:T(8,128)(2,1)S(1)}, bf16[192,384]{1,0:T(8,128)(2,1)S(1)}, u32[]{:S(2)}, u32[]{:S(2)}) collective-permute-start(bf16[192,384]{1,0:T(8,128)(2,1)S(1)} %add_convert_fusion.2), channel_id=1, source_target_pairs={{0,8},{4,12},{8,0},{12,4},{1,9},{5,13},{9,1},{13,5},{2,10},{6,14},... | collective-permute-start | bytes 442376 | tf_op jit(solution)/shard_map/ppermute | solution.py:30
  319.6 9.6 %collective-permute-start.52 = (bf16[384,384]{1,0:T(8,128)(2,1)S(1)}, bf16[384,384]{1,0:T(8,128)(2,1)}, u32[]{:S(2)}, u32[]{:S(2)}) collective-permute-start(bf16[384,384]{1,0:T(8,128)(2,1)S(1)} %pad_maximum_fusion.36), channel_id=1, source_target_pairs={{0,4},{4,0},{8,12},{12,8},{1,5},{5,1},{9,13},{13,9},{2,6},{6,2},{1... | collective-permute-start | bytes 884744 | tf_op jit(solution)/shard_map/ppermute | solution.py:30
  (95 other events, 552.2 us)
where the time goes:
time: 337 us; the launch traced here: 333 us
  waiting for transfers between devices  118 us (35%)
  starting transfers between devices  57 us (17%)
  Pallas kernels  44.8 us (13%)
  local copies, waits for them, and re-layouts  39.2 us (12%)
  other arithmetic  36 us (11%)
  matrix products  34.8 us (10%)
    ppermute x52, waiting for transfers between devices, swap(): return lax.ppermute(value, axis, [(i, i ^ k) for i in range(size)])  106 us
    ppermute x52, starting transfers between devices, swap(): return lax.ppermute(value, axis, [(i, i ^ k) for i in range(size)])  47.5 us
    dot_general x36, matrix products, dot(): lax.dot_general(left, right, (((left_dim,), (right_dim,)), ((), ())), pre...  34.8 us
    pallas_call x2, Pallas kernels, attend_back(): pl.pallas_call(functools.partial(attend_back_kernel, first), grid_spec=pl...  24.6 us
    pallas_call x2, Pallas kernels, attend(): pl.pallas_call(functools.partial(attend_kernel, first), grid_spec=pltpu.P...  20.2 us
    unnamed x186, local copies, waits for them, and re-layouts  17.8 us
    ppermute x1, waiting for transfers between devices, per_device(): lax.ppermute(part.astype(BF16), both, [(g * 4 + s, g * 4 + (s ^ 2)) for g...  10.3 us
  transfers between devices with their start and end apart: 58, of which 21 were waited for; matrix products, arithmetic and copies ran while one was open for 24% of the time, Pallas kernels for 13%

commit v1 on v0

--- a/solution.py
+++ b/solution.py
@@ -32,6 +32,12 @@
 
 def after(value, *others):
     return lax.optimization_barrier((value,) + others)[0]
+
+
+def together(values, *others):
+    there = [v for v in values if v is not None]
+    there = iter(lax.optimization_barrier(tuple(there) + others)[: len(there)])
+    return [None if v is None else next(there) for v in values]
 
 
 def pick(stack, index):
@@ -180,7 +186,7 @@
 def attend_back_kernel(
     first, flags, bases, q_ref, k_ref, v_ref, span_ref, o_ref, d_ref, lse_ref, *refs
 ):
-    if first == 0:
+    if first:
         dq_ref, dk_s, dv_s, q_s, d_s = refs
     else:
         dk_in, dv_in, dq_ref, own_k_ref, own_v_ref, far_k_ref, far_v_ref = refs[:7]
@@ -192,8 +198,8 @@
 
     @pl.when(pl.program_id(0) == 0)
     def _():
-        dk_s[...] = jnp.zeros(dk_s.shape, F32) if first == 0 else dk_in[...]
-        dv_s[...] = jnp.zeros(dv_s.shape, F32) if first == 0 else dv_in[...]
+        dk_s[...] = jnp.zeros(dk_s.shape, F32) if first else dk_in[...]
+        dv_s[...] = jnp.zeros(dv_s.shape, F32) if first else dv_in[...]
 
     dq_ref[...] = jnp.zeros(dq_ref.shape, F32)
     for h, part in enumerate(parts):
@@ -227,7 +233,7 @@
             dq_ref[0, part, :] += results[0][2][h] + results[1][2][h]
 
     each_block(flags, i, work)
-    if first == 0:
+    if first:
         return
 
     @pl.when(pl.program_id(0) == pl.num_programs(0) - 1)
@@ -254,7 +260,7 @@
         pltpu.VMEM((heads, HEAD_DIM + 16, rows), BF16),
         pltpu.VMEM((heads, HEAD_DIM + 16, rows), BF16),
     ]
-    if first == 0:
+    if first:
         out_shape += [total, total]
         out_specs += [whole(k.shape[0])] * 2
     else:
@@ -363,11 +369,11 @@
 
     def ctx_second(keep, got):
         keep, send = split_bit(keep + got.astype(F32), bit1)
-        return (keep + exchange(send, "ctx", 2)).astype(BF16)
-
-    def ctx_rest(keep):
-        keep = join_bit(keep, swap(keep, "ctx", 2), bit1)
-        return join_bit(keep, swap(keep, "ctx", 1), bit0).astype(F32)
+        return keep, swap(send.astype(BF16), "ctx", 2)
+
+    def ctx_third(keep, got):
+        keep = (keep + got.astype(F32)).astype(BF16)
+        return join_bit(keep, swap(keep, "ctx", 2), bit1)
 
     def own_tokens(value):
         return lax.dynamic_slice(value, (y, c * rows, 0), (1, rows, value.shape[2]))[0]
@@ -431,23 +437,33 @@
     queries = jnp.stack(queries)
     own = jnp.stack(keys + values)
     got = swap(own, "tp", 1)
-    down_corner = swap(after(down_x, own), "tp", 2) if pair else None
     keys = jnp.concatenate([own[:GROUP], got[:GROUP]])
     values = jnp.concatenate([own[GROUP:], got[GROUP:]])
 
     mixed_b, lse_b = attend(flags, bases, queries, keys, values, span, 2, 2)
-    mixed_a, lse_a = attend(
-        flags, after(bases, mixed_b), queries, keys, values, span, 0, 2
-    )
+    landed = [down_x, down_y] if pair else []
+    mixed_0, lse_0 = attend(
+        flags, after(bases, mixed_b, *landed), queries, keys, values, span, 0, 1
+    )
+    down_corner = None
     if pair:
-        down_x, down_y, down_corner = [after(v, mixed_a) for v in (down_x, down_y, down_corner)]
+        cut = down.shape[0] // 2
+        late_x, late_y = after(down_x, mixed_b), after(down_y, mixed_b)
+        low, high = swap(late_x[:cut], "tp", 2), swap(late_y[cut:], "dp", 1, 2)
+        landed = [low, high]
+    got_b = [swap(mixed_b[k], "ctx", k + 2) for k in range(2)]
+    mixed_1, lse_1 = attend(
+        flags, after(bases, mixed_0, *got_b, *landed), queries, keys, values, span, 1, 1
+    )
+    mixed_a, lse_a = jnp.concatenate([mixed_0, mixed_1]), jnp.concatenate([lse_0, lse_1])
+    if pair:
+        down_corner = jnp.concatenate([after(low, mixed_1), after(high, mixed_1)])
+        down_x, down_y = after(down_x, mixed_1), after(down_y, mixed_1)
     near, far = gather(down, down_x, down_y, down_corner, 1)
     w_out = by_group(near[:head_cols], far[:head_cols])
     w_up = jnp.concatenate([near[head_cols:mid], far[head_cols:mid]])
     w_in = jnp.concatenate([near[mid:], far[mid:]])
-    own_mixed = [
-        mixed_a[0], swap(mixed_a[1], "ctx", 1), swap(mixed_b[0], "ctx", 2), swap(mixed_b[1], "ctx", 3)
-    ]
+    own_mixed = [mixed_0[0], swap(mixed_1[0], "ctx", 1)] + [after(g, mixed_1) for g in got_b]
     attended = functools.reduce(
         jnp.add, [dot(own_mixed[k], w_out[k], 0, 0) for k in (3, 2, 0, 1)]
     )
@@ -467,6 +483,11 @@
     normal_f, scale_f = norm_stats(first + feed)
     second = (normal_f * gain_f + shift_f).astype(BF16)
 
+    def spread(own, got):
+        quad = jnp.stack([own[0], got[0], own[1], got[1]])
+        parts = [pick(quad, (k ^ t)) for k in range(GROUP)]
+        return jnp.stack(parts).reshape(seqs, local_rows, width)
+
     d_second = norm_back(own_cot, normal_f, scale_f, gain_f)
     d_feed_own = d_second.astype(BF16)
     d_feed = jnp.concatenate([d_feed_own, swap(d_feed_own, "tp", 1)])
@@ -520,82 +541,25 @@
         return low, high, send_dp(low), swap(far.astype(BF16), "tp", 2)
 
     def last_stage(low, high, got_low, got_high, *others):
-        low = keep_dp(low, after(got_low, *others) if pair else None)
-        return jnp.concatenate([low, high + after(got_high, *others).astype(F32)])
+        if others:
+            got_low, got_high = together([got_low, got_high], *others)
+        low = keep_dp(low, got_low)
+        return jnp.concatenate([low, high + got_high.astype(F32)])
 
     up_low, up_high, *up_got = second_stage(up[0], up_high, *up_got, *sent)
-    dq_a, sum_k, sum_v = attend_back(
-        flags, after(bases, up_low, up_high), queries, keys, values, span, mixed_a,
-        jnp.stack(d_mixed[:2]), lse_a, 0, (),
-    )
-    up = last_stage(up_low, up_high, *up_got, dq_a)
+    dq_b, sum_k, sum_v = attend_back(
+        flags, after(bases, up_low, up_high), queries, keys, values, span, mixed_b,
+        jnp.stack(d_mixed[2:]), lse_b, 2, (),
+    )
+    turn_q = lambda v, k: rotate(v * factor, cosines[k], -sines[k]).astype(BF16)
+    lin_q = [None, None, turn_q(dq_b[0], 2), turn_q(dq_b[1], 3)]
+    got_q = [None, None, swap(lin_q[2], "ctx", 2), swap(lin_q[3], "ctx", 3)]
+    own_out = turn(second)
+    *up_got, far_out = together([*up_got, swap(own_out, "tp", 2)], dq_b)
+    outs = jnp.stack([own_out, far_out])
+    up = last_stage(up_low, up_high, *up_got)
     up_keep, up_got = ctx_first(up)
-    in_low, in_high, *in_got = second_stage(inside[0], in_high, *in_got, dq_a)
-
-    d_query, d_key, d_value, sent_key, sent_value = attend_back(
-        flags, after(bases, up_keep, in_low, in_high), queries, keys, values, span,
-        mixed_b, jnp.stack(d_mixed[2:]), lse_b, 2, (sum_k, sum_v),
-    )
-    mark = d_query
-    d_query = [dq_a[0], dq_a[1], d_query[0], d_query[1]]
-    sibling = exchange(jnp.stack([sent_key, sent_value]), "tp", 1)
-    d_key = d_key + sibling[0]
-    d_value = d_value + sibling[1]
-    lin = [
-        jnp.concatenate(
-            [
-                rotate(d_query[k] * factor, cosines[k], -sines[k]).astype(BF16),
-                rotate(d_key[k] * (1.0 / LOG2E), cosines[k], -sines[k]).astype(BF16),
-                d_value[k].astype(BF16),
-            ]
-        )
-        for k in range(GROUP)
-    ]
-    received = [lin[0]] + [swap(lin[k], "ctx", k) for k in range(1, GROUP)]
-    grad_qkv = functools.reduce(
-        jnp.add, [dot(lin[k], in_blocks[k], 1, 0) for k in range(GROUP)]
-    )
-    through = functools.reduce(
-        jnp.add, [dot(received[k], w_qkv[k], 0, 1) for k in range(GROUP)]
-    )
-    input_own = (d_resid + through).astype(BF16)
-
-    def spread(value):
-        value = turn(value)
-        a = jnp.stack([value, swap(value, "tp", 2)])
-        b = swap(a, "tp", 1)
-        quad = [a[0], b[0], a[1], b[1]]
-        quad = jnp.stack(quad)
-        parts = [pick(quad, (k ^ t)) for k in range(GROUP)]
-        return jnp.stack(parts).reshape(seqs, local_rows, width)
-
-    outputs = spread(second)
-    input_grad = spread(input_own)
-
-    inside = last_stage(in_low, in_high, *in_got, mark)
-    in_keep, in_got = ctx_first(after(inside, *lin))
-
-    part = sum_dp(grad_qkv)
-    both = ("ctx", "tp")
-    up = ctx_second(up_keep, after(up_got, part))
-    part = part + lax.ppermute(
-        part.astype(BF16), both,
-        [(g * 4 + s, g * 4 + (s ^ 2)) for g in range(4) for s in range(4) if s // 2 != g // 2],
-    ).astype(F32)
-    inside = ctx_second(in_keep, after(in_got, part))
-    part = part + lax.ppermute(
-        part.astype(BF16), both, [(g * 4 + (g ^ 1), g * 4 + g) for g in range(4)]
-    ).astype(F32)
-    shard_up = ctx_rest(after(up, part))
-    shard_in = ctx_rest(inside)
-    shard_out = shard_in[hidden_cut:]
-    shard_in = shard_in[:hidden_cut]
-    part = part.astype(BF16)
-    moved = [
-        lax.ppermute(part, both, [(g * 4 + g, (g ^ k) * 4 + g) for g in range(4)])
-        for k in range(1, GROUP)
-    ]
-    shard_qkv = jnp.where(t == z, part, moved[0] + moved[1] + moved[2]).astype(F32)
+    in_low, in_high, *in_got = second_stage(inside[0], in_high, *in_got, dq_b)
 
     sums = jnp.stack(
         [
@@ -605,12 +569,81 @@
             jnp.sum(own_cot, 0),
         ]
     )
-    sums = after(turn(sums), *lin)
-    sums = sums + swap(sums, "tp", 1)
-    sums = sums + swap(sums, "tp", 2)
-    sums = after(sums, input_own)
-    sums = sums + swap(sums, "dp", 1, 2) if pair else lax.psum(sums, "dp")
-    sums = sums + swap(sums, "ctx", 1)
+    sums = turn(sums)
+    sums = sums + after(swap(sums, "tp", 1), dq_b)
+    dq_a, d_key, d_value, sent_key, sent_value = attend_back(
+        flags, after(bases, up_keep, in_low, in_high, lin_q[2], lin_q[3]), queries, keys, values,
+        span, mixed_a, jnp.stack(d_mixed[:2]), lse_a, 0, (sum_k, sum_v),
+    )
+    mark = dq_a
+    lin_q[:2] = [turn_q(dq_a[0], 0), turn_q(dq_a[1], 1)]
+    sums = sums + after(swap(sums, "tp", 2), mark)
+    sibling = exchange(jnp.stack([sent_key, sent_value]), "tp", 1)
+    got_q = [None, None] + together(got_q[2:], mark)
+    up_got, got_outs = together([up_got, swap(outs, "tp", 1)], mark)
+    up_keep, up_got = ctx_second(up_keep, up_got)
+    inside = last_stage(in_low, in_high, *in_got, mark)
+    d_key = d_key + sibling[0]
+    d_value = d_value + sibling[1]
+    lin_kv = [
+        jnp.concatenate(
+            [
+                rotate(d_key[k] * (1.0 / LOG2E), cosines[k], -sines[k]).astype(BF16),
+                d_value[k].astype(BF16),
+            ]
+        )
+        for k in range(GROUP)
+    ]
+    lin = [jnp.concatenate([lin_q[k], lin_kv[k]]) for k in range(GROUP)]
+    in_keep, in_got = ctx_first(after(inside, *lin))
+    grad_qkv = functools.reduce(
+        jnp.add, [dot(lin[k], in_blocks[k], 1, 0) for k in range(GROUP)]
+    )
+    part = sum_dp(grad_qkv)
+    arrived = [swap(lin[1], "ctx", 1)] + [swap(lin_kv[k], "ctx", k) for k in (2, 3)]
+    *arrived, up_got, in_got = together([*arrived, up_got, in_got], grad_qkv.astype(BF16))
+    received = [(lin[0], None), (arrived[0], None), (got_q[2], arrived[1]), (got_q[3], arrived[2])]
+    through = []
+    for k, (one, two) in enumerate(received):
+        through.append(dot(one, w_qkv[k][:, : one.shape[0]], 0, 1))
+        if two is not None:
+            through.append(dot(two, w_qkv[k][:, one.shape[0] :], 0, 1))
+    through = functools.reduce(jnp.add, through)
+    input_own = (d_resid + through).astype(BF16)
+
+    in_grad = turn(input_own)
+    in_grad = jnp.stack([in_grad, swap(in_grad, "tp", 2)])
+    outputs = spread(outs, got_outs)
+    input_grad = spread(in_grad, swap(in_grad, "tp", 1))
+
+    both = ("ctx", "tp")
+    keep, send = split_bit(part, c)
+    part = keep + exchange(send, "tp", 1)
+    in_keep, in_got = ctx_second(in_keep, in_got)
+    up = ctx_third(up_keep, up_got)
+    part = part + lax.ppermute(
+        part.astype(BF16), both,
+        [(g * 4 + s, g * 4 + (s ^ 2)) for g in range(4) for s in range(4) if s // 2 != g // 2],
+    ).astype(F32)
+    part = part.astype(BF16)
+    moved = lax.ppermute(
+        part, both,
+        [(g * 4 + s, (g ^ 2) * 4 + s) for g in range(4) for s in range(4) if s // 2 == g // 2],
+    )
+    held = jnp.where(y == z // 2, part, moved)
+    inside = ctx_third(in_keep, in_got)
+    shard_up = join_bit(up, swap(up, "ctx", 1), bit0).astype(F32)
+    moved = after(swap(held, "ctx", 1), outputs, input_grad, shard_up)
+    shard_in = join_bit(inside, swap(inside, "ctx", 1), bit0).astype(F32)
+    mine = jnp.where(c == bit0, held, moved)
+    theirs = jnp.where(c == bit0, moved, held)
+    shard_qkv = join_bit(mine, swap(theirs, "tp", 1), c).astype(F32)
+    shard_out = shard_in[hidden_cut:]
+    shard_in = shard_in[:hidden_cut]
+
+    got = swap(sums, "dp", 1, 2) if pair else None
+    sums = sums + after(got, *lin) if pair else lax.psum(sums, "dp")
+    sums = sums + after(swap(sums, "ctx", 1), input_own)
     sums = sums + swap(sums, "ctx", 2)
 
     return (

time: 337 us -> 318 us (0.944)
  waiting for transfers between devices: 118 us -> 71.5 us
  starting transfers between devices: 57 us -> 73.8 us
  other arithmetic: 36 us -> 45.2 us
    ppermute x52 -> x58, waiting for transfers between devices: 106 us -> 65.2 us  [swap(): return lax.ppermute(value, axis, [(i, i ^ k) for i in range(size)])]
    ppermute x52 -> x58, starting transfers between devices: 47.5 us -> 67.5 us  [swap(): return lax.ppermute(value, axis, [(i, i ^ k) for i in range(size)])]
    ppermute x1, waiting for transfers between devices: 10.3 us -> 0.01 us  [per_device(): lax.ppermute(part.astype(BF16), both, [(g * 4 + s, g * 4 + (s ^ 2)) for g...]
    ppermute x4 -> x1, waiting for transfers between devices: 0.91 us -> 6.3 us  [per_device(): lax.ppermute(part, both, [(g * 4 + s, (g ^ 2) * 4 + s) for g in range(4)...]
    another operation x15 -> x17, other arithmetic: 1.13 us -> 6.14 us  [the longest x2 3.18 us: per_device(): outs = jnp.stack([own_out, far_out])]
    slice x2 -> x4, local copies, waits for them, and re-layouts: 0.11 us -> 4.2 us  [the longest x2 2.98 us: per_device(): low, high = (swap(late_x[:cut], 'tp', 2), swap(late_y[cut:], 'dp', 1, 2))]
    ppermute x4 -> x1, starting transfers between devices: 6.8 us -> 3.58 us  [per_device(): lax.ppermute(part, both, [(g * 4 + s, (g ^ 2) * 4 + s) for g in range(4)...]
    pallas_call x2 -> x3, Pallas kernels: 20.2 us -> 22.8 us  [attend(): pl.pallas_call(functools.partial(attend_kernel, first), grid_spec=pltpu.P...]
  transfers between devices with their start and end apart: 58 -> 61, of which waited for: 21 -> 19; matrix products, arithmetic and copies ran while one was open for 24% -> 29% of each run, Pallas kernels for 13% -> 13%
where the time goes in v1:
time: 318 us; the launch traced here: 315 us
  starting transfers between devices  73.8 us (23%)
  waiting for transfers between devices  71.5 us (22%)
  Pallas kernels  47.5 us (15%)
  other arithmetic  45.2 us (14%)
  local copies, waits for them, and re-layouts  40.2 us (13%)
  matrix products  33.5 us (11%)
    ppermute x58, starting transfers between devices, swap(): return lax.ppermute(value, axis, [(i, i ^ k) for i in range(size)])  67.5 us
    ppermute x58, waiting for transfers between devices, swap(): return lax.ppermute(value, axis, [(i, i ^ k) for i in range(size)])  65.2 us
    dot_general x38, matrix products, dot(): lax.dot_general(left, right, (((left_dim,), (right_dim,)), ((), ())), pre...  33.5 us
    pallas_call x2, Pallas kernels, attend_back(): pl.pallas_call(functools.partial(attend_back_kernel, first), grid_spec=pl...  24.7 us
    pallas_call x3, Pallas kernels, attend(): pl.pallas_call(functools.partial(attend_kernel, first), grid_spec=pltpu.P...  22.8 us
    unnamed x171, local copies, waits for them, and re-layouts  16.7 us
  transfers between devices with their start and end apart: 61, of which 19 were waited for; matrix products, arithmetic and copies ran while one was open for 29% of the time, Pallas kernels for 13%

profile of v1, /device:TPU:0, one launch (start us, length us, event | category | flops | bytes accessed | tf_op | source)
XLA Modules:
  0.0 314.9 jit_solution(2267181799695203171)
XLA Ops:
  3.5 3.1 collective-permute-start.1
  10.2 3.0 collective-permute-start.5
  13.2 1.6 collective-permute-start.4
  16.7 9.5 %collective-permute-done.1 = bf16[384,576]{0,1:T(8,128)(2,1)S(1)} collective-permute-done((bf16[384,576]{0,1:T(8,128)(2,1)S(1)}, bf16[384,576]{0,1:T(8,128)(2,1)S(1)}, u32[]{:S(2)}, u32[]{:S(2)}) %collective-permute-start.1) | collective-permute-done | bytes 442400 | tf_op jit(solution)/shard_map/ppermute | solution.py:30
  32.7 2.3 pad_maximum_fusion.9
  35.0 1.7 collective-permute-start.6
  42.0 1.7 fusion.36
  43.7 3.0 collective-permute-done.6
  54.1 11.7 %attend.3 = (bf16[2,192,256]{2,1,0:T(8,128)(2,1)}, f32[2,3,256]{2,1,0:T(4,128)}) custom-call(s32[32]{0:T(128)} %reshape.374.flags, s32[8]{0:T(128)} %pad_add_fusion.2.bases, bf16[4,192,256]{2,1,0:T(8,128)(2,1)} %pad_maximum_fusion.21.q_ref, bf16[8,192,256]{2,1,0:T(8,128)(2,1)} %copy-done, bf16[8,192,256]{2,1,0:T(8,128)(2,1)} %copy-done.3, ...), custom_call_target="tpu_custom_call" | custom-call | tf_op jit(solution)/shard_map/attend/pallas_call | solution.py:165
  65.8 2.5 collective-permute-done.10
  70.7 2.0 slice.484
  74.3 2.7 collective-permute-start.11
  77.2 2.6 constant_dynamic-update-slice_fusion.22
  79.8 4.0 %attend.4 = (bf16[1,192,256]{2,1,0:T(8,128)(2,1)}, f32[1,3,256]{2,1,0:T(4,128)}) custom-call(s32[32]{0:T(128)} %reshape.374.flags, s32[8]{0:T(128)} %pad_add_fusion.2.bases, bf16[4,192,256]{2,1,0:T(8,128)(2,1)} %pad_maximum_fusion.21.q_ref, bf16[8,192,256]{2,1,0:T(8,128)(2,1)} %copy-done, bf16[8,192,256]{2,1,0:T(8,128)(2,1)} %copy-done.3, ...), custom_call_target="tpu_custom_call" | custom-call | tf_op jit(solution)/shard_map/attend/pallas_call | solution.py:165
  84.1 1.6 collective-permute-done.13
  85.7 3.3 %collective-permute-done.12 = bf16[864,384]{1,0:T(8,128)(2,1)} collective-permute-done((bf16[864,384]{1,0:T(8,128)(2,1)}, bf16[864,384]{1,0:T(8,128)(2,1)}, u32[]{:S(2)}, u32[]{:S(2)}) %collective-permute-start.12) | collective-permute-done | bytes 663584 | tf_op jit(solution)/shard_map/ppermute | solution.py:30
  89.0 7.1 %attend.5 = (bf16[1,192,256]{2,1,0:T(8,128)(2,1)}, f32[1,3,256]{2,1,0:T(4,128)}) custom-call(s32[32]{0:T(128)} %reshape.374.flags, s32[8]{0:T(128)} %pad_add_fusion.2.bases, bf16[4,192,256]{2,1,0:T(8,128)(2,1)} %pad_maximum_fusion.21.q_ref, bf16[8,192,256]{2,1,0:T(8,128)(2,1)} %copy-done, bf16[8,192,256]{2,1,0:T(8,128)(2,1)} %copy-done.3, ...), custom_call_target="tpu_custom_call" | custom-call | tf_op jit(solution)/shard_map/attend/pallas_call | solution.py:165
  96.2 2.6 constant_dynamic-update-slice_fusion.21
  101.1 1.8 fusion.155
  109.2 2.9 fusion.9
  112.1 2.3 fusion.148
  123.3 2.5 fusion.10
  134.3 2.7 collective-permute-start.25
  145.6 3.4 %collective-permute-done.32 = bf16[192,256]{1,0:T(8,128)(2,1)S(1)} collective-permute-done((bf16[192,256]{1,0:T(8,128)(2,1)S(1)}, bf16[192,256]{1,0:T(8,128)(2,1)S(1)}, u32[]{:S(2)}, u32[]{:S(2)}) %collective-permute-start.32) | collective-permute-done | bytes 98336 | tf_op jit(solution)/shard_map/ppermute | solution.py:30
  153.5 13.7 %attend_back.2 = (f32[2,192,256]{2,1,0:T(8,128)}, f32[8,192,256]{2,1,0:T(8,128)}, f32[8,192,256]{2,1,0:T(8,128)}) custom-call(s32[32]{0:T(128)} %reshape.374.flags, s32[8]{0:T(128)} %pad_add_fusion.2.bases, bf16[4,192,256]{2,1,0:T(8,128)(2,1)} %pad_maximum_fusion.21.q_ref, bf16[8,192,256]{2,1,0:T(8,128)(2,1)} %copy-done, bf16[8,192,256]{2,1,0:T(8,128)(2,1)} %copy-done.3, ...), custom_call_target="tpu_custom_call" | custom-call | tf_op jit(solution)/shard_map/attend_back/pallas_call | solution.py:270
  176.2 3.4 %collective-permute-done.23 = bf16[384,384]{1,0:T(8,128)(2,1)S(1)} collective-permute-done((bf16[384,384]{1,0:T(8,128)(2,1)S(1)}, bf16[384,384]{1,0:T(8,128)(2,1)S(1)}, u32[]{:S(2)}, u32[]{:S(2)}) %collective-permute-start.23) | collective-permute-done | bytes 294944 | tf_op jit(solution)/shard_map/ppermute | solution.py:30
  183.7 2.1 pad_maximum_fusion.14
  189.6 2.6 collective-permute-start.31
  192.2 1.9 convert_add_fusion
  195.5 11.0 %attend_back.3 = (f32[2,192,256]{2,1,0:T(8,128)}, f32[4,192,256]{2,1,0:T(8,128)}, f32[4,192,256]{2,1,0:T(8,128)}, bf16[4,192,256]{2,1,0:T(8,128)(2,1)}, bf16[4,192,256]{2,1,0:T(8,128)(2,1)}) custom-call(s32[32]{0:T(128)} %reshape.374.flags, s32[8]{0:T(128)} %pad_add_fusion.2.bases, bf16[4,192,256]{2,1,0:T(8,128)(2,1)} %pad_maximum_fusion.21.q_ref, ...), custom_call_target="tpu_custom_call" | custom-call | tf_op jit(solution)/shard_map/attend_back/pallas_call | solution.py:270
  209.3 4.2 %collective-permute-start.58 = (f32[4,768]{1,0:T(4,128)S(1)}, f32[4,768]{1,0:T(4,128)S(1)}, u32[]{:S(2)}, u32[]{:S(2)}) collective-permute-start(f32[4,768]{1,0:T(4,128)S(1)} %add.516), channel_id=1, source_target_pairs={{0,16},{16,0},{1,17},{17,1},{2,18},{18,2},{3,19},{19,3},{4,20},{20... | collective-permute-start | bytes 36872 | tf_op jit(solution)/shard_map/ppermute | solution.py:30
  217.0 2.5 collective-permute-start.39
  219.7 2.6 collective-permute-start.37
  229.6 1.6 collective-permute-start.36
  234.6 2.6 collective-permute-start.34
  242.5 5.8 %collective-permute-done.35 = bf16[384,256]{1,0:T(8,128)(2,1)S(1)} collective-permute-done((bf16[384,256]{1,0:T(8,128)(2,1)S(1)}, bf16[384,256]{1,0:T(8,128)(2,1)S(1)}, u32[]{:S(2)}, u32[]{:S(2)}) %collective-permute-start.35) | collective-permute-done | bytes 196640 | tf_op jit(solution)/shard_map/ppermute | solution.py:30
  249.3 6.8 %collective-permute-done.40 = bf16[480,384]{1,0:T(8,128)(2,1)S(1)} collective-permute-done((bf16[480,384]{1,0:T(8,128)(2,1)S(1)}, bf16[480,384]{1,0:T(8,128)(2,1)S(1)}, u32[]{:S(2)}, u32[]{:S(2)}) %collective-permute-start.40) | collective-permute-done | bytes 368672 | tf_op jit(solution)/shard_map/ppermute | solution.py:30
  260.9 2.6 collective-permute-start.53
  264.1 1.8 collective-permute-start.43
  265.9 4.9 %collective-permute-done.60 = f32[4,768]{1,0:T(4,128)S(1)} collective-permute-done((f32[4,768]{1,0:T(4,128)S(1)}, f32[4,768]{1,0:T(4,128)S(1)}, u32[]{:S(2)}, u32[]{:S(2)}) %collective-permute-start.60) | collective-permute-done | bytes 12320 | tf_op jit(solution)/shard_map/ppermute | solution.py:30
  271.7 5.9 %collective-permute-done.50 = bf16[192,384]{1,0:T(8,128)(2,1)S(1)} collective-permute-done((bf16[192,384]{1,0:T(8,128)(2,1)S(1)}, bf16[192,384]{1,0:T(8,128)(2,1)S(1)}, u32[]{:S(2)}, u32[]{:S(2)}) %collective-permute-start.50) | collective-permute-done | bytes 147488 | tf_op jit(solution)/shard_map/ppermute | solution.py:30
  277.8 2.0 collective-permute-start.54
  281.2 7.1 %collective-permute-done.54 = bf16[240,384]{1,0:T(8,128)(2,1)S(1)} collective-permute-done((bf16[240,384]{1,0:T(8,128)(2,1)S(1)}, bf16[240,384]{1,0:T(8,128)(2,1)S(1)}, u32[]{:S(2)}, u32[]{:S(2)}) %collective-permute-start.54) | collective-permute-done | bytes 184352 | tf_op jit(solution)/shard_map/ppermute | solution.py:30
  288.3 1.8 collective-permute-start.55
  290.4 3.6 %collective-permute-start.48 = (bf16[288,384]{1,0:T(8,128)(2,1)S(1)}, bf16[288,384]{1,0:T(8,128)(2,1)S(1)}, u32[]{:S(2)}, u32[]{:S(2)}) collective-permute-start(bf16[288,384]{1,0:T(8,128)(2,1)S(1)} %add_convert_fusion.1), channel_id=1, source_target_pairs={{0,8},{1,9},{4,12},{5,13},{10,2},{11,3},{14,6},{15,7},{16,24},{17,... | collective-permute-start | bytes 663560 | tf_op jit(solution)/shard_map/ppermute | solution.py:629
  295.2 6.3 %collective-permute-done.48 = bf16[288,384]{1,0:T(8,128)(2,1)S(1)} collective-permute-done((bf16[288,384]{1,0:T(8,128)(2,1)S(1)}, bf16[288,384]{1,0:T(8,128)(2,1)S(1)}, u32[]{:S(2)}, u32[]{:S(2)}) %collective-permute-start.48) | collective-permute-done | bytes 221216 | tf_op jit(solution)/shard_map/ppermute | solution.py:629
  301.5 4.3 %collective-permute-start.49 = (bf16[288,384]{1,0:T(8,128)(2,1)S(1)}, bf16[288,384]{1,0:T(8,128)(2,1)S(1)}, u32[]{:S(2)}, u32[]{:S(2)}) collective-permute-start(bf16[288,384]{1,0:T(8,128)(2,1)S(1)} %broadcast_select_fusion.4), channel_id=1, source_target_pairs={{0,4},{4,0},{8,12},{12,8},{1,5},{5,1},{9,13},{13,9},{2,6},{6,2},{1... | collective-permute-start | bytes 663560 | tf_op jit(solution)/shard_map/ppermute | solution.py:30
  307.7 3.6 %collective-permute-done.49 = bf16[288,384]{1,0:T(8,128)(2,1)S(1)} collective-permute-done((bf16[288,384]{1,0:T(8,128)(2,1)S(1)}, bf16[288,384]{1,0:T(8,128)(2,1)S(1)}, u32[]{:S(2)}, u32[]{:S(2)}) %collective-permute-start.49) | collective-permute-done | bytes 221216 | tf_op jit(solution)/shard_map/ppermute | solution.py:30
  (478 shorter events, 125.3 us)
Async XLA Ops:
  3.5 22.7 %collective-permute-start.1 = (bf16[384,576]{0,1:T(8,128)(2,1)S(1)}, bf16[384,576]{0,1:T(8,128)(2,1)S(1)}, u32[]{:S(2)}, u32[]{:S(2)}) collective-permute-start(bf16[384,576]{0,1:T(8,128)(2,1)S(1)} %constant_dynamic-update-slice_fusion), channel_id=1, source_target_pairs={{0,2},{1,3},{2,0},{3,1},{4,6},{5,7},{6,4},{7,5},{8,10},{9,11},{10,... | collective-permute-start | bytes 1327112 | tf_op jit(solution)/shard_map/ppermute | solution.py:30
  6.5 21.0 %collective-permute-start.2 = (bf16[384,576]{0,1:T(8,128)(2,1)S(1)}, bf16[384,576]{0,1:T(8,128)(2,1)S(1)}, u32[]{:S(2)}, u32[]{:S(2)}) collective-permute-start(bf16[384,576]{0,1:T(8,128)(2,1)S(1)} %constant_dynamic-update-slice_fusion), channel_id=1, source_target_pairs={{0,18},{1,19},{2,16},{3,17},{16,2},{17,3},{18,0},{19,1},{4,22},{5,... | collective-permute-start | bytes 1327112 | tf_op jit(solution)/shard_map/ppermute | solution.py:335
  8.0 19.5 %collective-permute-start = (bf16[384,576]{0,1:T(8,128)(2,1)S(1)}, bf16[384,576]{0,1:T(8,128)(2,1)S(1)}, u32[]{:S(2)}, u32[]{:S(2)}) collective-permute-start(bf16[384,576]{0,1:T(8,128)(2,1)S(1)} %constant_dynamic-update-slice_fusion), channel_id=1, source_target_pairs={{0,16},{16,0},{1,17},{17,1},{2,18},{18,2},{3,19},{19,3},{4,20},{20... | collective-permute-start | bytes 1327112 | tf_op jit(solution)/shard_map/ppermute | solution.py:30
  10.2 24.9 %collective-permute-start.5 = (bf16[256,768]{1,0:T(8,128)(2,1)}, bf16[256,768]{1,0:T(8,128)(2,1)}, u32[]{:S(2)}, u32[]{:S(2)}) collective-permute-start(bf16[256,768]{1,0:T(8,128)(2,1)} %pad_maximum_fusion.20), channel_id=1, source_target_pairs={{0,8},{4,12},{8,0},{12,4},{1,9},{5,13},{9,1},{13,5},{2,10},{6,14},... | collective-permute-start | bytes 1179656 | tf_op jit(solution)/shard_map/ppermute | solution.py:30
  13.2 34.6 %collective-permute-start.4 = (bf16[256,768]{1,0:T(8,128)(2,1)}, bf16[256,768]{1,0:T(8,128)(2,1)}, u32[]{:S(2)}, u32[]{:S(2)}) collective-permute-start(bf16[256,768]{1,0:T(8,128)(2,1)} %pad_maximum_fusion.20), channel_id=1, source_target_pairs={{0,4},{4,0},{8,12},{12,8},{1,5},{5,1},{9,13},{13,9},{2,6},{6,2},{1... | collective-permute-start | bytes 1179656 | tf_op jit(solution)/shard_map/ppermute | solution.py:30
  29.0 10.7 %collective-permute-start.3 = (bf16[2,768,576]{1,2,0:T(8,128)(2,1)}, bf16[2,768,576]{1,2,0:T(8,128)(2,1)}, u32[]{:S(2)}, u32[]{:S(2)}) collective-permute-start(bf16[2,768,576]{1,2,0:T(8,128)(2,1)} %pad_maximum_fusion.3), channel_id=1, source_target_pairs={{0,1},{1,0},{2,3},{3,2},{4,5},{5,4},{6,7},{7,6},{8,9},{9,8},{10,11... | collective-permute-start | bytes 5308424 | tf_op jit(solution)/shard_map/ppermute | solution.py:30
  35.0 11.7 %collective-permute-start.6 = (bf16[256,768]{1,0:T(8,128)(2,1)}, bf16[256,768]{1,0:T(8,128)(2,1)S(1)}, u32[]{:S(2)}, u32[]{:S(2)}) collective-permute-start(bf16[256,768]{1,0:T(8,128)(2,1)} %collective-permute-done.5), channel_id=1, source_target_pairs={{0,4},{4,0},{8,12},{12,8},{1,5},{5,1},{9,13},{13,9},{2,6},{6,2},{1... | collective-permute-start | bytes 1179656 | tf_op jit(solution)/shard_map/ppermute | solution.py:30
  36.8 31.5 %collective-permute-start.10 = (bf16[1728,384]{1,0:T(8,128)(2,1)}, bf16[1728,384]{1,0:T(8,128)(2,1)S(1)}, u32[]{:S(2)}, u32[]{:S(2)}) collective-permute-start(bf16[1728,384]{1,0:T(8,128)(2,1)} %pad_maximum_fusion.9), channel_id=1, source_target_pairs={{0,2},{1,3},{2,0},{3,1},{4,6},{5,7},{6,4},{7,5},{8,10},{9,11},{10,... | collective-permute-start | bytes 3981320 | tf_op jit(solution)/shard_map/ppermute | solution.py:30
  38.3 32.4 %collective-permute-start.9 = (bf16[1728,384]{1,0:T(8,128)(2,1)}, bf16[1728,384]{1,0:T(8,128)(2,1)}, u32[]{:S(2)}, u32[]{:S(2)}) collective-permute-start(bf16[1728,384]{1,0:T(8,128)(2,1)} %pad_maximum_fusion.9), channel_id=1, source_target_pairs={{0,16},{16,0},{1,17},{17,1},{2,18},{18,2},{3,19},{19,3},{4,20},{20... | collective-permute-start | bytes 3981320 | tf_op jit(solution)/shard_map/ppermute | solution.py:30
  69.2 16.5 %collective-permute-start.13 = (bf16[864,384]{1,0:T(8,128)(2,1)}, bf16[864,384]{1,0:T(8,128)(2,1)S(1)}, u32[]{:S(2)}, u32[]{:S(2)}) collective-permute-start(bf16[864,384]{1,0:T(8,128)(2,1)} %slice.485), channel_id=1, source_target_pairs={{0,16},{16,0},{1,17},{17,1},{2,18},{18,2},{3,19},{19,3},{4,20},{20... | collective-permute-start | bytes 1990664 | tf_op jit(solution)/shard_map/ppermute | solution.py:30
  72.7 16.3 %collective-permute-start.12 = (bf16[864,384]{1,0:T(8,128)(2,1)}, bf16[864,384]{1,0:T(8,128)(2,1)}, u32[]{:S(2)}, u32[]{:S(2)}) collective-permute-start(bf16[864,384]{1,0:T(8,128)(2,1)} %slice.484), channel_id=1, source_target_pairs={{0,2},{1,3},{2,0},{3,1},{4,6},{5,7},{6,4},{7,5},{8,10},{9,11},{10,... | collective-permute-start | bytes 1990664 | tf_op jit(solution)/shard_map/ppermute | solution.py:30
  74.3 9.7 %collective-permute-start.11 = (bf16[192,256]{1,0:T(8,128)(2,1)S(1)}, bf16[192,256]{1,0:T(8,128)(2,1)S(1)}, u32[]{:S(2)}, u32[]{:S(2)}) collective-permute-start(bf16[192,256]{1,0:T(8,128)(2,1)S(1)} %get-tuple-element.325), channel_id=1, source_target_pairs={{0,8},{4,12},{8,0},{12,4},{1,9},{5,13},{9,1},{13,5},{2,10},{6,14},... | collective-permute-start | bytes 294920 | tf_op jit(solution)/shard_map/ppermute | solution.py:30
  121.8 52.8 %collective-permute-start.24 = (bf16[256,768]{1,0:T(8,128)(2,1)}, bf16[256,768]{1,0:T(8,128)(2,1)}, u32[]{:S(2)}, u32[]{:S(2)}) collective-permute-start(bf16[256,768]{1,0:T(8,128)(2,1)} %get-tuple-element.285), channel_id=1, source_target_pairs={{0,2},{1,3},{2,0},{3,1},{4,6},{5,7},{6,4},{7,5},{8,10},{9,11},{10,... | collective-permute-start | bytes 1179656 | tf_op jit(solution)/shard_map/ppermute | solution.py:30
  127.9 23.3 %collective-permute-start.19 = (bf16[384,768]{1,0:T(8,128)(2,1)S(1)}, bf16[384,768]{1,0:T(8,128)(2,1)S(1)}, u32[]{:S(2)}, u32[]{:S(2)}) collective-permute-start(bf16[384,768]{1,0:T(8,128)(2,1)S(1)} %convolution_convert_fusion.1), channel_id=1, source_target_pairs={{0,2},{1,3},{2,0},{3,1},{4,6},{5,7},{6,4},{7,5},{8,10},{9,11},{10,... | collective-permute-start | bytes 1769480 | tf_op jit(solution)/shard_map/ppermute | solution.py:30
  130.5 37.8 %collective-permute-start.22 = (bf16[768,384]{1,0:T(8,128)(2,1)}, bf16[768,384]{1,0:T(8,128)(2,1)}, u32[]{:S(2)}, u32[]{:S(2)}) collective-permute-start(bf16[768,384]{1,0:T(8,128)(2,1)} %fusion.26), channel_id=1, source_target_pairs={{0,16},{16,0},{1,17},{17,1},{2,18},{18,2},{3,19},{19,3},{4,20},{20... | collective-permute-start | bytes 1769480 | tf_op jit(solution)/shard_map/ppermute | solution.py:30
  134.3 10.1 %collective-permute-start.25 = (bf16[192,256]{1,0:T(8,128)(2,1)S(1)}, bf16[192,256]{1,0:T(8,128)(2,1)S(1)}, u32[]{:S(2)}, u32[]{:S(2)}) collective-permute-start(bf16[192,256]{1,0:T(8,128)(2,1)S(1)} %convolution_convert_fusion.3), channel_id=1, source_target_pairs={{0,8},{4,12},{8,0},{12,4},{1,9},{5,13},{9,1},{13,5},{2,10},{6,14},... | collective-permute-start | bytes 294920 | tf_op jit(solution)/shard_map/ppermute | solution.py:30
  145.0 22.2 %collective-permute-start.56 = (f32[4,768]{1,0:T(4,128)}, f32[4,768]{1,0:T(4,128)}, u32[]{:S(2)}, u32[]{:S(2)}) collective-permute-start(f32[4,768]{1,0:T(4,128)} %pad_maximum_fusion.49), channel_id=1, source_target_pairs={{0,1},{1,0},{2,3},{3,2},{4,5},{5,4},{6,7},{7,6},{8,9},{9,8},{10,11... | collective-permute-start | bytes 36872 | tf_op jit(solution)/shard_map/ppermute | solution.py:30
  149.0 40.6 %collective-permute-start.29 = (bf16[512,768]{1,0:T(8,128)(2,1)}, bf16[512,768]{1,0:T(8,128)(2,1)}, u32[]{:S(2)}, u32[]{:S(2)}) collective-permute-start(bf16[512,768]{1,0:T(8,128)(2,1)} %convolution_convert_fusion), channel_id=1, source_target_pairs={{0,2},{1,3},{2,0},{3,1},{4,6},{5,7},{6,4},{7,5},{8,10},{9,11},{10,... | collective-permute-start | bytes 2359304 | tf_op jit(solution)/shard_map/ppermute | solution.py:30
  151.2 34.5 %collective-permute-start.30 = (bf16[2,192,768]{2,1,0:T(8,128)(2,1)}, bf16[2,192,768]{2,1,0:T(8,128)(2,1)}, u32[]{:S(2)}, u32[]{:S(2)}) collective-permute-start(bf16[2,192,768]{2,1,0:T(8,128)(2,1)} %pad_maximum_fusion.19), channel_id=1, source_target_pairs={{0,1},{1,0},{2,3},{3,2},{4,5},{5,4},{6,7},{7,6},{8,9},{9,8},{10,11... | collective-permute-start | bytes 1769480 | tf_op jit(solution)/shard_map/ppermute | solution.py:30
  170.5 10.5 %collective-permute-start.21 = (bf16[384,384]{1,0:T(8,128)(2,1)S(1)}, bf16[384,384]{1,0:T(8,128)(2,1)S(1)}, u32[]{:S(2)}, u32[]{:S(2)}) collective-permute-start(bf16[384,384]{1,0:T(8,128)(2,1)S(1)} %copy-done.56), channel_id=1, source_target_pairs={{0,16},{16,0},{1,17},{17,1},{2,18},{18,2},{3,19},{19,3},{4,20},{20... | collective-permute-start | bytes 884744 | tf_op jit(solution)/shard_map/ppermute | solution.py:30
  174.6 31.9 %collective-permute-start.57 = (f32[4,768]{1,0:T(4,128)}, f32[4,768]{1,0:T(4,128)S(1)}, u32[]{:S(2)}, u32[]{:S(2)}) collective-permute-start(f32[4,768]{1,0:T(4,128)} %fusion.139), channel_id=1, source_target_pairs={{0,2},{1,3},{2,0},{3,1},{4,6},{5,7},{6,4},{7,5},{8,10},{9,11},{10,... | collective-permute-start | bytes 36872 | tf_op jit(solution)/shard_map/ppermute | solution.py:30
  179.6 29.7 %collective-permute-start.42 = (bf16[192,256]{1,0:T(8,128)(2,1)}, bf16[192,256]{1,0:T(8,128)(2,1)}, u32[]{:S(2)}, u32[]{:S(2)}) collective-permute-start(bf16[192,256]{1,0:T(8,128)(2,1)} %bitcast.74), channel_id=1, source_target_pairs={{0,12},{4,8},{8,4},{12,0},{1,13},{5,9},{9,5},{13,1},{2,14},{6,10},... | collective-permute-start | bytes 294920 | tf_op jit(solution)/shard_map/ppermute | solution.py:30
  181.0 32.5 %collective-permute-start.41 = (bf16[192,256]{1,0:T(8,128)(2,1)}, bf16[192,256]{1,0:T(8,128)(2,1)}, u32[]{:S(2)}, u32[]{:S(2)}) collective-permute-start(bf16[192,256]{1,0:T(8,128)(2,1)} %bitcast.71), channel_id=1, source_target_pairs={{0,8},{4,12},{8,0},{12,4},{1,9},{5,13},{9,1},{13,5},{2,10},{6,14},... | collective-permute-start | bytes 294920 | tf_op jit(solution)/shard_map/ppermute | solution.py:30
  185.8 33.8 %collective-permute-start.28 = (bf16[2,256,768]{2,1,0:T(8,128)(2,1)}, bf16[2,256,768]{2,1,0:T(8,128)(2,1)}, u32[]{:S(2)}, u32[]{:S(2)}) collective-permute-start(bf16[2,256,768]{2,1,0:T(8,128)(2,1)} %pad_maximum_fusion.14), channel_id=1, source_target_pairs={{0,1},{1,0},{2,3},{3,2},{4,5},{5,4},{6,7},{7,6},{8,9},{9,8},{10,11... | collective-permute-start | bytes 2359304 | tf_op jit(solution)/shard_map/ppermute | solution.py:30
  189.6 25.3 %collective-permute-start.31 = (bf16[896,384]{1,0:T(8,128)(2,1)}, bf16[896,384]{1,0:T(8,128)(2,1)}, u32[]{:S(2)}, u32[]{:S(2)}) collective-permute-start(bf16[896,384]{1,0:T(8,128)(2,1)} %slice.883), channel_id=1, source_target_pairs={{0,16},{16,0},{1,17},{17,1},{2,18},{18,2},{3,19},{19,3},{4,20},{20... | collective-permute-start | bytes 2064392 | tf_op jit(solution)/shard_map/ppermute | solution.py:30
  206.5 10.5 %collective-permute-start.27 = (bf16[384,384]{1,0:T(8,128)(2,1)}, bf16[384,384]{1,0:T(8,128)(2,1)S(1)}, u32[]{:S(2)}, u32[]{:S(2)}) collective-permute-start(bf16[384,384]{1,0:T(8,128)(2,1)} %fusion.58), channel_id=1, source_target_pairs={{0,4},{4,0},{8,12},{12,8},{1,5},{5,1},{9,13},{13,9},{2,6},{6,2},{1... | collective-permute-start | bytes 884744 | tf_op jit(solution)/shard_map/ppermute | solution.py:30
  209.3 28.3 %collective-permute-start.58 = (f32[4,768]{1,0:T(4,128)S(1)}, f32[4,768]{1,0:T(4,128)S(1)}, u32[]{:S(2)}, u32[]{:S(2)}) collective-permute-start(f32[4,768]{1,0:T(4,128)S(1)} %add.516), channel_id=1, source_target_pairs={{0,16},{16,0},{1,17},{17,1},{2,18},{18,2},{3,19},{19,3},{4,20},{20... | collective-permute-start | bytes 36872 | tf_op jit(solution)/shard_map/ppermute | solution.py:30
  213.5 12.6 %collective-permute-start.33 = (bf16[2,4,192,256]{3,2,1,0:T(8,128)(2,1)S(1)}, bf16[2,4,192,256]{3,2,1,0:T(8,128)(2,1)S(1)}, u32[]{:S(2)}, u32[]{:S(2)}) collective-permute-start(bf16[2,4,192,256]{3,2,1,0:T(8,128)(2,1)S(1)} %pad_maximum_fusion.15), channel_id=1, source_target_pairs={{0,1},{1,0},{2,3},{3,2},{4,5},{5,4},{6,7},{7,6},{8,9},{9,8},{10,11... | collective-permute-start | bytes 2359304 | tf_op jit(solution)/shard_map/ppermute | solution.py:30
  214.9 19.4 %collective-permute-start.38 = (bf16[512,384]{1,0:T(8,128)(2,1)S(1)}, bf16[512,384]{1,0:T(8,128)(2,1)S(1)}, u32[]{:S(2)}, u32[]{:S(2)}) collective-permute-start(bf16[512,384]{1,0:T(8,128)(2,1)S(1)} %copy-done.50), channel_id=1, source_target_pairs={{0,16},{16,0},{1,17},{17,1},{2,18},{18,2},{3,19},{19,3},{4,20},{20... | collective-permute-start | bytes 1179656 | tf_op jit(solution)/shard_map/ppermute | solution.py:30
  217.0 17.6 %collective-permute-start.39 = (bf16[448,384]{1,0:T(8,128)(2,1)S(1)}, bf16[448,384]{1,0:T(8,128)(2,1)S(1)}, u32[]{:S(2)}, u32[]{:S(2)}) collective-permute-start(bf16[448,384]{1,0:T(8,128)(2,1)S(1)} %slice.888), channel_id=1, source_target_pairs={{0,2},{1,3},{2,0},{3,1},{4,6},{5,7},{6,4},{7,5},{8,10},{9,11},{10,... | collective-permute-start | bytes 1032200 | tf_op jit(solution)/shard_map/ppermute | solution.py:30
  219.7 20.1 %collective-permute-start.37 = (bf16[192,384]{1,0:T(8,128)(2,1)S(1)}, bf16[192,384]{1,0:T(8,128)(2,1)S(1)}, u32[]{:S(2)}, u32[]{:S(2)}) collective-permute-start(bf16[192,384]{1,0:T(8,128)(2,1)S(1)} %dynamic-slice_convert_fusion.5), channel_id=1, source_target_pairs={{0,8},{4,12},{8,0},{12,4},{1,9},{5,13},{9,1},{13,5},{2,10},{6,14},... | collective-permute-start | bytes 442376 | tf_op jit(solution)/shard_map/ppermute | solution.py:30
  229.6 11.6 %collective-permute-start.36 = (bf16[384,256]{1,0:T(8,128)(2,1)S(1)}, bf16[384,256]{1,0:T(8,128)(2,1)S(1)}, u32[]{:S(2)}, u32[]{:S(2)}) collective-permute-start(bf16[384,256]{1,0:T(8,128)(2,1)S(1)} %pad_maximum_fusion.35), channel_id=1, source_target_pairs={{0,12},{4,8},{8,4},{12,0},{1,13},{5,9},{9,5},{13,1},{2,14},{6,10},... | collective-permute-start | bytes 589832 | tf_op jit(solution)/shard_map/ppermute | solution.py:30
  234.4 14.0 %collective-permute-start.35 = (bf16[384,256]{1,0:T(8,128)(2,1)S(1)}, bf16[384,256]{1,0:T(8,128)(2,1)S(1)}, u32[]{:S(2)}, u32[]{:S(2)}) collective-permute-start(bf16[384,256]{1,0:T(8,128)(2,1)S(1)} %pad_maximum_fusion.34), channel_id=1, source_target_pairs={{0,8},{4,12},{8,0},{12,4},{1,9},{5,13},{9,1},{13,5},{2,10},{6,14},... | collective-permute-start | bytes 589832 | tf_op jit(solution)/shard_map/ppermute | solution.py:30
  234.6 14.7 %collective-permute-start.34 = (bf16[576,256]{1,0:T(8,128)(2,1)S(1)}, bf16[576,256]{1,0:T(8,128)(2,1)S(1)}, u32[]{:S(2)}, u32[]{:S(2)}) collective-permute-start(bf16[576,256]{1,0:T(8,128)(2,1)S(1)} %pad_maximum_fusion.27), channel_id=1, source_target_pairs={{0,4},{4,0},{8,12},{12,8},{1,5},{5,1},{9,13},{13,9},{2,6},{6,2},{1... | collective-permute-start | bytes 884744 | tf_op jit(solution)/shard_map/ppermute | solution.py:30
  237.6 18.6 %collective-permute-start.40 = (bf16[480,384]{1,0:T(8,128)(2,1)S(1)}, bf16[480,384]{1,0:T(8,128)(2,1)S(1)}, u32[]{:S(2)}, u32[]{:S(2)}) collective-permute-start(bf16[480,384]{1,0:T(8,128)(2,1)S(1)} %dynamic-slice_convert_fusion), channel_id=1, source_target_pairs={{0,4},{4,0},{8,12},{12,8},{1,5},{5,1},{9,13},{13,9},{2,6},{6,2},{1... | collective-permute-start | bytes 1105928 | tf_op jit(solution)/shard_map/ppermute | solution.py:30
  239.8 20.5 %collective-permute-start.59 = (f32[4,768]{1,0:T(4,128)S(1)}, f32[4,768]{1,0:T(4,128)S(1)}, u32[]{:S(2)}, u32[]{:S(2)}) collective-permute-start(f32[4,768]{1,0:T(4,128)S(1)} %add.517), channel_id=1, source_target_pairs={{0,4},{4,0},{8,12},{12,8},{1,5},{5,1},{9,13},{13,9},{2,6},{6,2},{1... | collective-permute-start | bytes 36872 | tf_op jit(solution)/shard_map/ppermute | solution.py:30
  241.1 30.3 %collective-permute-start.45 = (bf16[576,384]{1,0:T(8,128)(2,1)S(1)}, bf16[576,384]{1,0:T(8,128)(2,1)S(1)}, u32[]{:S(2)}, u32[]{:S(2)}) collective-permute-start(bf16[576,384]{1,0:T(8,128)(2,1)S(1)} %slice.884), channel_id=1, source_target_pairs={{0,16},{16,0},{1,17},{17,1},{2,18},{18,2},{3,19},{19,3},{4,20},{20... | collective-permute-start | bytes 1327112 | tf_op jit(solution)/shard_map/ppermute | solution.py:30
  260.4 10.5 %collective-permute-start.60 = (f32[4,768]{1,0:T(4,128)S(1)}, f32[4,768]{1,0:T(4,128)S(1)}, u32[]{:S(2)}, u32[]{:S(2)}) collective-permute-start(f32[4,768]{1,0:T(4,128)S(1)} %add.518), channel_id=1, source_target_pairs={{0,8},{4,12},{8,0},{12,4},{1,9},{5,13},{9,1},{13,5},{2,10},{6,14},... | collective-permute-start | bytes 36872 | tf_op jit(solution)/shard_map/ppermute | solution.py:30
  260.9 16.9 %collective-permute-start.53 = (bf16[240,384]{1,0:T(8,128)(2,1)S(1)}, bf16[240,384]{1,0:T(8,128)(2,1)S(1)}, u32[]{:S(2)}, u32[]{:S(2)}) collective-permute-start(bf16[240,384]{1,0:T(8,128)(2,1)S(1)} %dynamic-slice_convert_fusion.4), channel_id=1, source_target_pairs={{0,8},{4,12},{8,0},{12,4},{1,9},{5,13},{9,1},{13,5},{2,10},{6,14},... | collective-permute-start | bytes 552968 | tf_op jit(solution)/shard_map/ppermute | solution.py:30
  263.5 14.1 %collective-permute-start.50 = (bf16[192,384]{1,0:T(8,128)(2,1)S(1)}, bf16[192,384]{1,0:T(8,128)(2,1)S(1)}, u32[]{:S(2)}, u32[]{:S(2)}) collective-permute-start(bf16[192,384]{1,0:T(8,128)(2,1)S(1)} %add_convert_fusion.3), channel_id=1, source_target_pairs={{0,8},{4,12},{8,0},{12,4},{1,9},{5,13},{9,1},{13,5},{2,10},{6,14},... | collective-permute-start | bytes 442376 | tf_op jit(solution)/shard_map/ppermute | solution.py:30
  264.1 26.0 %collective-permute-start.43 = (bf16[256,768]{1,0:T(8,128)(2,1)S(1)}, bf16[256,768]{1,0:T(8,128)(2,1)S(1)}, u32[]{:S(2)}, u32[]{:S(2)}) collective-permute-start(bf16[256,768]{1,0:T(8,128)(2,1)S(1)} %get-tuple-element.273), channel_id=1, source_target_pairs={{0,2},{1,3},{2,0},{3,1},{4,6},{5,7},{6,4},{7,5},{8,10},{9,11},{10,... | collective-permute-start | bytes 1179656 | tf_op jit(solution)/shard_map/ppermute | solution.py:30
  277.7 16.3 %collective-permute-start.51 = (bf16[384,384]{1,0:T(8,128)(2,1)S(1)}, bf16[384,384]{1,0:T(8,128)(2,1)S(1)}, u32[]{:S(2)}, u32[]{:S(2)}) collective-permute-start(bf16[384,384]{1,0:T(8,128)(2,1)S(1)} %pad_maximum_fusion.30), channel_id=1, source_target_pairs={{0,4},{4,0},{8,12},{12,8},{1,5},{5,1},{9,13},{13,9},{2,6},{6,2},{1... | collective-permute-start | bytes 884744 | tf_op jit(solution)/shard_map/ppermute | solution.py:30
  277.8 10.4 %collective-permute-start.54 = (bf16[240,384]{1,0:T(8,128)(2,1)S(1)}, bf16[240,384]{1,0:T(8,128)(2,1)S(1)}, u32[]{:S(2)}, u32[]{:S(2)}) collective-permute-start(bf16[240,384]{1,0:T(8,128)(2,1)S(1)} %add_convert_fusion.2), channel_id=1, source_target_pairs={{0,8},{4,12},{8,0},{12,4},{1,9},{5,13},{9,1},{13,5},{2,10},{6,14},... | collective-permute-start | bytes 552968 | tf_op jit(solution)/shard_map/ppermute | solution.py:30
  279.9 10.4 %collective-permute-start.47 = (bf16[288,384]{1,0:T(8,128)(2,1)S(1)}, bf16[288,384]{1,0:T(8,128)(2,1)S(1)}, u32[]{:S(2)}, u32[]{:S(2)}) collective-permute-start(bf16[288,384]{1,0:T(8,128)(2,1)S(1)} %fusion.94), channel_id=1, source_target_pairs={{2,0},{3,1},{6,4},{7,5},{8,10},{9,11},{12,14},{13,15},{18,16},{19,... | collective-permute-start | bytes 663560 | tf_op jit(solution)/shard_map/ppermute | solution.py:624
  288.3 17.5 %collective-permute-start.55 = (bf16[480,384]{1,0:T(8,128)(2,1)S(1)}, bf16[480,384]{1,0:T(8,128)(2,1)S(1)}, u32[]{:S(2)}, u32[]{:S(2)}) collective-permute-start(bf16[480,384]{1,0:T(8,128)(2,1)S(1)} %pad_maximum_fusion.25), channel_id=1, source_target_pairs={{0,4},{4,0},{8,12},{12,8},{1,5},{5,1},{9,13},{13,9},{2,6},{6,2},{1... | collective-permute-start | bytes 1105928 | tf_op jit(solution)/shard_map/ppermute | solution.py:30
  290.2 15.8 %collective-permute-start.44 = (bf16[2,256,768]{2,1,0:T(8,128)(2,1)S(1)}, bf16[2,256,768]{2,1,0:T(8,128)(2,1)S(1)}, u32[]{:S(2)}, u32[]{:S(2)}) collective-permute-start(bf16[2,256,768]{2,1,0:T(8,128)(2,1)S(1)} %pad_maximum_fusion.16), channel_id=1, source_target_pairs={{0,1},{1,0},{2,3},{3,2},{4,5},{5,4},{6,7},{7,6},{8,9},{9,8},{10,11... | collective-permute-start | bytes 2359304 | tf_op jit(solution)/shard_map/ppermute | solution.py:30
  290.4 11.1 %collective-permute-start.48 = (bf16[288,384]{1,0:T(8,128)(2,1)S(1)}, bf16[288,384]{1,0:T(8,128)(2,1)S(1)}, u32[]{:S(2)}, u32[]{:S(2)}) collective-permute-start(bf16[288,384]{1,0:T(8,128)(2,1)S(1)} %add_convert_fusion.1), channel_id=1, source_target_pairs={{0,8},{1,9},{4,12},{5,13},{10,2},{11,3},{14,6},{15,7},{16,24},{17,... | collective-permute-start | bytes 663560 | tf_op jit(solution)/shard_map/ppermute | solution.py:629
  301.5 9.8 %collective-permute-start.49 = (bf16[288,384]{1,0:T(8,128)(2,1)S(1)}, bf16[288,384]{1,0:T(8,128)(2,1)S(1)}, u32[]{:S(2)}, u32[]{:S(2)}) collective-permute-start(bf16[288,384]{1,0:T(8,128)(2,1)S(1)} %broadcast_select_fusion.4), channel_id=1, source_target_pairs={{0,4},{4,0},{8,12},{12,8},{1,5},{5,1},{9,13},{13,9},{2,6},{6,2},{1... | collective-permute-start | bytes 663560 | tf_op jit(solution)/shard_map/ppermute | solution.py:30
  (91 other events, 617.1 us)

commit v2 on v1

--- a/solution.py
+++ b/solution.py
@@ -373,7 +373,7 @@
 
     def ctx_third(keep, got):
         keep = (keep + got.astype(F32)).astype(BF16)
-        return join_bit(keep, swap(keep, "ctx", 2), bit1)
+        return keep, swap(keep, "ctx", 2)
 
     def own_tokens(value):
         return lax.dynamic_slice(value, (y, c * rows, 0), (1, rows, value.shape[2]))[0]
@@ -555,8 +555,7 @@
     lin_q = [None, None, turn_q(dq_b[0], 2), turn_q(dq_b[1], 3)]
     got_q = [None, None, swap(lin_q[2], "ctx", 2), swap(lin_q[3], "ctx", 3)]
     own_out = turn(second)
-    *up_got, far_out = together([*up_got, swap(own_out, "tp", 2)], dq_b)
-    outs = jnp.stack([own_out, far_out])
+    up_got = together(up_got, dq_b)
     up = last_stage(up_low, up_high, *up_got)
     up_keep, up_got = ctx_first(up)
     in_low, in_high, *in_got = second_stage(inside[0], in_high, *in_got, dq_b)
@@ -580,8 +579,8 @@
     sums = sums + after(swap(sums, "tp", 2), mark)
     sibling = exchange(jnp.stack([sent_key, sent_value]), "tp", 1)
     got_q = [None, None] + together(got_q[2:], mark)
-    up_got, got_outs = together([up_got, swap(outs, "tp", 1)], mark)
-    up_keep, up_got = ctx_second(up_keep, up_got)
+    far_out = swap(after(own_out, mark, sent_key), "tp", 2)
+    up_keep, up_got = ctx_second(up_keep, after(up_got, mark))
     inside = last_stage(in_low, in_high, *in_got, mark)
     d_key = d_key + sibling[0]
     d_value = d_value + sibling[1]
@@ -613,14 +612,17 @@
 
     in_grad = turn(input_own)
     in_grad = jnp.stack([in_grad, swap(in_grad, "tp", 2)])
-    outputs = spread(outs, got_outs)
     input_grad = spread(in_grad, swap(in_grad, "tp", 1))
 
     both = ("ctx", "tp")
     keep, send = split_bit(part, c)
     part = keep + exchange(send, "tp", 1)
     in_keep, in_got = ctx_second(in_keep, in_got)
-    up = ctx_third(up_keep, up_got)
+    up, up_far = ctx_third(up_keep, up_got)
+    in_got, up_far, far_out = together([in_got, up_far, far_out], part)
+    outs = jnp.stack([own_out, far_out])
+    got_outs = swap(outs, "tp", 1)
+    up = join_bit(up, up_far, bit1)
     part = part + lax.ppermute(
         part.astype(BF16), both,
         [(g * 4 + s, g * 4 + (s ^ 2)) for g in range(4) for s in range(4) if s // 2 != g // 2],
@@ -631,8 +633,10 @@
         [(g * 4 + s, (g ^ 2) * 4 + s) for g in range(4) for s in range(4) if s // 2 == g // 2],
     )
     held = jnp.where(y == z // 2, part, moved)
-    inside = ctx_third(in_keep, in_got)
+    inside, in_far = ctx_third(in_keep, in_got)
+    inside = join_bit(inside, in_far, bit1)
     shard_up = join_bit(up, swap(up, "ctx", 1), bit0).astype(F32)
+    outputs = spread(outs, got_outs)
     moved = after(swap(held, "ctx", 1), outputs, input_grad, shard_up)
     shard_in = join_bit(inside, swap(inside, "ctx", 1), bit0).astype(F32)
     mine = jnp.where(c == bit0, held, moved)
@@ -644,7 +648,7 @@
     got = swap(sums, "dp", 1, 2) if pair else None
     sums = sums + after(got, *lin) if pair else lax.psum(sums, "dp")
     sums = sums + after(swap(sums, "ctx", 1), input_own)
-    sums = sums + swap(sums, "ctx", 2)
+    sums = sums + after(swap(sums, "ctx", 2), held)
 
     return (
         outputs,

time: 318 us -> 309 us (0.972)
  waiting for transfers between devices: 71.5 us -> 66.5 us
  starting transfers between devices: 73.8 us -> 70.5 us
    ppermute x58, waiting for transfers between devices: 65.2 us -> 59.3 us  [swap(): return lax.ppermute(value, axis, [(i, i ^ k) for i in range(size)])]
    unnamed x171 -> x173, local copies, waits for them, and re-layouts: 16.7 us -> 15 us
  transfers between devices with their start and end apart: 61 -> 61, of which waited for: 19 -> 21; matrix products, arithmetic and copies ran while one was open for 29% -> 29% of each run, Pallas kernels for 13% -> 13%
where the time goes in v2:
time: 309 us; the launch traced here: 304 us
  starting transfers between devices  70.5 us (23%)
  waiting for transfers between devices  66.5 us (22%)
  Pallas kernels  47.5 us (15%)
  other arithmetic  44.1 us (14%)
  local copies, waits for them, and re-layouts  38.5 us (12%)
  matrix products  33.5 us (11%)
  between operations  3.18 us (1%)
    ppermute x58, starting transfers between devices, swap(): return lax.ppermute(value, axis, [(i, i ^ k) for i in range(size)])  65.4 us
    ppermute x58, waiting for transfers between devices, swap(): return lax.ppermute(value, axis, [(i, i ^ k) for i in range(size)])  59.3 us
    dot_general x38, matrix products, dot(): lax.dot_general(left, right, (((left_dim,), (right_dim,)), ((), ())), pre...  33.5 us
    pallas_call x2, Pallas kernels, attend_back(): pl.pallas_call(functools.partial(attend_back_kernel, first), grid_spec=pl...  24.7 us
    pallas_call x3, Pallas kernels, attend(): pl.pallas_call(functools.partial(attend_kernel, first), grid_spec=pltpu.P...  22.8 us
    unnamed x173, local copies, waits for them, and re-layouts  15 us
    ppermute x1, waiting for transfers between devices, per_device(): lax.ppermute(part, both, [(g * 4 + s, (g ^ 2) * 4 + s) for g in range(4)...  7.23 us
  transfers between devices with their start and end apart: 61, of which 21 were waited for; matrix products, arithmetic and copies ran while one was open for 29% of the time, Pallas kernels for 13%

profile of v2, /device:TPU:0, one launch (start us, length us, event | category | flops | bytes accessed | tf_op | source)
XLA Modules:
  0.0 303.9 jit_solution(13839442180588846503)
XLA Ops:
  3.5 3.1 %collective-permute-start.1 = (bf16[384,576]{0,1:T(8,128)(2,1)S(1)}, bf16[384,576]{0,1:T(8,128)(2,1)S(1)}, u32[]{:S(2)}, u32[]{:S(2)}) collective-permute-start(bf16[384,576]{0,1:T(8,128)(2,1)S(1)} %constant_dynamic-update-slice_fusion), channel_id=1, source_target_pairs={{0,2},{1,3},{2,0},{3,1},{4,6},{5,7},{6,4},{7,5},{8,10},{9,11},{10,... | collective-permute-start | bytes 1327112 | tf_op jit(solution)/shard_map/ppermute | solution.py:30
  10.2 3.0 collective-permute-start.5
  13.2 1.6 collective-permute-start.4
  16.7 9.5 %collective-permute-done.1 = bf16[384,576]{0,1:T(8,128)(2,1)S(1)} collective-permute-done((bf16[384,576]{0,1:T(8,128)(2,1)S(1)}, bf16[384,576]{0,1:T(8,128)(2,1)S(1)}, u32[]{:S(2)}, u32[]{:S(2)}) %collective-permute-start.1) | collective-permute-done | bytes 442400 | tf_op jit(solution)/shard_map/ppermute | solution.py:30
  34.6 2.3 pad_maximum_fusion.9
  36.9 1.7 collective-permute-start.6
  41.6 1.5 fusion.156
  43.9 1.7 fusion.36
  45.6 3.0 %collective-permute-done.6 = bf16[256,768]{1,0:T(8,128)(2,1)S(1)} collective-permute-done((bf16[256,768]{1,0:T(8,128)(2,1)}, bf16[256,768]{1,0:T(8,128)(2,1)S(1)}, u32[]{:S(2)}, u32[]{:S(2)}) %collective-permute-start.6) | collective-permute-done | bytes 393248 | tf_op jit(solution)/shard_map/ppermute | solution.py:30
  55.9 11.7 %attend.3 = (bf16[2,192,256]{2,1,0:T(8,128)(2,1)}, f32[2,3,256]{2,1,0:T(4,128)}) custom-call(s32[32]{0:T(128)} %reshape.374.flags, s32[8]{0:T(128)} %pad_add_fusion.2.bases, bf16[4,192,256]{2,1,0:T(8,128)(2,1)} %pad_maximum_fusion.21.q_ref, bf16[8,192,256]{2,1,0:T(8,128)(2,1)} %copy-done, bf16[8,192,256]{2,1,0:T(8,128)(2,1)} %copy-done.3, ...), custom_call_target="tpu_custom_call" | custom-call | tf_op jit(solution)/shard_map/attend/pallas_call | solution.py:165
  67.6 2.5 collective-permute-done.10
  72.6 2.0 slice.484
  76.2 2.7 collective-permute-start.11
  79.1 2.6 constant_dynamic-update-slice_fusion.22
  81.7 4.0 %attend.4 = (bf16[1,192,256]{2,1,0:T(8,128)(2,1)}, f32[1,3,256]{2,1,0:T(4,128)}) custom-call(s32[32]{0:T(128)} %reshape.374.flags, s32[8]{0:T(128)} %pad_add_fusion.2.bases, bf16[4,192,256]{2,1,0:T(8,128)(2,1)} %pad_maximum_fusion.21.q_ref, bf16[8,192,256]{2,1,0:T(8,128)(2,1)} %copy-done, bf16[8,192,256]{2,1,0:T(8,128)(2,1)} %copy-done.3, ...), custom_call_target="tpu_custom_call" | custom-call | tf_op jit(solution)/shard_map/attend/pallas_call | solution.py:165
  86.0 1.6 collective-permute-done.13
  87.6 3.3 %collective-permute-done.12 = bf16[864,384]{1,0:T(8,128)(2,1)} collective-permute-done((bf16[864,384]{1,0:T(8,128)(2,1)}, bf16[864,384]{1,0:T(8,128)(2,1)}, u32[]{:S(2)}, u32[]{:S(2)}) %collective-permute-start.12) | collective-permute-done | bytes 663584 | tf_op jit(solution)/shard_map/ppermute | solution.py:30
  90.9 7.1 %attend.5 = (bf16[1,192,256]{2,1,0:T(8,128)(2,1)}, f32[1,3,256]{2,1,0:T(4,128)}) custom-call(s32[32]{0:T(128)} %reshape.374.flags, s32[8]{0:T(128)} %pad_add_fusion.2.bases, bf16[4,192,256]{2,1,0:T(8,128)(2,1)} %pad_maximum_fusion.21.q_ref, bf16[8,192,256]{2,1,0:T(8,128)(2,1)} %copy-done, bf16[8,192,256]{2,1,0:T(8,128)(2,1)} %copy-done.3, ...), custom_call_target="tpu_custom_call" | custom-call | tf_op jit(solution)/shard_map/attend/pallas_call | solution.py:165
  98.0 2.6 constant_dynamic-update-slice_fusion.21
  103.0 1.8 fusion.155
  111.1 2.9 fusion.9
  114.0 2.3 fusion.147
  123.7 2.5 fusion.10
  128.3 1.6 collective-permute-start.21
  135.3 2.6 collective-permute-start.23
  150.7 13.7 %attend_back.2 = (f32[2,192,256]{2,1,0:T(8,128)}, f32[8,192,256]{2,1,0:T(8,128)}, f32[8,192,256]{2,1,0:T(8,128)}) custom-call(s32[32]{0:T(128)} %reshape.374.flags, s32[8]{0:T(128)} %pad_add_fusion.2.bases, bf16[4,192,256]{2,1,0:T(8,128)(2,1)} %pad_maximum_fusion.21.q_ref, bf16[8,192,256]{2,1,0:T(8,128)(2,1)} %copy-done, bf16[8,192,256]{2,1,0:T(8,128)(2,1)} %copy-done.3, ...), custom_call_target="tpu_custom_call" | custom-call | tf_op jit(solution)/shard_map/attend_back/pallas_call | solution.py:270
  167.9 1.6 fusion.25
  173.3 5.2 %collective-permute-done.30 = bf16[384,384]{1,0:T(8,128)(2,1)S(1)} collective-permute-done((bf16[384,384]{1,0:T(8,128)(2,1)S(1)}, bf16[384,384]{1,0:T(8,128)(2,1)S(1)}, u32[]{:S(2)}, u32[]{:S(2)}) %collective-permute-start.30) | collective-permute-done | bytes 294944 | tf_op jit(solution)/shard_map/ppermute | solution.py:30
  179.2 3.6 %collective-permute-start.45 = (bf16[192,256]{1,0:T(8,128)(2,1)}, bf16[192,256]{1,0:T(8,128)(2,1)}, u32[]{:S(2)}, u32[]{:S(2)}) collective-permute-start(bf16[192,256]{1,0:T(8,128)(2,1)} %bitcast.70), channel_id=1, source_target_pairs={{0,8},{4,12},{8,0},{12,4},{1,9},{5,13},{9,1},{13,5},{2,10},{6,14},... | collective-permute-start | bytes 294920 | tf_op jit(solution)/shard_map/ppermute | solution.py:30
  189.9 1.9 convert_add_fusion
  193.1 11.0 %attend_back.3 = (f32[2,192,256]{2,1,0:T(8,128)}, f32[4,192,256]{2,1,0:T(8,128)}, f32[4,192,256]{2,1,0:T(8,128)}, bf16[4,192,256]{2,1,0:T(8,128)(2,1)}, bf16[4,192,256]{2,1,0:T(8,128)(2,1)}) custom-call(s32[32]{0:T(128)} %reshape.374.flags, s32[8]{0:T(128)} %pad_add_fusion.2.bases, bf16[4,192,256]{2,1,0:T(8,128)(2,1)} %pad_maximum_fusion.21.q_ref, ...), custom_call_target="tpu_custom_call" | custom-call | tf_op jit(solution)/shard_map/attend_back/pallas_call | solution.py:270
  204.9 4.1 %collective-permute-start.58 = (f32[4,768]{1,0:T(4,128)S(1)}, f32[4,768]{1,0:T(4,128)S(1)}, u32[]{:S(2)}, u32[]{:S(2)}) collective-permute-start(f32[4,768]{1,0:T(4,128)S(1)} %add.516), channel_id=1, source_target_pairs={{0,16},{16,0},{1,17},{17,1},{2,18},{18,2},{3,19},{19,3},{4,20},{20... | collective-permute-start | bytes 36872 | tf_op jit(solution)/shard_map/ppermute | solution.py:30
  211.8 3.1 %collective-permute-start.37 = (bf16[192,384]{1,0:T(8,128)(2,1)S(1)}, bf16[192,384]{1,0:T(8,128)(2,1)S(1)}, u32[]{:S(2)}, u32[]{:S(2)}) collective-permute-start(bf16[192,384]{1,0:T(8,128)(2,1)S(1)} %dynamic-slice_convert_fusion.5), channel_id=1, source_target_pairs={{0,8},{4,12},{8,0},{12,4},{1,9},{5,13},{9,1},{13,5},{2,10},{6,14},... | collective-permute-start | bytes 442376 | tf_op jit(solution)/shard_map/ppermute | solution.py:30
  217.5 1.8 collective-permute-start.28
  225.3 1.9 collective-permute-start.34
  227.3 1.9 collective-permute-start.33
  232.9 5.8 %collective-permute-start.59 = (f32[4,768]{1,0:T(4,128)S(1)}, f32[4,768]{1,0:T(4,128)S(1)}, u32[]{:S(2)}, u32[]{:S(2)}) collective-permute-start(f32[4,768]{1,0:T(4,128)S(1)} %add.517), channel_id=1, source_target_pairs={{0,4},{4,0},{8,12},{12,8},{1,5},{5,1},{9,13},{13,9},{2,6},{6,2},{1... | collective-permute-start | bytes 36872 | tf_op jit(solution)/shard_map/ppermute | solution.py:30
  238.7 2.3 collective-permute-done.34
  241.4 7.1 %collective-permute-done.38 = bf16[480,384]{1,0:T(8,128)(2,1)S(1)} collective-permute-done((bf16[480,384]{1,0:T(8,128)(2,1)S(1)}, bf16[480,384]{1,0:T(8,128)(2,1)S(1)}, u32[]{:S(2)}, u32[]{:S(2)}) %collective-permute-start.38) | collective-permute-done | bytes 368672 | tf_op jit(solution)/shard_map/ppermute | solution.py:30
  252.6 2.6 collective-permute-start.40
  259.8 6.0 %collective-permute-done.40 = bf16[192,384]{1,0:T(8,128)(2,1)S(1)} collective-permute-done((bf16[192,384]{1,0:T(8,128)(2,1)S(1)}, bf16[192,384]{1,0:T(8,128)(2,1)S(1)}, u32[]{:S(2)}, u32[]{:S(2)}) %collective-permute-start.40) | collective-permute-done | bytes 147488 | tf_op jit(solution)/shard_map/ppermute | solution.py:30
  265.8 3.5 %collective-permute-done.39 = bf16[240,384]{1,0:T(8,128)(2,1)S(1)} collective-permute-done((bf16[240,384]{1,0:T(8,128)(2,1)S(1)}, bf16[240,384]{1,0:T(8,128)(2,1)S(1)}, u32[]{:S(2)}, u32[]{:S(2)}) %collective-permute-start.39) | collective-permute-done | bytes 184352 | tf_op jit(solution)/shard_map/ppermute | solution.py:30
  269.5 2.3 collective-permute-start.52
  272.1 7.1 %collective-permute-done.54 = bf16[240,384]{1,0:T(8,128)(2,1)S(1)} collective-permute-done((bf16[240,384]{1,0:T(8,128)(2,1)S(1)}, bf16[240,384]{1,0:T(8,128)(2,1)S(1)}, u32[]{:S(2)}, u32[]{:S(2)}) %collective-permute-start.54) | collective-permute-done | bytes 184352 | tf_op jit(solution)/shard_map/ppermute | solution.py:30
  279.4 2.7 collective-permute-done.52
  282.1 2.4 collective-permute-start.50
  285.7 7.2 %collective-permute-done.50 = bf16[288,384]{1,0:T(8,128)(2,1)S(1)} collective-permute-done((bf16[288,384]{1,0:T(8,128)(2,1)S(1)}, bf16[288,384]{1,0:T(8,128)(2,1)S(1)}, u32[]{:S(2)}, u32[]{:S(2)}) %collective-permute-start.50) | collective-permute-done | bytes 221216 | tf_op jit(solution)/shard_map/ppermute | solution.py:631
  293.0 2.5 collective-permute-start.51
  (480 shorter events, 118.2 us)
Async XLA Ops:
  3.5 22.7 %collective-permute-start.1 = (bf16[384,576]{0,1:T(8,128)(2,1)S(1)}, bf16[384,576]{0,1:T(8,128)(2,1)S(1)}, u32[]{:S(2)}, u32[]{:S(2)}) collective-permute-start(bf16[384,576]{0,1:T(8,128)(2,1)S(1)} %constant_dynamic-update-slice_fusion), channel_id=1, source_target_pairs={{0,2},{1,3},{2,0},{3,1},{4,6},{5,7},{6,4},{7,5},{8,10},{9,11},{10,... | collective-permute-start | bytes 1327112 | tf_op jit(solution)/shard_map/ppermute | solution.py:30
  6.5 21.0 %collective-permute-start.2 = (bf16[384,576]{0,1:T(8,128)(2,1)S(1)}, bf16[384,576]{0,1:T(8,128)(2,1)S(1)}, u32[]{:S(2)}, u32[]{:S(2)}) collective-permute-start(bf16[384,576]{0,1:T(8,128)(2,1)S(1)} %constant_dynamic-update-slice_fusion), channel_id=1, source_target_pairs={{0,18},{1,19},{2,16},{3,17},{16,2},{17,3},{18,0},{19,1},{4,22},{5,... | collective-permute-start | bytes 1327112 | tf_op jit(solution)/shard_map/ppermute | solution.py:335
  8.0 19.5 %collective-permute-start = (bf16[384,576]{0,1:T(8,128)(2,1)S(1)}, bf16[384,576]{0,1:T(8,128)(2,1)S(1)}, u32[]{:S(2)}, u32[]{:S(2)}) collective-permute-start(bf16[384,576]{0,1:T(8,128)(2,1)S(1)} %constant_dynamic-update-slice_fusion), channel_id=1, source_target_pairs={{0,16},{16,0},{1,17},{17,1},{2,18},{18,2},{3,19},{19,3},{4,20},{20... | collective-permute-start | bytes 1327112 | tf_op jit(solution)/shard_map/ppermute | solution.py:30
  10.2 26.7 %collective-permute-start.5 = (bf16[256,768]{1,0:T(8,128)(2,1)}, bf16[256,768]{1,0:T(8,128)(2,1)}, u32[]{:S(2)}, u32[]{:S(2)}) collective-permute-start(bf16[256,768]{1,0:T(8,128)(2,1)} %pad_maximum_fusion.20), channel_id=1, source_target_pairs={{0,8},{4,12},{8,0},{12,4},{1,9},{5,13},{9,1},{13,5},{2,10},{6,14},... | collective-permute-start | bytes 1179656 | tf_op jit(solution)/shard_map/ppermute | solution.py:30
  13.2 36.4 %collective-permute-start.4 = (bf16[256,768]{1,0:T(8,128)(2,1)}, bf16[256,768]{1,0:T(8,128)(2,1)}, u32[]{:S(2)}, u32[]{:S(2)}) collective-permute-start(bf16[256,768]{1,0:T(8,128)(2,1)} %pad_maximum_fusion.20), channel_id=1, source_target_pairs={{0,4},{4,0},{8,12},{12,8},{1,5},{5,1},{9,13},{13,9},{2,6},{6,2},{1... | collective-permute-start | bytes 1179656 | tf_op jit(solution)/shard_map/ppermute | solution.py:30
  29.0 12.6 %collective-permute-start.3 = (bf16[2,768,576]{1,2,0:T(8,128)(2,1)}, bf16[2,768,576]{1,2,0:T(8,128)(2,1)}, u32[]{:S(2)}, u32[]{:S(2)}) collective-permute-start(bf16[2,768,576]{1,2,0:T(8,128)(2,1)} %pad_maximum_fusion.3), channel_id=1, source_target_pairs={{0,1},{1,0},{2,3},{3,2},{4,5},{5,4},{6,7},{7,6},{8,9},{9,8},{10,11... | collective-permute-start | bytes 5308424 | tf_op jit(solution)/shard_map/ppermute | solution.py:30
  36.9 11.7 %collective-permute-start.6 = (bf16[256,768]{1,0:T(8,128)(2,1)}, bf16[256,768]{1,0:T(8,128)(2,1)S(1)}, u32[]{:S(2)}, u32[]{:S(2)}) collective-permute-start(bf16[256,768]{1,0:T(8,128)(2,1)} %collective-permute-done.5), channel_id=1, source_target_pairs={{0,4},{4,0},{8,12},{12,8},{1,5},{5,1},{9,13},{13,9},{2,6},{6,2},{1... | collective-permute-start | bytes 1179656 | tf_op jit(solution)/shard_map/ppermute | solution.py:30
  38.6 31.5 %collective-permute-start.10 = (bf16[1728,384]{1,0:T(8,128)(2,1)}, bf16[1728,384]{1,0:T(8,128)(2,1)S(1)}, u32[]{:S(2)}, u32[]{:S(2)}) collective-permute-start(bf16[1728,384]{1,0:T(8,128)(2,1)} %pad_maximum_fusion.9), channel_id=1, source_target_pairs={{0,2},{1,3},{2,0},{3,1},{4,6},{5,7},{6,4},{7,5},{8,10},{9,11},{10,... | collective-permute-start | bytes 3981320 | tf_op jit(solution)/shard_map/ppermute | solution.py:30
  40.1 32.4 %collective-permute-start.9 = (bf16[1728,384]{1,0:T(8,128)(2,1)}, bf16[1728,384]{1,0:T(8,128)(2,1)}, u32[]{:S(2)}, u32[]{:S(2)}) collective-permute-start(bf16[1728,384]{1,0:T(8,128)(2,1)} %pad_maximum_fusion.9), channel_id=1, source_target_pairs={{0,16},{16,0},{1,17},{17,1},{2,18},{18,2},{3,19},{19,3},{4,20},{20... | collective-permute-start | bytes 3981320 | tf_op jit(solution)/shard_map/ppermute | solution.py:30
  71.1 16.5 %collective-permute-start.13 = (bf16[864,384]{1,0:T(8,128)(2,1)}, bf16[864,384]{1,0:T(8,128)(2,1)S(1)}, u32[]{:S(2)}, u32[]{:S(2)}) collective-permute-start(bf16[864,384]{1,0:T(8,128)(2,1)} %slice.485), channel_id=1, source_target_pairs={{0,16},{16,0},{1,17},{17,1},{2,18},{18,2},{3,19},{19,3},{4,20},{20... | collective-permute-start | bytes 1990664 | tf_op jit(solution)/shard_map/ppermute | solution.py:30
  74.6 16.3 %collective-permute-start.12 = (bf16[864,384]{1,0:T(8,128)(2,1)}, bf16[864,384]{1,0:T(8,128)(2,1)}, u32[]{:S(2)}, u32[]{:S(2)}) collective-permute-start(bf16[864,384]{1,0:T(8,128)(2,1)} %slice.484), channel_id=1, source_target_pairs={{0,2},{1,3},{2,0},{3,1},{4,6},{5,7},{6,4},{7,5},{8,10},{9,11},{10,... | collective-permute-start | bytes 1990664 | tf_op jit(solution)/shard_map/ppermute | solution.py:30
  76.2 9.7 %collective-permute-start.11 = (bf16[192,256]{1,0:T(8,128)(2,1)S(1)}, bf16[192,256]{1,0:T(8,128)(2,1)S(1)}, u32[]{:S(2)}, u32[]{:S(2)}) collective-permute-start(bf16[192,256]{1,0:T(8,128)(2,1)S(1)} %get-tuple-element.333), channel_id=1, source_target_pairs={{0,8},{4,12},{8,0},{12,4},{1,9},{5,13},{9,1},{13,5},{2,10},{6,14},... | collective-permute-start | bytes 294920 | tf_op jit(solution)/shard_map/ppermute | solution.py:30
  128.3 20.1 %collective-permute-start.21 = (bf16[384,768]{1,0:T(8,128)(2,1)S(1)}, bf16[384,768]{1,0:T(8,128)(2,1)S(1)}, u32[]{:S(2)}, u32[]{:S(2)}) collective-permute-start(bf16[384,768]{1,0:T(8,128)(2,1)S(1)} %convolution_convert_fusion.1), channel_id=1, source_target_pairs={{0,2},{1,3},{2,0},{3,1},{4,6},{5,7},{6,4},{7,5},{8,10},{9,11},{10,... | collective-permute-start | bytes 1769480 | tf_op jit(solution)/shard_map/ppermute | solution.py:30
  131.9 35.9 %collective-permute-start.22 = (bf16[768,384]{1,0:T(8,128)(2,1)}, bf16[768,384]{1,0:T(8,128)(2,1)}, u32[]{:S(2)}, u32[]{:S(2)}) collective-permute-start(bf16[768,384]{1,0:T(8,128)(2,1)} %fusion.26), channel_id=1, source_target_pairs={{0,16},{16,0},{1,17},{17,1},{2,18},{18,2},{3,19},{19,3},{4,20},{20... | collective-permute-start | bytes 1769480 | tf_op jit(solution)/shard_map/ppermute | solution.py:30
  135.3 10.6 %collective-permute-start.23 = (bf16[192,256]{1,0:T(8,128)(2,1)S(1)}, bf16[192,256]{1,0:T(8,128)(2,1)S(1)}, u32[]{:S(2)}, u32[]{:S(2)}) collective-permute-start(bf16[192,256]{1,0:T(8,128)(2,1)S(1)} %convolution_convert_fusion.3), channel_id=1, source_target_pairs={{0,8},{4,12},{8,0},{12,4},{1,9},{5,13},{9,1},{13,5},{2,10},{6,14},... | collective-permute-start | bytes 294920 | tf_op jit(solution)/shard_map/ppermute | solution.py:30
  138.4 9.1 %collective-permute-start.31 = (bf16[192,256]{1,0:T(8,128)(2,1)S(1)}, bf16[192,256]{1,0:T(8,128)(2,1)S(1)}, u32[]{:S(2)}, u32[]{:S(2)}) collective-permute-start(bf16[192,256]{1,0:T(8,128)(2,1)S(1)} %convolution_convert_fusion.4), channel_id=1, source_target_pairs={{0,4},{4,0},{8,12},{12,8},{1,5},{5,1},{9,13},{13,9},{2,6},{6,2},{1... | collective-permute-start | bytes 294920 | tf_op jit(solution)/shard_map/ppermute | solution.py:30
  145.9 18.5 %collective-permute-start.56 = (f32[4,768]{1,0:T(4,128)}, f32[4,768]{1,0:T(4,128)}, u32[]{:S(2)}, u32[]{:S(2)}) collective-permute-start(f32[4,768]{1,0:T(4,128)} %pad_maximum_fusion.49), channel_id=1, source_target_pairs={{0,1},{1,0},{2,3},{3,2},{4,5},{5,4},{6,7},{7,6},{8,9},{9,8},{10,11... | collective-permute-start | bytes 36872 | tf_op jit(solution)/shard_map/ppermute | solution.py:30
  145.9 42.8 %collective-permute-start.20 = (bf16[512,768]{1,0:T(8,128)(2,1)}, bf16[512,768]{1,0:T(8,128)(2,1)}, u32[]{:S(2)}, u32[]{:S(2)}) collective-permute-start(bf16[512,768]{1,0:T(8,128)(2,1)} %convolution_convert_fusion), channel_id=1, source_target_pairs={{0,2},{1,3},{2,0},{3,1},{4,6},{5,7},{6,4},{7,5},{8,10},{9,11},{10,... | collective-permute-start | bytes 2359304 | tf_op jit(solution)/shard_map/ppermute | solution.py:30
  147.5 37.3 %collective-permute-start.26 = (bf16[2,192,768]{2,1,0:T(8,128)(2,1)}, bf16[2,192,768]{2,1,0:T(8,128)(2,1)}, u32[]{:S(2)}, u32[]{:S(2)}) collective-permute-start(bf16[2,192,768]{2,1,0:T(8,128)(2,1)} %pad_maximum_fusion.19), channel_id=1, source_target_pairs={{0,1},{1,0},{2,3},{3,2},{4,5},{5,4},{6,7},{7,6},{8,9},{9,8},{10,11... | collective-permute-start | bytes 1769480 | tf_op jit(solution)/shard_map/ppermute | solution.py:30
  165.6 38.5 %collective-permute-start.57 = (f32[4,768]{1,0:T(4,128)}, f32[4,768]{1,0:T(4,128)S(1)}, u32[]{:S(2)}, u32[]{:S(2)}) collective-permute-start(f32[4,768]{1,0:T(4,128)} %fusion.138), channel_id=1, source_target_pairs={{0,2},{1,3},{2,0},{3,1},{4,6},{5,7},{6,4},{7,5},{8,10},{9,11},{10,... | collective-permute-start | bytes 36872 | tf_op jit(solution)/shard_map/ppermute | solution.py:30
  169.5 9.1 %collective-permute-start.30 = (bf16[384,384]{1,0:T(8,128)(2,1)S(1)}, bf16[384,384]{1,0:T(8,128)(2,1)S(1)}, u32[]{:S(2)}, u32[]{:S(2)}) collective-permute-start(bf16[384,384]{1,0:T(8,128)(2,1)S(1)} %slice.891), channel_id=1, source_target_pairs={{0,2},{1,3},{2,0},{3,1},{4,6},{5,7},{6,4},{7,5},{8,10},{9,11},{10,... | collective-permute-start | bytes 884744 | tf_op jit(solution)/shard_map/ppermute | solution.py:30
  178.6 33.1 %collective-permute-start.46 = (bf16[192,256]{1,0:T(8,128)(2,1)}, bf16[192,256]{1,0:T(8,128)(2,1)}, u32[]{:S(2)}, u32[]{:S(2)}) collective-permute-start(bf16[192,256]{1,0:T(8,128)(2,1)} %bitcast.73), channel_id=1, source_target_pairs={{0,12},{4,8},{8,4},{12,0},{1,13},{5,9},{9,5},{13,1},{2,14},{6,10},... | collective-permute-start | bytes 294920 | tf_op jit(solution)/shard_map/ppermute | solution.py:30
  179.2 32.6 %collective-permute-start.45 = (bf16[192,256]{1,0:T(8,128)(2,1)}, bf16[192,256]{1,0:T(8,128)(2,1)}, u32[]{:S(2)}, u32[]{:S(2)}) collective-permute-start(bf16[192,256]{1,0:T(8,128)(2,1)} %bitcast.70), channel_id=1, source_target_pairs={{0,8},{4,12},{8,0},{12,4},{1,9},{5,13},{9,1},{13,5},{2,10},{6,14},... | collective-permute-start | bytes 294920 | tf_op jit(solution)/shard_map/ppermute | solution.py:30
  184.8 25.5 %collective-permute-start.36 = (bf16[384,384]{1,0:T(8,128)(2,1)}, bf16[384,384]{1,0:T(8,128)(2,1)}, u32[]{:S(2)}, u32[]{:S(2)}) collective-permute-start(bf16[384,384]{1,0:T(8,128)(2,1)} %fusion.57), channel_id=1, source_target_pairs={{0,4},{4,0},{8,12},{12,8},{1,5},{5,1},{9,13},{13,9},{2,6},{6,2},{1... | collective-permute-start | bytes 884744 | tf_op jit(solution)/shard_map/ppermute | solution.py:30
  188.7 27.4 %collective-permute-start.27 = (bf16[896,384]{1,0:T(8,128)(2,1)}, bf16[896,384]{1,0:T(8,128)(2,1)}, u32[]{:S(2)}, u32[]{:S(2)}) collective-permute-start(bf16[896,384]{1,0:T(8,128)(2,1)} %slice.885), channel_id=1, source_target_pairs={{0,16},{16,0},{1,17},{17,1},{2,18},{18,2},{3,19},{19,3},{4,20},{20... | collective-permute-start | bytes 2064392 | tf_op jit(solution)/shard_map/ppermute | solution.py:30
  204.9 24.6 %collective-permute-start.58 = (f32[4,768]{1,0:T(4,128)S(1)}, f32[4,768]{1,0:T(4,128)S(1)}, u32[]{:S(2)}, u32[]{:S(2)}) collective-permute-start(f32[4,768]{1,0:T(4,128)S(1)} %add.516), channel_id=1, source_target_pairs={{0,16},{16,0},{1,17},{17,1},{2,18},{18,2},{3,19},{19,3},{4,20},{20... | collective-permute-start | bytes 36872 | tf_op jit(solution)/shard_map/ppermute | solution.py:30
  210.4 8.9 %collective-permute-start.32 = (bf16[2,4,192,256]{3,2,1,0:T(8,128)(2,1)S(1)}, bf16[2,4,192,256]{3,2,1,0:T(8,128)(2,1)S(1)}, u32[]{:S(2)}, u32[]{:S(2)}) collective-permute-start(bf16[2,4,192,256]{3,2,1,0:T(8,128)(2,1)S(1)} %pad_maximum_fusion.14), channel_id=1, source_target_pairs={{0,1},{1,0},{2,3},{3,2},{4,5},{5,4},{6,7},{7,6},{8,9},{9,8},{10,11... | collective-permute-start | bytes 2359304 | tf_op jit(solution)/shard_map/ppermute | solution.py:30
  211.7 13.6 %collective-permute-start.25 = (bf16[512,384]{1,0:T(8,128)(2,1)S(1)}, bf16[512,384]{1,0:T(8,128)(2,1)S(1)}, u32[]{:S(2)}, u32[]{:S(2)}) collective-permute-start(bf16[512,384]{1,0:T(8,128)(2,1)S(1)} %copy-done.49), channel_id=1, source_target_pairs={{0,16},{16,0},{1,17},{17,1},{2,18},{18,2},{3,19},{19,3},{4,20},{20... | collective-permute-start | bytes 1179656 | tf_op jit(solution)/shard_map/ppermute | solution.py:30
  211.8 19.9 %collective-permute-start.37 = (bf16[192,384]{1,0:T(8,128)(2,1)S(1)}, bf16[192,384]{1,0:T(8,128)(2,1)S(1)}, u32[]{:S(2)}, u32[]{:S(2)}) collective-permute-start(bf16[192,384]{1,0:T(8,128)(2,1)S(1)} %dynamic-slice_convert_fusion.5), channel_id=1, source_target_pairs={{0,8},{4,12},{8,0},{12,4},{1,9},{5,13},{9,1},{13,5},{2,10},{6,14},... | collective-permute-start | bytes 442376 | tf_op jit(solution)/shard_map/ppermute | solution.py:30
  217.5 9.8 %collective-permute-start.28 = (bf16[448,384]{1,0:T(8,128)(2,1)S(1)}, bf16[448,384]{1,0:T(8,128)(2,1)S(1)}, u32[]{:S(2)}, u32[]{:S(2)}) collective-permute-start(bf16[448,384]{1,0:T(8,128)(2,1)S(1)} %slice.890), channel_id=1, source_target_pairs={{0,2},{1,3},{2,0},{3,1},{4,6},{5,7},{6,4},{7,5},{8,10},{9,11},{10,... | collective-permute-start | bytes 1032200 | tf_op jit(solution)/shard_map/ppermute | solution.py:30
  221.5 11.4 %collective-permute-start.35 = (bf16[384,256]{1,0:T(8,128)(2,1)S(1)}, bf16[384,256]{1,0:T(8,128)(2,1)S(1)}, u32[]{:S(2)}, u32[]{:S(2)}) collective-permute-start(bf16[384,256]{1,0:T(8,128)(2,1)S(1)} %pad_maximum_fusion.35), channel_id=1, source_target_pairs={{0,12},{4,8},{8,4},{12,0},{1,13},{5,9},{9,5},{13,1},{2,14},{6,10},... | collective-permute-start | bytes 589832 | tf_op jit(solution)/shard_map/ppermute | solution.py:30
  225.3 15.7 %collective-permute-start.34 = (bf16[384,256]{1,0:T(8,128)(2,1)S(1)}, bf16[384,256]{1,0:T(8,128)(2,1)S(1)}, u32[]{:S(2)}, u32[]{:S(2)}) collective-permute-start(bf16[384,256]{1,0:T(8,128)(2,1)S(1)} %pad_maximum_fusion.34), channel_id=1, source_target_pairs={{0,8},{4,12},{8,0},{12,4},{1,9},{5,13},{9,1},{13,5},{2,10},{6,14},... | collective-permute-start | bytes 589832 | tf_op jit(solution)/shard_map/ppermute | solution.py:30
  227.3 14.1 %collective-permute-start.33 = (bf16[576,256]{1,0:T(8,128)(2,1)S(1)}, bf16[576,256]{1,0:T(8,128)(2,1)S(1)}, u32[]{:S(2)}, u32[]{:S(2)}) collective-permute-start(bf16[576,256]{1,0:T(8,128)(2,1)S(1)} %pad_maximum_fusion.27), channel_id=1, source_target_pairs={{0,4},{4,0},{8,12},{12,8},{1,5},{5,1},{9,13},{13,9},{2,6},{6,2},{1... | collective-permute-start | bytes 884744 | tf_op jit(solution)/shard_map/ppermute | solution.py:30
  229.6 18.9 %collective-permute-start.38 = (bf16[480,384]{1,0:T(8,128)(2,1)S(1)}, bf16[480,384]{1,0:T(8,128)(2,1)S(1)}, u32[]{:S(2)}, u32[]{:S(2)}) collective-permute-start(bf16[480,384]{1,0:T(8,128)(2,1)S(1)} %dynamic-slice_convert_fusion), channel_id=1, source_target_pairs={{0,4},{4,0},{8,12},{12,8},{1,5},{5,1},{9,13},{13,9},{2,6},{6,2},{1... | collective-permute-start | bytes 1105928 | tf_op jit(solution)/shard_map/ppermute | solution.py:30
  231.7 26.8 %collective-permute-start.41 = (bf16[256,768]{1,0:T(8,128)(2,1)S(1)}, bf16[256,768]{1,0:T(8,128)(2,1)S(1)}, u32[]{:S(2)}, u32[]{:S(2)}) collective-permute-start(bf16[256,768]{1,0:T(8,128)(2,1)S(1)} %copy-done.51), channel_id=1, source_target_pairs={{0,2},{1,3},{2,0},{3,1},{4,6},{5,7},{6,4},{7,5},{8,10},{9,11},{10,... | collective-permute-start | bytes 1179656 | tf_op jit(solution)/shard_map/ppermute | solution.py:30
  232.9 19.1 %collective-permute-start.59 = (f32[4,768]{1,0:T(4,128)S(1)}, f32[4,768]{1,0:T(4,128)S(1)}, u32[]{:S(2)}, u32[]{:S(2)}) collective-permute-start(f32[4,768]{1,0:T(4,128)S(1)} %add.517), channel_id=1, source_target_pairs={{0,4},{4,0},{8,12},{12,8},{1,5},{5,1},{9,13},{13,9},{2,6},{6,2},{1... | collective-permute-start | bytes 36872 | tf_op jit(solution)/shard_map/ppermute | solution.py:30
  241.0 14.3 %collective-permute-start.42 = (bf16[576,384]{1,0:T(8,128)(2,1)S(1)}, bf16[576,384]{1,0:T(8,128)(2,1)S(1)}, u32[]{:S(2)}, u32[]{:S(2)}) collective-permute-start(bf16[576,384]{1,0:T(8,128)(2,1)S(1)} %slice.886), channel_id=1, source_target_pairs={{0,16},{16,0},{1,17},{17,1},{2,18},{18,2},{3,19},{19,3},{4,20},{20... | collective-permute-start | bytes 1327112 | tf_op jit(solution)/shard_map/ppermute | solution.py:30
  252.1 43.4 %collective-permute-start.60 = (f32[4,768]{1,0:T(4,128)S(1)}, f32[4,768]{1,0:T(4,128)S(1)}, u32[]{:S(2)}, u32[]{:S(2)}) collective-permute-start(f32[4,768]{1,0:T(4,128)S(1)} %add.518), channel_id=1, source_target_pairs={{0,8},{4,12},{8,0},{12,4},{1,9},{5,13},{9,1},{13,5},{2,10},{6,14},... | collective-permute-start | bytes 36872 | tf_op jit(solution)/shard_map/ppermute | solution.py:30
  252.6 13.2 %collective-permute-start.40 = (bf16[192,384]{1,0:T(8,128)(2,1)S(1)}, bf16[192,384]{1,0:T(8,128)(2,1)S(1)}, u32[]{:S(2)}, u32[]{:S(2)}) collective-permute-start(bf16[192,384]{1,0:T(8,128)(2,1)S(1)} %add_convert_fusion.3), channel_id=1, source_target_pairs={{0,8},{4,12},{8,0},{12,4},{1,9},{5,13},{9,1},{13,5},{2,10},{6,14},... | collective-permute-start | bytes 442376 | tf_op jit(solution)/shard_map/ppermute | solution.py:30
  255.6 13.7 %collective-permute-start.39 = (bf16[240,384]{1,0:T(8,128)(2,1)S(1)}, bf16[240,384]{1,0:T(8,128)(2,1)S(1)}, u32[]{:S(2)}, u32[]{:S(2)}) collective-permute-start(bf16[240,384]{1,0:T(8,128)(2,1)S(1)} %dynamic-slice_convert_fusion.4), channel_id=1, source_target_pairs={{0,8},{4,12},{8,0},{12,4},{1,9},{5,13},{9,1},{13,5},{2,10},{6,14},... | collective-permute-start | bytes 552968 | tf_op jit(solution)/shard_map/ppermute | solution.py:30
  257.0 14.9 %collective-permute-start.47 = (bf16[256,768]{1,0:T(8,128)(2,1)S(1)}, bf16[256,768]{1,0:T(8,128)(2,1)S(1)}, u32[]{:S(2)}, u32[]{:S(2)}) collective-permute-start(bf16[256,768]{1,0:T(8,128)(2,1)S(1)} %get-tuple-element.281), channel_id=1, source_target_pairs={{0,2},{1,3},{2,0},{3,1},{4,6},{5,7},{6,4},{7,5},{8,10},{9,11},{10,... | collective-permute-start | bytes 1179656 | tf_op jit(solution)/shard_map/ppermute | solution.py:30
  258.5 20.7 %collective-permute-start.49 = (bf16[288,384]{1,0:T(8,128)(2,1)S(1)}, bf16[288,384]{1,0:T(8,128)(2,1)S(1)}, u32[]{:S(2)}, u32[]{:S(2)}) collective-permute-start(bf16[288,384]{1,0:T(8,128)(2,1)S(1)} %get-tuple-element.204), channel_id=1, source_target_pairs={{2,0},{3,1},{6,4},{7,5},{8,10},{9,11},{12,14},{13,15},{18,16},{19,... | collective-permute-start | bytes 663560 | tf_op jit(solution)/shard_map/ppermute | solution.py:626
  269.4 9.8 %collective-permute-start.54 = (bf16[240,384]{1,0:T(8,128)(2,1)S(1)}, bf16[240,384]{1,0:T(8,128)(2,1)S(1)}, u32[]{:S(2)}, u32[]{:S(2)}) collective-permute-start(bf16[240,384]{1,0:T(8,128)(2,1)S(1)} %add_convert_fusion.2), channel_id=1, source_target_pairs={{0,8},{4,12},{8,0},{12,4},{1,9},{5,13},{9,1},{13,5},{2,10},{6,14},... | collective-permute-start | bytes 552968 | tf_op jit(solution)/shard_map/ppermute | solution.py:30
  269.5 12.6 %collective-permute-start.52 = (bf16[384,384]{1,0:T(8,128)(2,1)S(1)}, bf16[384,384]{1,0:T(8,128)(2,1)S(1)}, u32[]{:S(2)}, u32[]{:S(2)}) collective-permute-start(bf16[384,384]{1,0:T(8,128)(2,1)S(1)} %pad_maximum_fusion.30), channel_id=1, source_target_pairs={{0,4},{4,0},{8,12},{12,8},{1,5},{5,1},{9,13},{13,9},{2,6},{6,2},{1... | collective-permute-start | bytes 884744 | tf_op jit(solution)/shard_map/ppermute | solution.py:30
  271.9 24.4 %collective-permute-start.44 = (bf16[2,256,768]{2,1,0:T(8,128)(2,1)S(1)}, bf16[2,256,768]{2,1,0:T(8,128)(2,1)S(1)}, u32[]{:S(2)}, u32[]{:S(2)}) collective-permute-start(bf16[2,256,768]{2,1,0:T(8,128)(2,1)S(1)} %pad_maximum_fusion.15), channel_id=1, source_target_pairs={{0,1},{1,0},{2,3},{3,2},{4,5},{5,4},{6,7},{7,6},{8,9},{9,8},{10,11... | collective-permute-start | bytes 2359304 | tf_op jit(solution)/shard_map/ppermute | solution.py:30
  279.2 18.9 %collective-permute-start.48 = (bf16[2,256,768]{2,1,0:T(8,128)(2,1)S(1)}, bf16[2,256,768]{2,1,0:T(8,128)(2,1)S(1)}, u32[]{:S(2)}, u32[]{:S(2)}) collective-permute-start(bf16[2,256,768]{2,1,0:T(8,128)(2,1)S(1)} %pad_maximum_fusion.16), channel_id=1, source_target_pairs={{0,1},{1,0},{2,3},{3,2},{4,5},{5,4},{6,7},{7,6},{8,9},{9,8},{10,11... | collective-permute-start | bytes 2359304 | tf_op jit(solution)/shard_map/ppermute | solution.py:30
  279.3 16.9 %collective-permute-start.55 = (bf16[480,384]{1,0:T(8,128)(2,1)S(1)}, bf16[480,384]{1,0:T(8,128)(2,1)S(1)}, u32[]{:S(2)}, u32[]{:S(2)}) collective-permute-start(bf16[480,384]{1,0:T(8,128)(2,1)S(1)} %pad_maximum_fusion.25), channel_id=1, source_target_pairs={{0,4},{4,0},{8,12},{12,8},{1,5},{5,1},{9,13},{13,9},{2,6},{6,2},{1... | collective-permute-start | bytes 1105928 | tf_op jit(solution)/shard_map/ppermute | solution.py:30
  282.1 10.8 %collective-permute-start.50 = (bf16[288,384]{1,0:T(8,128)(2,1)S(1)}, bf16[288,384]{1,0:T(8,128)(2,1)S(1)}, u32[]{:S(2)}, u32[]{:S(2)}) collective-permute-start(bf16[288,384]{1,0:T(8,128)(2,1)S(1)} %add_convert_fusion.1), channel_id=1, source_target_pairs={{0,8},{1,9},{4,12},{5,13},{10,2},{11,3},{14,6},{15,7},{16,24},{17,... | collective-permute-start | bytes 663560 | tf_op jit(solution)/shard_map/ppermute | solution.py:631
  (92 other events, 629.2 us)

commit v3 on v2

--- a/solution.py
+++ b/solution.py
@@ -610,9 +610,6 @@
     through = functools.reduce(jnp.add, through)
     input_own = (d_resid + through).astype(BF16)
 
-    in_grad = turn(input_own)
-    in_grad = jnp.stack([in_grad, swap(in_grad, "tp", 2)])
-    input_grad = spread(in_grad, swap(in_grad, "tp", 1))
 
     both = ("ctx", "tp")
     keep, send = split_bit(part, c)
@@ -628,6 +625,9 @@
         [(g * 4 + s, g * 4 + (s ^ 2)) for g in range(4) for s in range(4) if s // 2 != g // 2],
     ).astype(F32)
     part = part.astype(BF16)
+    in_grad = after(turn(input_own), part)
+    in_grad = jnp.stack([in_grad, swap(in_grad, "tp", 2)])
+    input_grad = spread(in_grad, swap(in_grad, "tp", 1))
     moved = lax.ppermute(
         part, both,
         [(g * 4 + s, (g ^ 2) * 4 + s) for g in range(4) for s in range(4) if s // 2 == g // 2],

time: 309 us -> 308 us (level)
  Pallas kernels: 47.5 us -> 54.1 us
  waiting for transfers between devices: 66.5 us -> 61.6 us
    ppermute x58, waiting for transfers between devices: 59.3 us -> 54.4 us  [swap(): return lax.ppermute(value, axis, [(i, i ^ k) for i in range(size)])]
    ppermute x58, starting transfers between devices: 65.4 us -> 61.7 us  [swap(): return lax.ppermute(value, axis, [(i, i ^ k) for i in range(size)])]
    pallas_call x2, Pallas kernels: 24.7 us -> 28 us  [attend_back(): pl.pallas_call(functools.partial(attend_back_kernel, first), grid_spec=pl...]
    pallas_call x3, Pallas kernels: 22.8 us -> 26.1 us  [attend(): pl.pallas_call(functools.partial(attend_kernel, first), grid_spec=pltpu.P...]
  transfers between devices with their start and end apart: 61 -> 61, of which waited for: 21 -> 20; matrix products, arithmetic and copies ran while one was open for 29% -> 29% of each run, Pallas kernels for 13% -> 15%
where the time goes in v3:
time: 308 us; the launch traced here: 304 us
  starting transfers between devices  69 us (22%)
  waiting for transfers between devices  61.6 us (20%)
  Pallas kernels  54.1 us (18%)
  other arithmetic  44.1 us (14%)
  local copies, waits for them, and re-layouts  38.3 us (12%)
  matrix products  33.5 us (11%)
  between operations  3.25 us (1%)
    ppermute x58, starting transfers between devices, swap(): return lax.ppermute(value, axis, [(i, i ^ k) for i in range(size)])  61.7 us
    ppermute x58, waiting for transfers between devices, swap(): return lax.ppermute(value, axis, [(i, i ^ k) for i in range(size)])  54.4 us
    dot_general x38, matrix products, dot(): lax.dot_general(left, right, (((left_dim,), (right_dim,)), ((), ())), pre...  33.5 us
    pallas_call x2, Pallas kernels, attend_back(): pl.pallas_call(functools.partial(attend_back_kernel, first), grid_spec=pl...  28 us
    pallas_call x3, Pallas kernels, attend(): pl.pallas_call(functools.partial(attend_kernel, first), grid_spec=pltpu.P...  26.1 us
    unnamed x173, local copies, waits for them, and re-layouts  14.7 us
    ppermute x1, waiting for transfers between devices, per_device(): lax.ppermute(part, both, [(g * 4 + s, (g ^ 2) * 4 + s) for g in range(4)...  7.12 us
  transfers between devices with their start and end apart: 61, of which 20 were waited for; matrix products, arithmetic and copies ran while one was open for 29% of the time, Pallas kernels for 15%

profile of v3, /device:TPU:0, one launch (start us, length us, event | category | flops | bytes accessed | tf_op | source)
XLA Modules:
  0.0 303.8 jit_solution(7475217684999869353)
XLA Ops:
  3.5 3.1 %collective-permute-start.1 = (bf16[384,576]{0,1:T(8,128)(2,1)S(1)}, bf16[384,576]{0,1:T(8,128)(2,1)S(1)}, u32[]{:S(2)}, u32[]{:S(2)}) collective-permute-start(bf16[384,576]{0,1:T(8,128)(2,1)S(1)} %constant_dynamic-update-slice_fusion), channel_id=1, source_target_pairs={{0,2},{1,3},{2,0},{3,1},{4,6},{5,7},{6,4},{7,5},{8,10},{9,11},{10,... | collective-permute-start | bytes 1327112 | tf_op jit(solution)/shard_map/ppermute | solution.py:30
  10.2 3.0 collective-permute-start.5
  13.2 1.6 collective-permute-start.4
  16.7 9.4 %collective-permute-done.1 = bf16[384,576]{0,1:T(8,128)(2,1)S(1)} collective-permute-done((bf16[384,576]{0,1:T(8,128)(2,1)S(1)}, bf16[384,576]{0,1:T(8,128)(2,1)S(1)}, u32[]{:S(2)}, u32[]{:S(2)}) %collective-permute-start.1) | collective-permute-done | bytes 442400 | tf_op jit(solution)/shard_map/ppermute | solution.py:30
  34.6 2.3 pad_maximum_fusion.9
  36.9 1.7 collective-permute-start.6
  38.6 1.5 collective-permute-start.10
  40.1 1.5 collective-permute-start.9
  41.6 1.5 fusion.155
  43.9 1.7 fusion.36
  45.6 3.0 %collective-permute-done.6 = bf16[256,768]{1,0:T(8,128)(2,1)S(1)} collective-permute-done((bf16[256,768]{1,0:T(8,128)(2,1)}, bf16[256,768]{1,0:T(8,128)(2,1)S(1)}, u32[]{:S(2)}, u32[]{:S(2)}) %collective-permute-start.6) | collective-permute-done | bytes 393248 | tf_op jit(solution)/shard_map/ppermute | solution.py:30
  55.9 11.7 %attend.3 = (bf16[2,192,256]{2,1,0:T(8,128)(2,1)}, f32[2,3,256]{2,1,0:T(4,128)}) custom-call(s32[32]{0:T(128)} %reshape.374.flags, s32[8]{0:T(128)} %pad_add_fusion.2.bases, bf16[4,192,256]{2,1,0:T(8,128)(2,1)} %pad_maximum_fusion.21.q_ref, bf16[8,192,256]{2,1,0:T(8,128)(2,1)} %copy-done, bf16[8,192,256]{2,1,0:T(8,128)(2,1)} %copy-done.3, ...), custom_call_target="tpu_custom_call" | custom-call | tf_op jit(solution)/shard_map/attend/pallas_call | solution.py:165
  67.7 2.4 collective-permute-done.10
  72.6 2.0 slice.484
  74.6 1.5 collective-permute-start.12
  76.2 2.7 collective-permute-start.11
  79.1 2.6 constant_dynamic-update-slice_fusion.22
  81.7 7.2 %attend.4 = (bf16[1,192,256]{2,1,0:T(8,128)(2,1)}, f32[1,3,256]{2,1,0:T(4,128)}) custom-call(s32[32]{0:T(128)} %reshape.374.flags, s32[8]{0:T(128)} %pad_add_fusion.2.bases, bf16[4,192,256]{2,1,0:T(8,128)(2,1)} %pad_maximum_fusion.21.q_ref, bf16[8,192,256]{2,1,0:T(8,128)(2,1)} %copy-done, bf16[8,192,256]{2,1,0:T(8,128)(2,1)} %copy-done.3, ...), custom_call_target="tpu_custom_call" | custom-call | tf_op jit(solution)/shard_map/attend/pallas_call | solution.py:165
  89.0 1.9 collective-permute-done.12
  90.9 7.1 %attend.5 = (bf16[1,192,256]{2,1,0:T(8,128)(2,1)}, f32[1,3,256]{2,1,0:T(4,128)}) custom-call(s32[32]{0:T(128)} %reshape.374.flags, s32[8]{0:T(128)} %pad_add_fusion.2.bases, bf16[4,192,256]{2,1,0:T(8,128)(2,1)} %pad_maximum_fusion.21.q_ref, bf16[8,192,256]{2,1,0:T(8,128)(2,1)} %copy-done, bf16[8,192,256]{2,1,0:T(8,128)(2,1)} %copy-done.3, ...), custom_call_target="tpu_custom_call" | custom-call | tf_op jit(solution)/shard_map/attend/pallas_call | solution.py:165
  98.0 2.6 constant_dynamic-update-slice_fusion.21
  103.5 1.8 fusion.154
  111.1 2.9 fusion.9
  114.0 2.3 fusion.146
  123.7 2.5 fusion.10
  128.3 1.6 collective-permute-start.21
  135.7 2.7 collective-permute-start.23
  139.2 1.5 convolution_convert_fusion
  150.7 13.7 %attend_back.2 = (f32[2,192,256]{2,1,0:T(8,128)}, f32[8,192,256]{2,1,0:T(8,128)}, f32[8,192,256]{2,1,0:T(8,128)}) custom-call(s32[32]{0:T(128)} %reshape.374.flags, s32[8]{0:T(128)} %pad_add_fusion.2.bases, bf16[4,192,256]{2,1,0:T(8,128)(2,1)} %pad_maximum_fusion.21.q_ref, bf16[8,192,256]{2,1,0:T(8,128)(2,1)} %copy-done, bf16[8,192,256]{2,1,0:T(8,128)(2,1)} %copy-done.3, ...), custom_call_target="tpu_custom_call" | custom-call | tf_op jit(solution)/shard_map/attend_back/pallas_call | solution.py:270
  168.3 1.6 fusion.25
  173.3 3.4 %collective-permute-done.30 = bf16[384,384]{1,0:T(8,128)(2,1)S(1)} collective-permute-done((bf16[384,384]{1,0:T(8,128)(2,1)S(1)}, bf16[384,384]{1,0:T(8,128)(2,1)S(1)}, u32[]{:S(2)}, u32[]{:S(2)}) %collective-permute-start.30) | collective-permute-done | bytes 294944 | tf_op jit(solution)/shard_map/ppermute | solution.py:30
  176.7 5.2 %collective-permute-start.46 = (bf16[192,256]{1,0:T(8,128)(2,1)}, bf16[192,256]{1,0:T(8,128)(2,1)}, u32[]{:S(2)}, u32[]{:S(2)}) collective-permute-start(bf16[192,256]{1,0:T(8,128)(2,1)} %bitcast.73), channel_id=1, source_target_pairs={{0,12},{4,8},{8,4},{12,0},{1,13},{5,9},{9,5},{13,1},{2,14},{6,10},... | collective-permute-start | bytes 294920 | tf_op jit(solution)/shard_map/ppermute | solution.py:30
  190.3 1.9 convert_add_fusion
  193.5 14.3 %attend_back.3 = (f32[2,192,256]{2,1,0:T(8,128)}, f32[4,192,256]{2,1,0:T(8,128)}, f32[4,192,256]{2,1,0:T(8,128)}, bf16[4,192,256]{2,1,0:T(8,128)(2,1)}, bf16[4,192,256]{2,1,0:T(8,128)(2,1)}) custom-call(s32[32]{0:T(128)} %reshape.374.flags, s32[8]{0:T(128)} %pad_add_fusion.2.bases, bf16[4,192,256]{2,1,0:T(8,128)(2,1)} %pad_maximum_fusion.21.q_ref, ...), custom_call_target="tpu_custom_call" | custom-call | tf_op jit(solution)/shard_map/attend_back/pallas_call | solution.py:270
  211.3 2.1 collective-permute-start.25
  213.3 2.9 collective-permute-start.37
  222.2 1.6 collective-permute-start.35
  225.5 1.5 fusion.140
  233.5 5.9 %collective-permute-start.59 = (f32[4,768]{1,0:T(4,128)S(1)}, f32[4,768]{1,0:T(4,128)S(1)}, u32[]{:S(2)}, u32[]{:S(2)}) collective-permute-start(f32[4,768]{1,0:T(4,128)S(1)} %add.517), channel_id=1, source_target_pairs={{0,4},{4,0},{8,12},{12,8},{1,5},{5,1},{9,13},{13,9},{2,6},{6,2},{1... | collective-permute-start | bytes 36872 | tf_op jit(solution)/shard_map/ppermute | solution.py:30
  239.4 2.6 collective-permute-done.34
  242.7 6.8 %collective-permute-done.38 = bf16[480,384]{1,0:T(8,128)(2,1)S(1)} collective-permute-done((bf16[480,384]{1,0:T(8,128)(2,1)S(1)}, bf16[480,384]{1,0:T(8,128)(2,1)S(1)}, u32[]{:S(2)}, u32[]{:S(2)}) %collective-permute-start.38) | collective-permute-done | bytes 368672 | tf_op jit(solution)/shard_map/ppermute | solution.py:30
  253.5 2.7 collective-permute-start.40
  259.5 7.6 %collective-permute-done.40 = bf16[192,384]{1,0:T(8,128)(2,1)S(1)} collective-permute-done((bf16[192,384]{1,0:T(8,128)(2,1)S(1)}, bf16[192,384]{1,0:T(8,128)(2,1)S(1)}, u32[]{:S(2)}, u32[]{:S(2)}) %collective-permute-start.40) | collective-permute-done | bytes 147488 | tf_op jit(solution)/shard_map/ppermute | solution.py:30
  267.0 3.2 %collective-permute-done.39 = bf16[240,384]{1,0:T(8,128)(2,1)S(1)} collective-permute-done((bf16[240,384]{1,0:T(8,128)(2,1)S(1)}, bf16[240,384]{1,0:T(8,128)(2,1)S(1)}, u32[]{:S(2)}, u32[]{:S(2)}) %collective-permute-start.39) | collective-permute-done | bytes 184352 | tf_op jit(solution)/shard_map/ppermute | solution.py:30
  270.5 2.1 collective-permute-start.52
  272.7 7.5 %collective-permute-done.54 = bf16[240,384]{1,0:T(8,128)(2,1)S(1)} collective-permute-done((bf16[240,384]{1,0:T(8,128)(2,1)S(1)}, bf16[240,384]{1,0:T(8,128)(2,1)S(1)}, u32[]{:S(2)}, u32[]{:S(2)}) %collective-permute-start.54) | collective-permute-done | bytes 184352 | tf_op jit(solution)/shard_map/ppermute | solution.py:30
  280.5 4.6 %collective-permute-start.50 = (bf16[288,384]{1,0:T(8,128)(2,1)S(1)}, bf16[288,384]{1,0:T(8,128)(2,1)S(1)}, u32[]{:S(2)}, u32[]{:S(2)}) collective-permute-start(bf16[288,384]{1,0:T(8,128)(2,1)S(1)} %add_convert_fusion.1), channel_id=1, source_target_pairs={{0,8},{1,9},{4,12},{5,13},{10,2},{11,3},{14,6},{15,7},{16,24},{17,... | collective-permute-start | bytes 663560 | tf_op jit(solution)/shard_map/ppermute | solution.py:631
  286.4 7.1 %collective-permute-done.50 = bf16[288,384]{1,0:T(8,128)(2,1)S(1)} collective-permute-done((bf16[288,384]{1,0:T(8,128)(2,1)S(1)}, bf16[288,384]{1,0:T(8,128)(2,1)S(1)}, u32[]{:S(2)}, u32[]{:S(2)}) %collective-permute-start.50) | collective-permute-done | bytes 221216 | tf_op jit(solution)/shard_map/ppermute | solution.py:631
  (480 shorter events, 114.6 us)
Async XLA Ops:
  3.5 22.7 %collective-permute-start.1 = (bf16[384,576]{0,1:T(8,128)(2,1)S(1)}, bf16[384,576]{0,1:T(8,128)(2,1)S(1)}, u32[]{:S(2)}, u32[]{:S(2)}) collective-permute-start(bf16[384,576]{0,1:T(8,128)(2,1)S(1)} %constant_dynamic-update-slice_fusion), channel_id=1, source_target_pairs={{0,2},{1,3},{2,0},{3,1},{4,6},{5,7},{6,4},{7,5},{8,10},{9,11},{10,... | collective-permute-start | bytes 1327112 | tf_op jit(solution)/shard_map/ppermute | solution.py:30
  6.5 21.0 %collective-permute-start.2 = (bf16[384,576]{0,1:T(8,128)(2,1)S(1)}, bf16[384,576]{0,1:T(8,128)(2,1)S(1)}, u32[]{:S(2)}, u32[]{:S(2)}) collective-permute-start(bf16[384,576]{0,1:T(8,128)(2,1)S(1)} %constant_dynamic-update-slice_fusion), channel_id=1, source_target_pairs={{0,18},{1,19},{2,16},{3,17},{16,2},{17,3},{18,0},{19,1},{4,22},{5,... | collective-permute-start | bytes 1327112 | tf_op jit(solution)/shard_map/ppermute | solution.py:335
  8.0 19.5 %collective-permute-start = (bf16[384,576]{0,1:T(8,128)(2,1)S(1)}, bf16[384,576]{0,1:T(8,128)(2,1)S(1)}, u32[]{:S(2)}, u32[]{:S(2)}) collective-permute-start(bf16[384,576]{0,1:T(8,128)(2,1)S(1)} %constant_dynamic-update-slice_fusion), channel_id=1, source_target_pairs={{0,16},{16,0},{1,17},{17,1},{2,18},{18,2},{3,19},{19,3},{4,20},{20... | collective-permute-start | bytes 1327112 | tf_op jit(solution)/shard_map/ppermute | solution.py:30
  10.2 26.7 %collective-permute-start.5 = (bf16[256,768]{1,0:T(8,128)(2,1)}, bf16[256,768]{1,0:T(8,128)(2,1)}, u32[]{:S(2)}, u32[]{:S(2)}) collective-permute-start(bf16[256,768]{1,0:T(8,128)(2,1)} %pad_maximum_fusion.20), channel_id=1, source_target_pairs={{0,8},{4,12},{8,0},{12,4},{1,9},{5,13},{9,1},{13,5},{2,10},{6,14},... | collective-permute-start | bytes 1179656 | tf_op jit(solution)/shard_map/ppermute | solution.py:30
  13.2 36.4 %collective-permute-start.4 = (bf16[256,768]{1,0:T(8,128)(2,1)}, bf16[256,768]{1,0:T(8,128)(2,1)}, u32[]{:S(2)}, u32[]{:S(2)}) collective-permute-start(bf16[256,768]{1,0:T(8,128)(2,1)} %pad_maximum_fusion.20), channel_id=1, source_target_pairs={{0,4},{4,0},{8,12},{12,8},{1,5},{5,1},{9,13},{13,9},{2,6},{6,2},{1... | collective-permute-start | bytes 1179656 | tf_op jit(solution)/shard_map/ppermute | solution.py:30
  29.0 12.6 %collective-permute-start.3 = (bf16[2,768,576]{1,2,0:T(8,128)(2,1)}, bf16[2,768,576]{1,2,0:T(8,128)(2,1)}, u32[]{:S(2)}, u32[]{:S(2)}) collective-permute-start(bf16[2,768,576]{1,2,0:T(8,128)(2,1)} %pad_maximum_fusion.3), channel_id=1, source_target_pairs={{0,1},{1,0},{2,3},{3,2},{4,5},{5,4},{6,7},{7,6},{8,9},{9,8},{10,11... | collective-permute-start | bytes 5308424 | tf_op jit(solution)/shard_map/ppermute | solution.py:30
  36.9 11.7 %collective-permute-start.6 = (bf16[256,768]{1,0:T(8,128)(2,1)}, bf16[256,768]{1,0:T(8,128)(2,1)S(1)}, u32[]{:S(2)}, u32[]{:S(2)}) collective-permute-start(bf16[256,768]{1,0:T(8,128)(2,1)} %collective-permute-done.5), channel_id=1, source_target_pairs={{0,4},{4,0},{8,12},{12,8},{1,5},{5,1},{9,13},{13,9},{2,6},{6,2},{1... | collective-permute-start | bytes 1179656 | tf_op jit(solution)/shard_map/ppermute | solution.py:30
  38.6 31.5 %collective-permute-start.10 = (bf16[1728,384]{1,0:T(8,128)(2,1)}, bf16[1728,384]{1,0:T(8,128)(2,1)S(1)}, u32[]{:S(2)}, u32[]{:S(2)}) collective-permute-start(bf16[1728,384]{1,0:T(8,128)(2,1)} %pad_maximum_fusion.9), channel_id=1, source_target_pairs={{0,2},{1,3},{2,0},{3,1},{4,6},{5,7},{6,4},{7,5},{8,10},{9,11},{10,... | collective-permute-start | bytes 3981320 | tf_op jit(solution)/shard_map/ppermute | solution.py:30
  40.1 32.4 %collective-permute-start.9 = (bf16[1728,384]{1,0:T(8,128)(2,1)}, bf16[1728,384]{1,0:T(8,128)(2,1)}, u32[]{:S(2)}, u32[]{:S(2)}) collective-permute-start(bf16[1728,384]{1,0:T(8,128)(2,1)} %pad_maximum_fusion.9), channel_id=1, source_target_pairs={{0,16},{16,0},{1,17},{17,1},{2,18},{18,2},{3,19},{19,3},{4,20},{20... | collective-permute-start | bytes 3981320 | tf_op jit(solution)/shard_map/ppermute | solution.py:30
  71.1 17.9 %collective-permute-start.13 = (bf16[864,384]{1,0:T(8,128)(2,1)}, bf16[864,384]{1,0:T(8,128)(2,1)S(1)}, u32[]{:S(2)}, u32[]{:S(2)}) collective-permute-start(bf16[864,384]{1,0:T(8,128)(2,1)} %slice.485), channel_id=1, source_target_pairs={{0,16},{16,0},{1,17},{17,1},{2,18},{18,2},{3,19},{19,3},{4,20},{20... | collective-permute-start | bytes 1990664 | tf_op jit(solution)/shard_map/ppermute | solution.py:30
  74.6 16.3 %collective-permute-start.12 = (bf16[864,384]{1,0:T(8,128)(2,1)}, bf16[864,384]{1,0:T(8,128)(2,1)}, u32[]{:S(2)}, u32[]{:S(2)}) collective-permute-start(bf16[864,384]{1,0:T(8,128)(2,1)} %slice.484), channel_id=1, source_target_pairs={{0,2},{1,3},{2,0},{3,1},{4,6},{5,7},{6,4},{7,5},{8,10},{9,11},{10,... | collective-permute-start | bytes 1990664 | tf_op jit(solution)/shard_map/ppermute | solution.py:30
  76.2 12.7 %collective-permute-start.11 = (bf16[192,256]{1,0:T(8,128)(2,1)S(1)}, bf16[192,256]{1,0:T(8,128)(2,1)S(1)}, u32[]{:S(2)}, u32[]{:S(2)}) collective-permute-start(bf16[192,256]{1,0:T(8,128)(2,1)S(1)} %get-tuple-element.333), channel_id=1, source_target_pairs={{0,8},{4,12},{8,0},{12,4},{1,9},{5,13},{9,1},{13,5},{2,10},{6,14},... | collective-permute-start | bytes 294920 | tf_op jit(solution)/shard_map/ppermute | solution.py:30
  78.9 10.1 %collective-permute-start.8 = (bf16[192,256]{1,0:T(8,128)(2,1)S(1)}, bf16[192,256]{1,0:T(8,128)(2,1)S(1)}, u32[]{:S(2)}, u32[]{:S(2)}) collective-permute-start(bf16[192,256]{1,0:T(8,128)(2,1)S(1)} %get-tuple-element.332), channel_id=1, source_target_pairs={{0,12},{4,8},{8,4},{12,0},{1,13},{5,9},{9,5},{13,1},{2,14},{6,10},... | collective-permute-start | bytes 294920 | tf_op jit(solution)/shard_map/ppermute | solution.py:30
  128.3 20.1 %collective-permute-start.21 = (bf16[384,768]{1,0:T(8,128)(2,1)S(1)}, bf16[384,768]{1,0:T(8,128)(2,1)S(1)}, u32[]{:S(2)}, u32[]{:S(2)}) collective-permute-start(bf16[384,768]{1,0:T(8,128)(2,1)S(1)} %convolution_convert_fusion.1), channel_id=1, source_target_pairs={{0,2},{1,3},{2,0},{3,1},{4,6},{5,7},{6,4},{7,5},{8,10},{9,11},{10,... | collective-permute-start | bytes 1769480 | tf_op jit(solution)/shard_map/ppermute | solution.py:30
  131.9 36.4 %collective-permute-start.22 = (bf16[768,384]{1,0:T(8,128)(2,1)}, bf16[768,384]{1,0:T(8,128)(2,1)}, u32[]{:S(2)}, u32[]{:S(2)}) collective-permute-start(bf16[768,384]{1,0:T(8,128)(2,1)} %fusion.26), channel_id=1, source_target_pairs={{0,16},{16,0},{1,17},{17,1},{2,18},{18,2},{3,19},{19,3},{4,20},{20... | collective-permute-start | bytes 1769480 | tf_op jit(solution)/shard_map/ppermute | solution.py:30
  135.7 10.6 %collective-permute-start.23 = (bf16[192,256]{1,0:T(8,128)(2,1)S(1)}, bf16[192,256]{1,0:T(8,128)(2,1)S(1)}, u32[]{:S(2)}, u32[]{:S(2)}) collective-permute-start(bf16[192,256]{1,0:T(8,128)(2,1)S(1)} %convolution_convert_fusion.3), channel_id=1, source_target_pairs={{0,8},{4,12},{8,0},{12,4},{1,9},{5,13},{9,1},{13,5},{2,10},{6,14},... | collective-permute-start | bytes 294920 | tf_op jit(solution)/shard_map/ppermute | solution.py:30
  138.8 8.8 %collective-permute-start.31 = (bf16[192,256]{1,0:T(8,128)(2,1)S(1)}, bf16[192,256]{1,0:T(8,128)(2,1)S(1)}, u32[]{:S(2)}, u32[]{:S(2)}) collective-permute-start(bf16[192,256]{1,0:T(8,128)(2,1)S(1)} %convolution_convert_fusion.4), channel_id=1, source_target_pairs={{0,4},{4,0},{8,12},{12,8},{1,5},{5,1},{9,13},{13,9},{2,6},{6,2},{1... | collective-permute-start | bytes 294920 | tf_op jit(solution)/shard_map/ppermute | solution.py:30
  146.3 18.2 %collective-permute-start.56 = (f32[4,768]{1,0:T(4,128)}, f32[4,768]{1,0:T(4,128)}, u32[]{:S(2)}, u32[]{:S(2)}) collective-permute-start(f32[4,768]{1,0:T(4,128)} %pad_maximum_fusion.49), channel_id=1, source_target_pairs={{0,1},{1,0},{2,3},{3,2},{4,5},{5,4},{6,7},{7,6},{8,9},{9,8},{10,11... | collective-permute-start | bytes 36872 | tf_op jit(solution)/shard_map/ppermute | solution.py:30
  146.3 42.6 %collective-permute-start.20 = (bf16[512,768]{1,0:T(8,128)(2,1)}, bf16[512,768]{1,0:T(8,128)(2,1)}, u32[]{:S(2)}, u32[]{:S(2)}) collective-permute-start(bf16[512,768]{1,0:T(8,128)(2,1)} %convolution_convert_fusion), channel_id=1, source_target_pairs={{0,2},{1,3},{2,0},{3,1},{4,6},{5,7},{6,4},{7,5},{8,10},{9,11},{10,... | collective-permute-start | bytes 2359304 | tf_op jit(solution)/shard_map/ppermute | solution.py:30
  147.6 37.2 %collective-permute-start.26 = (bf16[2,192,768]{2,1,0:T(8,128)(2,1)}, bf16[2,192,768]{2,1,0:T(8,128)(2,1)}, u32[]{:S(2)}, u32[]{:S(2)}) collective-permute-start(bf16[2,192,768]{2,1,0:T(8,128)(2,1)} %pad_maximum_fusion.19), channel_id=1, source_target_pairs={{0,1},{1,0},{2,3},{3,2},{4,5},{5,4},{6,7},{7,6},{8,9},{9,8},{10,11... | collective-permute-start | bytes 1769480 | tf_op jit(solution)/shard_map/ppermute | solution.py:30
  165.7 42.1 %collective-permute-start.57 = (f32[4,768]{1,0:T(4,128)}, f32[4,768]{1,0:T(4,128)S(1)}, u32[]{:S(2)}, u32[]{:S(2)}) collective-permute-start(f32[4,768]{1,0:T(4,128)} %fusion.138), channel_id=1, source_target_pairs={{0,2},{1,3},{2,0},{3,1},{4,6},{5,7},{6,4},{7,5},{8,10},{9,11},{10,... | collective-permute-start | bytes 36872 | tf_op jit(solution)/shard_map/ppermute | solution.py:30
  170.6 11.4 %collective-permute-start.29 = (bf16[384,384]{1,0:T(8,128)(2,1)S(1)}, bf16[384,384]{1,0:T(8,128)(2,1)S(1)}, u32[]{:S(2)}, u32[]{:S(2)}) collective-permute-start(bf16[384,384]{1,0:T(8,128)(2,1)S(1)} %copy-done.56), channel_id=1, source_target_pairs={{0,16},{16,0},{1,17},{17,1},{2,18},{18,2},{3,19},{19,3},{4,20},{20... | collective-permute-start | bytes 884744 | tf_op jit(solution)/shard_map/ppermute | solution.py:30
  176.7 34.5 %collective-permute-start.46 = (bf16[192,256]{1,0:T(8,128)(2,1)}, bf16[192,256]{1,0:T(8,128)(2,1)}, u32[]{:S(2)}, u32[]{:S(2)}) collective-permute-start(bf16[192,256]{1,0:T(8,128)(2,1)} %bitcast.73), channel_id=1, source_target_pairs={{0,12},{4,8},{8,4},{12,0},{1,13},{5,9},{9,5},{13,1},{2,14},{6,10},... | collective-permute-start | bytes 294920 | tf_op jit(solution)/shard_map/ppermute | solution.py:30
  182.0 31.4 %collective-permute-start.45 = (bf16[192,256]{1,0:T(8,128)(2,1)}, bf16[192,256]{1,0:T(8,128)(2,1)}, u32[]{:S(2)}, u32[]{:S(2)}) collective-permute-start(bf16[192,256]{1,0:T(8,128)(2,1)} %bitcast.70), channel_id=1, source_target_pairs={{0,8},{4,12},{8,0},{12,4},{1,9},{5,13},{9,1},{13,5},{2,10},{6,14},... | collective-permute-start | bytes 294920 | tf_op jit(solution)/shard_map/ppermute | solution.py:30
  184.8 25.2 %collective-permute-start.36 = (bf16[384,384]{1,0:T(8,128)(2,1)}, bf16[384,384]{1,0:T(8,128)(2,1)}, u32[]{:S(2)}, u32[]{:S(2)}) collective-permute-start(bf16[384,384]{1,0:T(8,128)(2,1)} %fusion.57), channel_id=1, source_target_pairs={{0,4},{4,0},{8,12},{12,8},{1,5},{5,1},{9,13},{13,9},{2,6},{6,2},{1... | collective-permute-start | bytes 884744 | tf_op jit(solution)/shard_map/ppermute | solution.py:30
  188.8 28.7 %collective-permute-start.27 = (bf16[896,384]{1,0:T(8,128)(2,1)}, bf16[896,384]{1,0:T(8,128)(2,1)}, u32[]{:S(2)}, u32[]{:S(2)}) collective-permute-start(bf16[896,384]{1,0:T(8,128)(2,1)} %slice.885), channel_id=1, source_target_pairs={{0,16},{16,0},{1,17},{17,1},{2,18},{18,2},{3,19},{19,3},{4,20},{20... | collective-permute-start | bytes 2064392 | tf_op jit(solution)/shard_map/ppermute | solution.py:30
  208.6 21.6 %collective-permute-start.58 = (f32[4,768]{1,0:T(4,128)S(1)}, f32[4,768]{1,0:T(4,128)S(1)}, u32[]{:S(2)}, u32[]{:S(2)}) collective-permute-start(f32[4,768]{1,0:T(4,128)S(1)} %add.516), channel_id=1, source_target_pairs={{0,16},{16,0},{1,17},{17,1},{2,18},{18,2},{3,19},{19,3},{4,20},{20... | collective-permute-start | bytes 36872 | tf_op jit(solution)/shard_map/ppermute | solution.py:30
  209.9 9.5 %collective-permute-start.32 = (bf16[2,4,192,256]{3,2,1,0:T(8,128)(2,1)S(1)}, bf16[2,4,192,256]{3,2,1,0:T(8,128)(2,1)S(1)}, u32[]{:S(2)}, u32[]{:S(2)}) collective-permute-start(bf16[2,4,192,256]{3,2,1,0:T(8,128)(2,1)S(1)} %pad_maximum_fusion.14), channel_id=1, source_target_pairs={{0,1},{1,0},{2,3},{3,2},{4,5},{5,4},{6,7},{7,6},{8,9},{9,8},{10,11... | collective-permute-start | bytes 2359304 | tf_op jit(solution)/shard_map/ppermute | solution.py:30
  211.3 15.7 %collective-permute-start.25 = (bf16[512,384]{1,0:T(8,128)(2,1)S(1)}, bf16[512,384]{1,0:T(8,128)(2,1)S(1)}, u32[]{:S(2)}, u32[]{:S(2)}) collective-permute-start(bf16[512,384]{1,0:T(8,128)(2,1)S(1)} %copy-done.49), channel_id=1, source_target_pairs={{0,16},{16,0},{1,17},{17,1},{2,18},{18,2},{3,19},{19,3},{4,20},{20... | collective-permute-start | bytes 1179656 | tf_op jit(solution)/shard_map/ppermute | solution.py:30
  213.3 19.1 %collective-permute-start.37 = (bf16[192,384]{1,0:T(8,128)(2,1)S(1)}, bf16[192,384]{1,0:T(8,128)(2,1)S(1)}, u32[]{:S(2)}, u32[]{:S(2)}) collective-permute-start(bf16[192,384]{1,0:T(8,128)(2,1)S(1)} %dynamic-slice_convert_fusion.5), channel_id=1, source_target_pairs={{0,8},{4,12},{8,0},{12,4},{1,9},{5,13},{9,1},{13,5},{2,10},{6,14},... | collective-permute-start | bytes 442376 | tf_op jit(solution)/shard_map/ppermute | solution.py:30
  218.8 9.8 %collective-permute-start.28 = (bf16[448,384]{1,0:T(8,128)(2,1)S(1)}, bf16[448,384]{1,0:T(8,128)(2,1)S(1)}, u32[]{:S(2)}, u32[]{:S(2)}) collective-permute-start(bf16[448,384]{1,0:T(8,128)(2,1)S(1)} %slice.890), channel_id=1, source_target_pairs={{0,2},{1,3},{2,0},{3,1},{4,6},{5,7},{6,4},{7,5},{8,10},{9,11},{10,... | collective-permute-start | bytes 1032200 | tf_op jit(solution)/shard_map/ppermute | solution.py:30
  222.2 11.2 %collective-permute-start.35 = (bf16[384,256]{1,0:T(8,128)(2,1)S(1)}, bf16[384,256]{1,0:T(8,128)(2,1)S(1)}, u32[]{:S(2)}, u32[]{:S(2)}) collective-permute-start(bf16[384,256]{1,0:T(8,128)(2,1)S(1)} %pad_maximum_fusion.35), channel_id=1, source_target_pairs={{0,12},{4,8},{8,4},{12,0},{1,13},{5,9},{9,5},{13,1},{2,14},{6,10},... | collective-permute-start | bytes 589832 | tf_op jit(solution)/shard_map/ppermute | solution.py:30
  227.0 14.9 %collective-permute-start.34 = (bf16[384,256]{1,0:T(8,128)(2,1)S(1)}, bf16[384,256]{1,0:T(8,128)(2,1)S(1)}, u32[]{:S(2)}, u32[]{:S(2)}) collective-permute-start(bf16[384,256]{1,0:T(8,128)(2,1)S(1)} %pad_maximum_fusion.34), channel_id=1, source_target_pairs={{0,8},{4,12},{8,0},{12,4},{1,9},{5,13},{9,1},{13,5},{2,10},{6,14},... | collective-permute-start | bytes 589832 | tf_op jit(solution)/shard_map/ppermute | solution.py:30
  228.6 14.1 %collective-permute-start.33 = (bf16[576,256]{1,0:T(8,128)(2,1)S(1)}, bf16[576,256]{1,0:T(8,128)(2,1)S(1)}, u32[]{:S(2)}, u32[]{:S(2)}) collective-permute-start(bf16[576,256]{1,0:T(8,128)(2,1)S(1)} %pad_maximum_fusion.27), channel_id=1, source_target_pairs={{0,4},{4,0},{8,12},{12,8},{1,5},{5,1},{9,13},{13,9},{2,6},{6,2},{1... | collective-permute-start | bytes 884744 | tf_op jit(solution)/shard_map/ppermute | solution.py:30
  230.2 19.3 %collective-permute-start.38 = (bf16[480,384]{1,0:T(8,128)(2,1)S(1)}, bf16[480,384]{1,0:T(8,128)(2,1)S(1)}, u32[]{:S(2)}, u32[]{:S(2)}) collective-permute-start(bf16[480,384]{1,0:T(8,128)(2,1)S(1)} %dynamic-slice_convert_fusion), channel_id=1, source_target_pairs={{0,4},{4,0},{8,12},{12,8},{1,5},{5,1},{9,13},{13,9},{2,6},{6,2},{1... | collective-permute-start | bytes 1105928 | tf_op jit(solution)/shard_map/ppermute | solution.py:30
  232.5 27.0 %collective-permute-start.41 = (bf16[256,768]{1,0:T(8,128)(2,1)S(1)}, bf16[256,768]{1,0:T(8,128)(2,1)S(1)}, u32[]{:S(2)}, u32[]{:S(2)}) collective-permute-start(bf16[256,768]{1,0:T(8,128)(2,1)S(1)} %copy-done.51), channel_id=1, source_target_pairs={{0,2},{1,3},{2,0},{3,1},{4,6},{5,7},{6,4},{7,5},{8,10},{9,11},{10,... | collective-permute-start | bytes 1179656 | tf_op jit(solution)/shard_map/ppermute | solution.py:30
  233.5 19.7 %collective-permute-start.59 = (f32[4,768]{1,0:T(4,128)S(1)}, f32[4,768]{1,0:T(4,128)S(1)}, u32[]{:S(2)}, u32[]{:S(2)}) collective-permute-start(f32[4,768]{1,0:T(4,128)S(1)} %add.517), channel_id=1, source_target_pairs={{0,4},{4,0},{8,12},{12,8},{1,5},{5,1},{9,13},{13,9},{2,6},{6,2},{1... | collective-permute-start | bytes 36872 | tf_op jit(solution)/shard_map/ppermute | solution.py:30
  241.9 14.4 %collective-permute-start.42 = (bf16[576,384]{1,0:T(8,128)(2,1)S(1)}, bf16[576,384]{1,0:T(8,128)(2,1)S(1)}, u32[]{:S(2)}, u32[]{:S(2)}) collective-permute-start(bf16[576,384]{1,0:T(8,128)(2,1)S(1)} %slice.886), channel_id=1, source_target_pairs={{0,16},{16,0},{1,17},{17,1},{2,18},{18,2},{3,19},{19,3},{4,20},{20... | collective-permute-start | bytes 1327112 | tf_op jit(solution)/shard_map/ppermute | solution.py:30
  253.2 40.5 %collective-permute-start.60 = (f32[4,768]{1,0:T(4,128)S(1)}, f32[4,768]{1,0:T(4,128)S(1)}, u32[]{:S(2)}, u32[]{:S(2)}) collective-permute-start(f32[4,768]{1,0:T(4,128)S(1)} %add.518), channel_id=1, source_target_pairs={{0,8},{4,12},{8,0},{12,4},{1,9},{5,13},{9,1},{13,5},{2,10},{6,14},... | collective-permute-start | bytes 36872 | tf_op jit(solution)/shard_map/ppermute | solution.py:30
  253.5 13.5 %collective-permute-start.40 = (bf16[192,384]{1,0:T(8,128)(2,1)S(1)}, bf16[192,384]{1,0:T(8,128)(2,1)S(1)}, u32[]{:S(2)}, u32[]{:S(2)}) collective-permute-start(bf16[192,384]{1,0:T(8,128)(2,1)S(1)} %add_convert_fusion.3), channel_id=1, source_target_pairs={{0,8},{4,12},{8,0},{12,4},{1,9},{5,13},{9,1},{13,5},{2,10},{6,14},... | collective-permute-start | bytes 442376 | tf_op jit(solution)/shard_map/ppermute | solution.py:30
  256.6 13.6 %collective-permute-start.39 = (bf16[240,384]{1,0:T(8,128)(2,1)S(1)}, bf16[240,384]{1,0:T(8,128)(2,1)S(1)}, u32[]{:S(2)}, u32[]{:S(2)}) collective-permute-start(bf16[240,384]{1,0:T(8,128)(2,1)S(1)} %dynamic-slice_convert_fusion.4), channel_id=1, source_target_pairs={{0,8},{4,12},{8,0},{12,4},{1,9},{5,13},{9,1},{13,5},{2,10},{6,14},... | collective-permute-start | bytes 552968 | tf_op jit(solution)/shard_map/ppermute | solution.py:30
  258.1 22.3 %collective-permute-start.47 = (bf16[288,384]{1,0:T(8,128)(2,1)S(1)}, bf16[288,384]{1,0:T(8,128)(2,1)S(1)}, u32[]{:S(2)}, u32[]{:S(2)}) collective-permute-start(bf16[288,384]{1,0:T(8,128)(2,1)S(1)} %get-tuple-element.206), channel_id=1, source_target_pairs={{2,0},{3,1},{6,4},{7,5},{8,10},{9,11},{12,14},{13,15},{18,16},{19,... | collective-permute-start | bytes 663560 | tf_op jit(solution)/shard_map/ppermute | solution.py:623
  270.3 10.0 %collective-permute-start.54 = (bf16[240,384]{1,0:T(8,128)(2,1)S(1)}, bf16[240,384]{1,0:T(8,128)(2,1)S(1)}, u32[]{:S(2)}, u32[]{:S(2)}) collective-permute-start(bf16[240,384]{1,0:T(8,128)(2,1)S(1)} %add_convert_fusion.2), channel_id=1, source_target_pairs={{0,8},{4,12},{8,0},{12,4},{1,9},{5,13},{9,1},{13,5},{2,10},{6,14},... | collective-permute-start | bytes 552968 | tf_op jit(solution)/shard_map/ppermute | solution.py:30
  270.5 14.7 %collective-permute-start.52 = (bf16[384,384]{1,0:T(8,128)(2,1)S(1)}, bf16[384,384]{1,0:T(8,128)(2,1)S(1)}, u32[]{:S(2)}, u32[]{:S(2)}) collective-permute-start(bf16[384,384]{1,0:T(8,128)(2,1)S(1)} %pad_maximum_fusion.30), channel_id=1, source_target_pairs={{0,4},{4,0},{8,12},{12,8},{1,5},{5,1},{9,13},{13,9},{2,6},{6,2},{1... | collective-permute-start | bytes 884744 | tf_op jit(solution)/shard_map/ppermute | solution.py:30
  272.7 23.3 %collective-permute-start.44 = (bf16[2,256,768]{2,1,0:T(8,128)(2,1)S(1)}, bf16[2,256,768]{2,1,0:T(8,128)(2,1)S(1)}, u32[]{:S(2)}, u32[]{:S(2)}) collective-permute-start(bf16[2,256,768]{2,1,0:T(8,128)(2,1)S(1)} %pad_maximum_fusion.15), channel_id=1, source_target_pairs={{0,1},{1,0},{2,3},{3,2},{4,5},{5,4},{6,7},{7,6},{8,9},{9,8},{10,11... | collective-permute-start | bytes 2359304 | tf_op jit(solution)/shard_map/ppermute | solution.py:30
  280.4 15.4 %collective-permute-start.55 = (bf16[480,384]{1,0:T(8,128)(2,1)S(1)}, bf16[480,384]{1,0:T(8,128)(2,1)S(1)}, u32[]{:S(2)}, u32[]{:S(2)}) collective-permute-start(bf16[480,384]{1,0:T(8,128)(2,1)S(1)} %pad_maximum_fusion.25), channel_id=1, source_target_pairs={{0,4},{4,0},{8,12},{12,8},{1,5},{5,1},{9,13},{13,9},{2,6},{6,2},{1... | collective-permute-start | bytes 1105928 | tf_op jit(solution)/shard_map/ppermute | solution.py:30
  280.5 13.0 %collective-permute-start.50 = (bf16[288,384]{1,0:T(8,128)(2,1)S(1)}, bf16[288,384]{1,0:T(8,128)(2,1)S(1)}, u32[]{:S(2)}, u32[]{:S(2)}) collective-permute-start(bf16[288,384]{1,0:T(8,128)(2,1)S(1)} %add_convert_fusion.1), channel_id=1, source_target_pairs={{0,8},{1,9},{4,12},{5,13},{10,2},{11,3},{14,6},{15,7},{16,24},{17,... | collective-permute-start | bytes 663560 | tf_op jit(solution)/shard_map/ppermute | solution.py:631
  285.1 10.5 %collective-permute-start.48 = (bf16[256,768]{1,0:T(8,128)(2,1)S(1)}, bf16[256,768]{1,0:T(8,128)(2,1)S(1)}, u32[]{:S(2)}, u32[]{:S(2)}) collective-permute-start(bf16[256,768]{1,0:T(8,128)(2,1)S(1)} %pad_maximum_fusion.24), channel_id=1, source_target_pairs={{0,2},{1,3},{2,0},{3,1},{4,6},{5,7},{6,4},{7,5},{8,10},{9,11},{10,... | collective-permute-start | bytes 1179656 | tf_op jit(solution)/shard_map/ppermute | solution.py:30
  (92 other events, 616.1 us)
